TPU v7x, 32 devices: a whole 2x2x4 slice. The times are simulated.
32 devices in a mesh: dp: 4 (over z), seq: 4 (over y, x), expert: 2 (over core).
Axes of the slice: x: 2, y: 2, z: 4, core: 2. Of those that a mesh axis runs over, the one named last changes fastest.
Arguments:
- block_input: float32 [8, 512, 768], P(('dp', 'expert'), 'seq'), may hold values from -12 to 12
- documents: int32 [8, 512], P(('dp', 'expert')), may hold values from 0 to 2, never falling along the last dimension, each value on 1 to 320 neighbouring positions
- route_experts: int32 [8, 512, 2], P(('dp', 'expert'), 'seq'), may hold values from 0 to 7, all different within a row; in each aligned block of 128 rows (0 to 127, 128 to 255, ..., all dimensions but the last counted through in order) at most 48 rows name the same one
- route_gate: float32 [8, 512, 2], P(('dp', 'expert'), 'seq'), may hold values from 0.25 to 1
- first_gain: bfloat16 [768], P(('dp', 'seq', 'expert')), may hold values from 0.25 to 1.75
- entry_weight: bfloat16 [768, 2304], P(None, ('dp', 'seq', 'expert')), may hold values from -0.21875 to 0.21875
- exit_weight: bfloat16 [768, 768], P(None, ('dp', 'seq', 'expert')), may hold values from -0.875 to 0.875
- position_bias: float32 [32, 12], replicated, may hold values from -4 to 260
- second_gain: bfloat16 [768], P(('dp', 'seq', 'expert')), may hold values from 0.25 to 1.75
- expert_up: bfloat16 [8, 768, 3072], P(('dp', 'expert'), None, 'seq'), may hold values from -0.21875 to 0.21875
- expert_down: bfloat16 [8, 3072, 768], P(('dp', 'expert'), 'seq'), may hold values from -0.109375 to 0.109375
- cotangent: float32 [8, 512, 768], P(('dp', 'expert'), 'seq'), may hold values from -6 to 6
Outputs:
- block_output: float32 [8, 512, 768], P(('dp', 'expert'), 'seq')
- back_input: float32 [8, 512, 768], P(('dp', 'expert'), 'seq')
- back_first_gain: float32 [768], P(('dp', 'seq', 'expert'))
- back_entry: float32 [768, 2304], P(None, ('dp', 'seq', 'expert'))
- back_exit: float32 [768, 768], P(None, ('dp', 'seq', 'expert'))
- back_bias: float32 [32, 12], replicated
- back_second_gain: float32 [768], P(('dp', 'seq', 'expert'))
- back_expert_up: float32 [8, 768, 3072], P(('dp', 'expert'), None, 'seq')
- back_expert_down: float32 [8, 3072, 768], P(('dp', 'expert'), 'seq')
Inputs may be any that keep to these rules, and one draw needn't show every extreme that they name: `route_experts`: in each device's aligned block of 128 tokens no expert is named by more than 48 routes, a bound that some block reaches; a token's two experts differ. `documents`: document numbers never fall along a sequence; no document is longer than five eighths of 512 tokens, and one is that long.
All inputs are finite; a program needn't handle non-finite values.
Results may differ from a plain program's by a relative error of at most 0.014.
Values may be sent and summed in bfloat16 or wider, within the bound.
No kernel may reach another device: no remote copies, remote signals or barrier semaphores. Data moves between devices by JAX's collectives and lax.ppermute only.
A program may use at most 128 MiB of HBM per device.

v0:
```python
import jax
import jax.numpy as jnp
from jax import lax
from jax.sharding import PartitionSpec as P

EPSILON = 1e-06
SLOPE = 0.7978845608028654
CUBIC = 0.044715
LIMITS = (19, 21, 24, 27, 31, 35, 40, 46, 52, 59, 67, 77, 87, 99, 113)
MASKED = -1e30
HIGH = lax.Precision.HIGHEST


def gelu_value(values):
    return 0.5 * values * (1.0 + jnp.tanh(SLOPE * (values + CUBIC * values * values * values)))


def gelu_slope(values):
    tangent = jnp.tanh(SLOPE * (values + CUBIC * values * values * values))
    return 0.5 * (1.0 + tangent) + 0.5 * values * (1.0 - tangent * tangent) * SLOPE * (
        1.0 + 3.0 * CUBIC * values * values
    )


def bucket_onehot(lag, count):
    bucket = jnp.minimum(lag, 16)
    for threshold in LIMITS:
        bucket = bucket + (lag >= threshold).astype(jnp.int32)
    return (bucket[..., None] == jnp.arange(count, dtype=jnp.int32)).astype(jnp.float32)


def rms_scale(values):
    return lax.rsqrt(jnp.mean(values * values, axis=-1, keepdims=True) + EPSILON)


def contract_rows(left, right):
    return lax.dot_general(
        left, right, (((0,), (0,)), ((), ())), preferred_element_type=jnp.float32
    )


def contract_cols(left, right):
    return lax.dot_general(
        left, right, (((1,), (1,)), ((), ())), preferred_element_type=jnp.float32
    )


def masked_scores(queries, key_heads, bias_block, allowed, factor):
    scores = (
        jnp.einsum("qhd,khd->hqk", queries, key_heads, preferred_element_type=jnp.float32) * factor
        + bias_block
    )
    return jnp.where(allowed[None], scores, MASKED)


def expert_work(rows, upstream, up_weight, down_weight):
    before = jnp.dot(rows, up_weight, preferred_element_type=jnp.float32)
    active = gelu_value(before).astype(jnp.bfloat16)
    result = jnp.dot(active, down_weight, preferred_element_type=jnp.float32)
    back_active = contract_cols(upstream, down_weight)
    back_before = (back_active * gelu_slope(before)).astype(jnp.bfloat16)
    down_grad = contract_rows(active, upstream)
    up_grad = contract_rows(rows, back_before)
    back_rows = contract_cols(back_before, up_weight)
    return (result, back_rows, up_grad, down_grad)


def local(
    block_input,
    documents,
    route_experts,
    route_gate,
    first_gain,
    entry_weight,
    exit_weight,
    position_bias,
    second_gain,
    expert_up,
    expert_down,
    cotangent,
):
    rows_here = block_input.shape[1]
    features = block_input.shape[2]
    head_count = position_bias.shape[1]
    head_size = features // head_count
    factor = head_size ** (-0.5)
    top_count = route_experts.shape[2]
    inputs = block_input.reshape(rows_here, features)
    upstream = cotangent.reshape(rows_here, features)
    gain_one, entry_full, exit_full, gain_two = (
        lax.all_gather(first_gain, ("dp", "seq", "expert"), axis=0, tiled=True),
        lax.all_gather(entry_weight, ("dp", "seq", "expert"), axis=1, tiled=True),
        lax.all_gather(exit_weight, ("dp", "seq", "expert"), axis=1, tiled=True),
        lax.all_gather(second_gain, ("dp", "seq", "expert"), axis=0, tiled=True),
    )
    gain_one = gain_one.astype(jnp.float32)
    gain_two = gain_two.astype(jnp.float32)
    scale_one = rms_scale(inputs)
    normed_one = (inputs * scale_one * gain_one).astype(jnp.bfloat16)
    projected = jnp.dot(normed_one, entry_full, preferred_element_type=jnp.float32).astype(
        jnp.bfloat16
    )
    queries = projected[:, :features].reshape(rows_here, head_count, head_size)
    key_value = lax.all_gather(projected[:, features:], "seq", axis=0, tiled=True)
    seq_length = key_value.shape[0]
    key_heads = key_value[:, :features].reshape(seq_length, head_count, head_size)
    values = key_value[:, features:].reshape(seq_length, head_count, head_size)
    offset = lax.axis_index("seq") * rows_here
    query_index = offset + jnp.arange(rows_here, dtype=jnp.int32)
    key_index = jnp.arange(seq_length, dtype=jnp.int32)
    segment_keys = documents.reshape(seq_length)
    segment_queries = lax.dynamic_slice_in_dim(segment_keys, offset, rows_here)
    allowed = (key_index[None, :] <= query_index[:, None]) & (
        segment_queries[:, None] == segment_keys[None, :]
    )
    lag_table = jnp.maximum(query_index[:, None] - key_index[None, :], 0)
    bucket_hot = bucket_onehot(lag_table, position_bias.shape[0])
    bias_block = jnp.einsum("qkb,bh->hqk", bucket_hot, position_bias, precision=HIGH)
    scores = masked_scores(queries, key_heads, bias_block, allowed, factor)
    row_peak = jnp.max(scores, axis=2, keepdims=True)
    log_total = row_peak + jnp.log(jnp.sum(jnp.exp(scores - row_peak), axis=2, keepdims=True))
    weights = jnp.where(allowed[None], jnp.exp(scores - log_total), 0.0).astype(jnp.bfloat16)
    context = (
        jnp.einsum("hqk,khd->qhd", weights, values, preferred_element_type=jnp.float32)
        .astype(jnp.bfloat16)
        .reshape(rows_here, features)
    )
    hidden = inputs + jnp.dot(context, exit_full, preferred_element_type=jnp.float32)
    scale_two = rms_scale(hidden)
    normed_two = (hidden * scale_two * gain_two).astype(jnp.bfloat16)
    group_size = lax.axis_size(("dp", "expert"))
    capacity = 3 * rows_here // group_size
    route_count = rows_here * top_count
    flat_routes = route_experts.reshape(route_count)
    flat_gates = route_gate.reshape(route_count)
    member = (flat_routes[:, None] == jnp.arange(group_size, dtype=jnp.int32)[None, :]).astype(
        jnp.int32
    )
    route_rank = jnp.sum(member * (jnp.cumsum(member, axis=0) - 1), axis=1)
    slot_of = flat_routes * capacity + route_rank
    filler = (
        jnp.full((group_size * capacity,), -1, jnp.int32)
        .at[slot_of]
        .set(jnp.arange(route_count, dtype=jnp.int32))
    )
    present = filler >= 0
    source = jnp.maximum(filler, 0)
    token_of = source // top_count
    send_rows = jnp.where(present[:, None], normed_two[token_of], jnp.zeros((), jnp.bfloat16))
    send_upstream = jnp.where(
        present[:, None], upstream[token_of] * flat_gates[source][:, None], 0.0
    ).astype(jnp.bfloat16)
    shaped = (group_size, capacity, features)
    arrived_input, arrived_upstream = (
        lax.all_to_all(
            send_rows.reshape(shaped), ("dp", "expert"), split_axis=0, concat_axis=0, tiled=True
        ),
        lax.all_to_all(
            send_upstream.reshape(shaped), ("dp", "expert"), split_axis=0, concat_axis=0, tiled=True
        ),
    )
    rows_flat = arrived_input.reshape(group_size * capacity, features)
    upstream_flat = arrived_upstream.reshape(group_size * capacity, features)
    full_up, full_down = (
        lax.all_gather(expert_up, "seq", axis=2, tiled=True),
        lax.all_gather(expert_down, "seq", axis=1, tiled=True),
    )
    result, back_rows, up_grad, down_grad = expert_work(
        rows_flat, upstream_flat, full_up[0], full_down[0]
    )
    up_share, down_share = (
        lax.psum_scatter(
            up_grad[None].astype(jnp.bfloat16), "seq", scatter_dimension=2, tiled=True
        ).astype(jnp.float32),
        lax.psum_scatter(
            down_grad[None].astype(jnp.bfloat16), "seq", scatter_dimension=1, tiled=True
        ).astype(jnp.float32),
    )
    returned_out, returned_back = (
        lax.all_to_all(
            result.astype(jnp.bfloat16).reshape(shaped),
            ("dp", "expert"),
            split_axis=0,
            concat_axis=0,
            tiled=True,
        ),
        lax.all_to_all(
            back_rows.astype(jnp.bfloat16).reshape(shaped),
            ("dp", "expert"),
            split_axis=0,
            concat_axis=0,
            tiled=True,
        ),
    )
    route_out = (
        returned_out.reshape(group_size * capacity, features)[slot_of]
        .astype(jnp.float32)
        .reshape(rows_here, top_count, features)
    )
    mixture = jnp.sum(route_out * route_gate.reshape(rows_here, top_count, 1), axis=1)
    block_output = hidden + mixture
    route_back = (
        returned_back.reshape(group_size * capacity, features)[slot_of]
        .astype(jnp.float32)
        .reshape(rows_here, top_count, features)
    )
    back_normed_two = jnp.sum(route_back, axis=1)
    upper_two = back_normed_two * gain_two
    gain_two_grad = jnp.sum(back_normed_two * hidden * scale_two, axis=0)
    back_hidden = upstream + scale_two * (
        upper_two
        - hidden * scale_two * scale_two * jnp.mean(upper_two * hidden, axis=1, keepdims=True)
    )
    entry_back, exit_back = (
        lax.all_gather(entry_weight, ("dp", "seq", "expert"), axis=1, tiled=True),
        lax.all_gather(exit_weight, ("dp", "seq", "expert"), axis=1, tiled=True),
    )
    upstream_hidden = back_hidden.astype(jnp.bfloat16)
    exit_grad = contract_rows(context, upstream_hidden)
    back_context = (
        contract_cols(upstream_hidden, exit_back)
        .astype(jnp.bfloat16)
        .reshape(rows_here, head_count, head_size)
    )
    scores_again = masked_scores(queries, key_heads, bias_block, allowed, factor)
    probs = jnp.where(allowed[None], jnp.exp(scores_again - log_total), 0.0)
    back_probs = jnp.einsum(
        "qhd,khd->hqk", back_context, values, preferred_element_type=jnp.float32
    )
    row_dot = jnp.sum(probs * back_probs, axis=2, keepdims=True)
    back_scores = probs * (back_probs - row_dot)
    bias_grad = jnp.einsum("hqk,qkb->bh", back_scores, bucket_hot, precision=HIGH)
    scaled_back = (back_scores * factor).astype(jnp.bfloat16)
    back_queries = jnp.einsum(
        "hqk,khd->qhd", scaled_back, key_heads, preferred_element_type=jnp.float32
    ).reshape(rows_here, features)
    back_keys = jnp.einsum(
        "hqk,qhd->khd", scaled_back, queries, preferred_element_type=jnp.float32
    ).reshape(seq_length, features)
    back_values = jnp.einsum(
        "hqk,qhd->khd", probs.astype(jnp.bfloat16), back_context, preferred_element_type=jnp.float32
    ).reshape(seq_length, features)
    back_pairs = lax.psum_scatter(
        jnp.concatenate([back_keys, back_values], axis=1).astype(jnp.bfloat16),
        "seq",
        scatter_dimension=0,
        tiled=True,
    ).astype(jnp.float32)
    back_projected = jnp.concatenate([back_queries, back_pairs], axis=1).astype(jnp.bfloat16)
    entry_grad = contract_rows(normed_one, back_projected)
    back_normed_one = contract_cols(back_projected, entry_back)
    upper_one = back_normed_one * gain_one
    gain_one_grad = jnp.sum(back_normed_one * inputs * scale_one, axis=0)
    back_input = back_hidden + scale_one * (
        upper_one
        - inputs * scale_one * scale_one * jnp.mean(upper_one * inputs, axis=1, keepdims=True)
    )
    gain_one_share, entry_share, exit_share, gain_two_share = (
        lax.psum_scatter(gain_one_grad, ("dp", "seq", "expert"), scatter_dimension=0, tiled=True),
        lax.psum_scatter(entry_grad, ("dp", "seq", "expert"), scatter_dimension=1, tiled=True),
        lax.psum_scatter(exit_grad, ("dp", "seq", "expert"), scatter_dimension=1, tiled=True),
        lax.psum_scatter(gain_two_grad, ("dp", "seq", "expert"), scatter_dimension=0, tiled=True),
    )
    bias_total = lax.psum(bias_grad, ("dp", "seq", "expert"))
    return (
        block_output.reshape(block_input.shape),
        back_input.reshape(block_input.shape),
        gain_one_share,
        entry_share,
        exit_share,
        bias_total,
        gain_two_share,
        up_share,
        down_share,
    )


def solution(mesh):
    placed = (
        P(("dp", "expert"), "seq", None),
        P(("dp", "expert"), None),
        P(("dp", "expert"), "seq", None),
        P(("dp", "expert"), "seq", None),
        P(("dp", "seq", "expert")),
        P(None, ("dp", "seq", "expert")),
        P(None, ("dp", "seq", "expert")),
        P(),
        P(("dp", "seq", "expert")),
        P(("dp", "expert"), None, "seq"),
        P(("dp", "expert"), "seq", None),
        P(("dp", "expert"), "seq", None),
    )
    return jax.shard_map(
        local,
        mesh=mesh,
        in_specs=placed,
        out_specs=(
            P(("dp", "expert"), "seq", None),
            P(("dp", "expert"), "seq", None),
            P(("dp", "seq", "expert")),
            P(None, ("dp", "seq", "expert")),
            P(None, ("dp", "seq", "expert")),
            P(),
            P(("dp", "seq", "expert")),
            P(("dp", "expert"), None, "seq"),
            P(("dp", "expert"), "seq", None),
        ),
        check_vma=False,
    )
```

profile of v0, /device:TPU:18, one launch (start us, length us, event | category | flops | bytes accessed | tf_op | source)
XLA Modules:
  0.0 736.2 jit_solution(6812603287576350508)
XLA Ops:
  9.7 41.1 %all-reduce.5 = (bf16[768]{0:T(1024)(128)(2,1)S(1)}, bf16[768]{0:T(1024)(128)(2,1)S(1)}) all-reduce(bf16[768]{0:T(1024)(128)(2,1)S(1)} %dynamic-update-slice, bf16[768]{0:T(1024)(128)(2,1)S(1)} %dynamic-update-slice.1), channel_id=1, replica_groups=mesh['dp'=4,'seq'=4,'expert'=2] {'dp','seq','expert'}, use_global_device_ids=true, to_apply=%add | all-reduce | flops 1536 | bytes 6144
  51.9 18.5 %all-gather.6.cloned.1.call-done = bf16[768,2304]{0,1:T(8,128)(2,1)} async-done(((bf16[768,72]{0,1:T(8,128)(2,1)}), bf16[768,2304]{0,1:T(8,128)(2,1)}) %all-gather.6.cloned.1.call-update) | async-done | bytes 3538960 | tf_op jit(solution)/shard_map/all_gather | solution.py:92
  92.2 14.5 %all-gather.8.cloned.1.call-done = bf16[512,1536]{1,0:T(8,128)(2,1)} async-done(((bf16[128,1536]{1,0:T(8,128)(2,1)}), bf16[512,1536]{1,0:T(8,128)(2,1)}) %all-gather.8.cloned.1.call-update) | async-done | bytes 1572880 | tf_op jit(solution)/shard_map/all_gather | solution.py:104
  118.5 43.7 %all-gather.10.cloned.1.call-done = bf16[768,768]{0,1:T(8,128)(2,1)} async-done(((bf16[768,24]{0,1:T(8,128)(2,1)}), bf16[768,768]{0,1:T(8,128)(2,1)}) %all-gather.10.cloned.1.call-update) | async-done | bytes 1179664 | tf_op jit(solution)/shard_map/all_gather | solution.py:93
  167.5 5.6 all-to-all-start
  179.1 7.3 all-to-all-done
  186.5 6.7 all-to-all-start.2
  193.2 28.0 %all-gather.12.cloned.1.call-done = bf16[1,768,3072]{2,1,0:T(8,128)(2,1)} async-done(((bf16[1,768,768]{2,1,0:T(8,128)(2,1)}), bf16[1,768,3072]{2,1,0:T(8,128)(2,1)}) %all-gather.12.cloned.1.call-update) | async-done | bytes 4718608 | tf_op jit(solution)/shard_map/all_gather | solution.py:165
  221.2 6.5 fusion.15
  227.7 52.1 %all-gather.14.cloned.1.call-done = bf16[1,3072,768]{2,1,0:T(8,128)(2,1)} async-done(((bf16[1,768,768]{2,1,0:T(8,128)(2,1)}), bf16[1,3072,768]{2,1,0:T(8,128)(2,1)}) %all-gather.14.cloned.1.call-update) | async-done | bytes 4718608 | tf_op jit(solution)/shard_map/all_gather | solution.py:166
  279.8 7.6 %fusion.8 = bf16[384,3072]{1,0:T(8,128)(2,1)S(1)} fusion(f32[384,3072]{1,0:T(8,128)} %fusion.15, bf16[384,768]{1,0:T(8,128)(2,1)S(1)} %bitcast.134, bf16[1,3072,768]{2,1,0:T(8,128)(2,1)} %all-gather.14.cloned.1.call-done), kind=kOutput, calls=%fused_computation.19 | convolution fusion | flops 1834352640 | bytes 12386304 | tf_op jit(solution)/shard_map/dot_general | solution.py:43
  295.5 7.4 %fusion.28 = bf16[384,768]{1,0:T(8,128)(2,1)} fusion(bf16[1,3072,768]{2,1,0:T(8,128)(2,1)} %all-gather.14.cloned.1.call-done, f32[384,3072]{1,0:T(8,128)} %fusion.15), kind=kOutput, calls=%fused_computation.46 | convolution fusion | flops 1822851072 | bytes 10027008 | tf_op jit(solution)/shard_map/dot_general | solution.py:59
  302.9 6.0 all-to-all-done.3
  309.0 6.7 all-to-all-start.1
  320.4 8.7 %all-to-all-done.1 = bf16[8,48,768]{2,1,0:T(8,128)(2,1)S(1)} async-done(((bf16[8,48,768]{2,1,0:T(8,128)(2,1)}), bf16[8,48,768]{2,1,0:T(8,128)(2,1)S(1)}, u32[]{:S(2)}, u32[]{:S(2)}) %all-to-all-start.1) | async-done | bytes 589856 | tf_op jit(solution)/shard_map/all_to_all | solution.py:180
  346.5 6.0 fusion.17
  353.6 7.7 %fusion.18 = bf16[1,3072,768]{2,1,0:T(8,128)(2,1)} fusion(bf16[384,768]{1,0:T(8,128)(2,1)S(1)} %bitcast.135, f32[384,3072]{1,0:T(8,128)} %fusion.15), kind=kOutput, calls=%fused_computation.30 | convolution fusion | flops 1824915456 | bytes 10027008 | tf_op jit(solution)/shard_map/dot_general | solution.py:37
  367.9 10.6 %reduce-scatter.16.cloned.1.call-done = bf16[128,1536]{1,0:T(8,128)(2,1)} async-done(((bf16[512,1536]{1,0:T(8,128)(2,1)}), bf16[128,1536]{1,0:T(8,128)(2,1)}) %reduce-scatter.16.cloned.1.call-update) | async-done | bytes 393232
  380.4 5.1 fusion.36
  389.1 6.3 fusion.31
  396.2 41.6 %all-reduce.4 = (f32[768]{0:T(1024)S(1)}, f32[32,12]{0,1:T(8,128)}, f32[768]{0:T(1024)S(1)}) all-reduce(f32[768]{0:T(1024)S(1)} %get-tuple-element.11, f32[32,12]{0,1:T(8,128)S(1)} %fusion.31, f32[768]{0:T(1024)S(1)} %copy-done.33), channel_id=3, replica_groups=mesh['dp'=4,'seq'=4,'expert'=2] {'dp','seq','expert'}, use_global_device_ids=true, to_apply=%region_15.16.clone | all-reduce | flops 1920 | bytes 15360
  442.8 57.0 %reduce-scatter.14.cloned.1.call-done = bf16[1,768,768]{2,1,0:T(8,128)(2,1)} async-done(((bf16[1,3072,768]{2,1,0:T(8,128)(2,1)}), bf16[1,768,768]{2,1,0:T(8,128)(2,1)}) %reduce-scatter.14.cloned.1.call-update) | async-done | bytes 1179664 | tf_op jit(solution)/shard_map/reduce_scatter | solution.py:175
  502.6 101.7 %reduce-scatter.10.cloned.1.call-done = f32[768,24]{0,1:T(8,128)} async-done(((f32[768,768]{0,1:T(8,128)}), f32[768,24]{0,1:T(8,128)}) %reduce-scatter.10.cloned.1.call-update) | async-done | bytes 73744 | tf_op jit(solution)/shard_map/reduce_scatter | solution.py:261
  604.3 124.6 %reduce-scatter.8.cloned.1.call-done = f32[768,72]{0,1:T(8,128)} async-done(((f32[768,2304]{0,1:T(8,128)}), f32[768,72]{0,1:T(8,128)}) %reduce-scatter.8.cloned.1.call-update) | async-done | bytes 221200 | tf_op jit(solution)/shard_map/reduce_scatter | solution.py:260
  (203 shorter events, 99.6 us)
Async XLA Ops:
  7.2 72.0 %copy-start = (f32[32,12]{0,1:T(8,128)S(1)}, f32[32,12]{0,1:T(8,128)}, u32[]{:S(2)}) copy-start(f32[32,12]{0,1:T(8,128)} %param.19) | copy-start | bytes 4612
  7.2 63.2 %all-gather.6.cloned.1.call-start = ((), (), s32[]{:S(2)}) async-start(), calls=%async_computation.9 | async-start | bytes 3649536 | tf_op jit(solution)/shard_map/all_gather | solution.py:92
  7.9 98.8 %all-gather.8.cloned.1.call-start = ((), (), s32[]{:S(2)}) async-start(), calls=%async_computation.10 | async-start | bytes 1966080 | tf_op jit(solution)/shard_map/all_gather | solution.py:104
  75.5 86.7 %all-gather.10.cloned.1.call-start = ((), (), s32[]{:S(2)}) async-start(), calls=%async_computation.11 | async-start | bytes 1216512 | tf_op jit(solution)/shard_map/all_gather | solution.py:93
  76.2 145.0 %all-gather.12.cloned.1.call-start = ((), (), s32[]{:S(2)}) async-start(), calls=%async_computation.12 | async-start | bytes 5898240 | tf_op jit(solution)/shard_map/all_gather | solution.py:165
  76.8 203.0 %all-gather.14.cloned.1.call-start = ((), (), s32[]{:S(2)}) async-start(), calls=%async_computation.13 | async-start | bytes 5898240 | tf_op jit(solution)/shard_map/all_gather | solution.py:166
  116.0 46.2 %copy-start.7 = (f32[1,128,768]{2,1,0:T(8,128)S(1)}, f32[1,128,768]{2,1,0:T(8,128)}, u32[]{:S(2)}) copy-start(f32[1,128,768]{2,1,0:T(8,128)} %param.12) | copy-start | bytes 1179652
  117.7 46.5 %copy-start.31 = (f32[768]{0:T(1024)S(1)}, f32[768]{0:T(1024)}, u32[]{:S(2)}) copy-start(f32[768]{0:T(1024)} %convert_element_type.218) | copy-start | bytes 9220
  117.7 46.6 %copy-start.32 = (s32[1024]{0:T(1024)S(1)}, s32[1024]{0:T(1024)}, u32[]{:S(2)}) copy-start(s32[1024]{0:T(1024)} %get-tuple-element.32) | copy-start | bytes 12292
  118.5 45.7 %copy-start.24 = (bf16[12,64,128]{2,1,0:T(8,128)(2,1)}, bf16[12,64,128]{2,1,0:T(8,128)(2,1)S(1)}, u32[]{:S(2)}) copy-start(bf16[12,64,128]{2,1,0:T(8,128)(2,1)S(1)} %convolution_convert_fusion.7) | copy-start | bytes 589828
  164.1 155.0 %copy-start.10 = (f32[128,768]{1,0:T(8,128)}, f32[128,768]{1,0:T(8,128)S(1)}, u32[]{:S(2)}) copy-start(f32[128,768]{1,0:T(8,128)S(1)} %get-tuple-element.27) | copy-start | bytes 1179652
  164.2 155.0 %copy-start.37 = (f32[128]{0:T(128)}, f32[128]{0:T(128)S(1)}, u32[]{:S(2)}) copy-start(f32[128]{0:T(128)S(1)} %add_rsqrt_fusion) | copy-start | bytes 1540
  167.5 19.0 %all-to-all-start = ((bf16[8,48,768]{2,1,0:T(8,128)(2,1)}), bf16[8,48,768]{2,1,0:T(8,128)(2,1)S(1)}, u32[]{:S(2)}, u32[]{:S(2)}) async-start(bf16[8,48,768]{2,1,0:T(8,128)(2,1)} %broadcast_select_fusion), calls=%async_computation | async-start | bytes 1179648 | tf_op jit(solution)/shard_map/all_to_all | solution.py:155
  186.5 41.2 %all-to-all-start.2 = ((bf16[8,48,768]{2,1,0:T(8,128)(2,1)}), bf16[8,48,768]{2,1,0:T(8,128)(2,1)S(1)}, u32[]{:S(2)}, u32[]{:S(2)}) async-start(bf16[8,48,768]{2,1,0:T(8,128)(2,1)} %select_convert_fusion), calls=%async_computation.2 | async-start | bytes 1179648 | tf_op jit(solution)/shard_map/all_to_all | solution.py:158
  227.7 59.8 %copy-start.27 = (bf16[8,48,768]{2,1,0:T(8,128)(2,1)}, bf16[8,48,768]{2,1,0:T(8,128)(2,1)S(1)}, u32[]{:S(2)}) copy-start(bf16[8,48,768]{2,1,0:T(8,128)(2,1)S(1)} %all-to-all-done.2) | copy-start | bytes 1769476
  290.4 18.6 %all-to-all-start.3 = ((bf16[8,48,768]{2,1,0:T(8,128)(2,1)}), bf16[8,48,768]{2,1,0:T(8,128)(2,1)S(1)}, u32[]{:S(2)}, u32[]{:S(2)}) async-start(bf16[8,48,768]{2,1,0:T(8,128)(2,1)} %bitcast.25), calls=%async_computation.3 | async-start | bytes 1179648 | tf_op jit(solution)/shard_map/all_to_all | solution.py:187
  309.0 20.2 %all-to-all-start.1 = ((bf16[8,48,768]{2,1,0:T(8,128)(2,1)}), bf16[8,48,768]{2,1,0:T(8,128)(2,1)S(1)}, u32[]{:S(2)}, u32[]{:S(2)}) async-start(bf16[8,48,768]{2,1,0:T(8,128)(2,1)} %bitcast.18), calls=%async_computation.1 | async-start | bytes 1179648 | tf_op jit(solution)/shard_map/all_to_all | solution.py:180
  315.7 62.7 %reduce-scatter.16.cloned.1.call-start = ((), (), s32[]{:S(2)}) async-start(), calls=%async_computation.18 | async-start | bytes 1966080
  346.4 93.5 %reduce-scatter.12.cloned.1.call-start = ((), (), s32[]{:S(2)}) async-start(), calls=%async_computation.16 | async-start | bytes 5898240 | tf_op jit(solution)/shard_map/reduce_scatter | solution.py:172
  352.6 147.2 %reduce-scatter.14.cloned.1.call-start = ((), (), s32[]{:S(2)}) async-start(), calls=%async_computation.17 | async-start | bytes 5898240 | tf_op jit(solution)/shard_map/reduce_scatter | solution.py:175
  361.3 243.0 %reduce-scatter.10.cloned.1.call-start = ((), (), s32[]{:S(2)}) async-start(), calls=%async_computation.15 | async-start | bytes 2433024 | tf_op jit(solution)/shard_map/reduce_scatter | solution.py:261
  365.3 363.6 %reduce-scatter.8.cloned.1.call-start = ((), (), s32[]{:S(2)}) async-start(), calls=%async_computation.14 | async-start | bytes 7299072 | tf_op jit(solution)/shard_map/reduce_scatter | solution.py:260
  395.4 43.6 %copy-start.13 = (f32[128,768]{1,0:T(8,128)S(1)}, f32[128,768]{1,0:T(8,128)}, u32[]{:S(2)}) copy-start(f32[128,768]{1,0:T(8,128)} %copy-done.11) | copy-start | bytes 1179652
  439.0 289.9 %copy-start.1 = (f32[32,12]{0,1:T(8,128)S(1)}, f32[32,12]{0,1:T(8,128)}, u32[]{:S(2)}) copy-start(f32[32,12]{0,1:T(8,128)} %param.19) | copy-start | bytes 4612
  (37 other events, 329.7 us)
Sparse Core Ops, SparseCore 0:
  10.9 59.4 all-gather.5
  75.6 31.1 all-gather.7
  109.7 52.5 all-gather.9
  163.9 57.2 all-gather.11
  222.9 56.9 all-gather.13
  346.6 31.8 reduce-scatter.15
  381.4 58.2 reduce-scatter.11
  442.7 57.0 reduce-scatter.13
  505.7 98.6 reduce-scatter.9
  610.4 118.4 reduce-scatter.7
where the time goes:
time: 748 us; the launch traced here: 736 us
  waiting for transfers between devices  475 us (64%)
  blocking collectives  82.7 us (11%)
  matrix products  73.2 us (10%)
  local copies, waits for them, and re-layouts  43.3 us (6%)
  starting transfers between devices  25 us (3%)
  other arithmetic  21.4 us (3%)
  between operations  15.3 us (2%)
    reduce_scatter x1, waiting for transfers between devices, local(): lax.psum_scatter(entry_grad, ('dp', 'seq', 'expert'), scatter_dimension=1...  125 us
    reduce_scatter x1, waiting for transfers between devices, local(): lax.psum_scatter(exit_grad, ('dp', 'seq', 'expert'), scatter_dimension=1,...  102 us
    unnamed x2, blocking collectives  82.7 us
    reduce_scatter x1, waiting for transfers between devices, local(): lax.psum_scatter(down_grad[None].astype(jnp.bfloat16), 'seq', scatter_dim...  57 us
    all_gather x1, waiting for transfers between devices, local(): lax.all_gather(expert_down, 'seq', axis=1, tiled=True)  52.1 us
    all_gather x1, waiting for transfers between devices, local(): lax.all_gather(exit_weight, ('dp', 'seq', 'expert'), axis=1, tiled=True)  43.7 us
    all_gather x1, waiting for transfers between devices, local(): lax.all_gather(expert_up, 'seq', axis=2, tiled=True)  28 us
    dot_general x4, matrix products, contract_rows(): lax.dot_general(left, right, (((0,), (0,)), ((), ())), preferred_element_...  21.8 us
  transfers between devices with their start and end apart: 14, of which 12 were waited for; matrix products, arithmetic and copies ran while one was open for 14% of the time, Pallas kernels for 0%

commit v1 on v0

v1 whole, which is shorter than its diff:
```python
import functools
import math

import jax
import jax.numpy as jnp
import numpy as np
from jax import lax
from jax.experimental import pallas as pl
from jax.experimental.pallas import tpu as pltpu
from jax.sharding import PartitionSpec as P

EPSILON = 1e-06
SLOPE = 0.7978845608028654
CUBIC = 0.044715
LIMITS = (19, 21, 24, 27, 31, 35, 40, 46, 52, 59, 67, 77, 87, 99, 113)
MASKED = -1e30
HIGH = lax.Precision.HIGHEST
ALL = ("dp", "seq", "expert")
GROUP = ("dp", "expert")
BLOCK = 128
BF = jnp.bfloat16
F32 = jnp.float32


def dot(left, right, left_dim, right_dim):
    return lax.dot_general(
        left, right, (((left_dim,), (right_dim,)), ((), ())), preferred_element_type=F32
    )


def rms_scale(values):
    return lax.rsqrt(jnp.mean(values * values, axis=-1, keepdims=True) + EPSILON)


def bucket_hot(lag, count):
    bucket = jnp.minimum(lag, 16)
    for threshold in LIMITS:
        bucket = bucket + (lag >= threshold).astype(jnp.int32)
    return (jnp.arange(count, dtype=jnp.int32)[:, None] == bucket[None, :]).astype(F32)


@functools.lru_cache(maxsize=None)
def weight_routes(features, columns, n_dp, n_seq, n_ex):
    width = features // n_seq
    chunk = math.gcd(columns, width)
    per = columns // chunk
    devices = n_dp * n_seq * n_ex
    edges = []
    for group in range(n_seq):
        index = 0
        for part in range(3):
            for i in range(width // chunk):
                piece = (part * features + group * width) // chunk + i
                ex, rest = divmod(index, n_dp * per)
                dp, slot = divmod(rest, per)
                target = (dp * n_seq + group) * n_ex + ex
                edges.append((piece // per, piece % per, target, slot))
                index += 1
    rounds = []
    left = list(edges)
    for _ in range(per):
        out_edges = [[] for _ in range(devices)]
        for edge in left:
            out_edges[edge[0]].append(edge)
        matched = {}

        def place(source, seen):
            for edge in out_edges[source]:
                if edge[2] in seen:
                    continue
                seen.add(edge[2])
                if edge[2] not in matched or place(matched[edge[2]][0], seen):
                    matched[edge[2]] = edge
                    return True
            return False

        for source in range(devices):
            assert place(source, set())
        rounds.append(sorted(matched.values()))
        for edge in matched.values():
            left.remove(edge)
    pairs = tuple(tuple((e[0], e[2]) for e in r) for r in rounds)
    send = np.zeros((devices, per), np.int32)
    receive = np.zeros((devices, per), np.int32)
    for m, r in enumerate(rounds):
        for source, sub, target, slot in r:
            send[source, m] = sub
            receive[target, slot] = m
    return chunk, per, pairs, send, receive


def inverse_rows(table):
    return np.argsort(table, axis=1).astype(np.int32)


def pick(stack, table, me):
    row = jnp.asarray(table)[me]
    return [
        lax.dynamic_index_in_dim(stack, row[j], axis=0, keepdims=False)
        for j in range(table.shape[1])
    ]


def spread_out(array, axis):
    count = lax.axis_size(axis)
    return lax.all_to_all(
        jnp.broadcast_to(array[None], (count,) + array.shape), axis, 0, 0, tiled=True
    )


def allowed_of(docs_row, docs_col, start, rows, keys):
    query = start + lax.broadcasted_iota(jnp.int32, (rows, keys), 0)
    key = lax.broadcasted_iota(jnp.int32, (rows, keys), 1)
    return (key <= query) & (docs_col[start : start + rows, :] == docs_row[:, :keys])


def bias_rows(lag_ref, head, start, rows, keys):
    length = lag_ref.shape[1]
    flat = jnp.broadcast_to(lag_ref[head : head + 1, :], (rows, length))
    return pltpu.roll(flat, start, 1, stride=1, stride_axis=0)[:, :keys]


def attend_kernel(
    heads, size, x_ref, gain_ref, w_ref, exit_ref, row_ref, col_ref, lag_ref,
    qkv_ref, ctx_ref, log_ref, part_ref,
):
    length = x_ref.shape[0]
    width = heads * size
    factor = size ** (-0.5)
    normed = (x_ref[...].astype(F32) * gain_ref[...]).astype(BF)
    qkv_ref[...] = dot(normed, w_ref[...], 1, 1).astype(BF)
    for start in range(0, length, BLOCK):
        keys = start + BLOCK
        allowed = allowed_of(row_ref, col_ref, start, BLOCK, keys)
        for head in range(heads):
            lo = head * size
            q = qkv_ref[start:keys, lo : lo + size]
            k = qkv_ref[:keys, width + lo : width + lo + size]
            v = qkv_ref[:keys, 2 * width + lo : 2 * width + lo + size]
            scores = dot(q, k, 1, 1) * factor + bias_rows(lag_ref, head, start, BLOCK, keys)
            scores = jnp.where(allowed, scores, MASKED)
            peak = jnp.max(scores, axis=1, keepdims=True)
            raised = jnp.exp(scores - peak)
            total = jnp.sum(raised, axis=1, keepdims=True)
            weights = (raised / total).astype(BF)
            log_ref[start:keys, head : head + 1] = peak + jnp.log(total)
            ctx_ref[start:keys, lo : lo + size] = dot(weights, v, 1, 0).astype(BF)
    part_ref[...] = dot(ctx_ref[...], exit_ref[...], 1, 1).astype(BF)


def attend(heads, size, xhat, gain, w, exit_t, docs_row, docs_col, lag):
    length, features = xhat.shape
    width = heads * size
    return pl.pallas_call(
        functools.partial(attend_kernel, heads, size),
        out_shape=(
            jax.ShapeDtypeStruct((length, 3 * width), BF),
            jax.ShapeDtypeStruct((length, width), BF),
            jax.ShapeDtypeStruct((length, heads), F32),
            jax.ShapeDtypeStruct((length, features), BF),
        ),
        name="attend",
    )(xhat, gain, w, exit_t, docs_row, docs_col, lag)


def attend_back_kernel(
    heads, size, up_ref, exit_ref, qkv_ref, ctx_ref, log_ref, row_ref, col_ref, lag_ref,
    x_ref, gain_ref, w_ref,
    entry_ref, exit_grad_ref, back_ref, diag_ref, gain_grad_ref,
    bctx_ref, bqkv_ref, bk_ref, bv_ref, lines_ref,
):
    length = up_ref.shape[0]
    width = heads * size
    factor = size ** (-0.5)
    bctx_ref[...] = dot(up_ref[...], exit_ref[...], 1, 0).astype(BF)
    exit_grad_ref[...] = dot(up_ref[...], ctx_ref[...], 0, 0).astype(BF)
    bk_ref[...] = jnp.zeros_like(bk_ref)
    bv_ref[...] = jnp.zeros_like(bv_ref)
    lines_ref[...] = jnp.zeros_like(lines_ref)
    for start in range(0, length, BLOCK):
        keys = start + BLOCK
        allowed = allowed_of(row_ref, col_ref, start, BLOCK, keys)
        for head in range(heads):
            lo = head * size
            q = qkv_ref[start:keys, lo : lo + size]
            k = qkv_ref[:keys, width + lo : width + lo + size]
            v = qkv_ref[:keys, 2 * width + lo : 2 * width + lo + size]
            bc = bctx_ref[start:keys, lo : lo + size]
            scores = dot(q, k, 1, 1) * factor + bias_rows(lag_ref, head, start, BLOCK, keys)
            probs = jnp.where(
                allowed, jnp.exp(scores - log_ref[start:keys, head : head + 1]), 0.0
            )
            back_probs = dot(bc, v, 1, 1)
            row_dot = jnp.sum(probs * back_probs, axis=1, keepdims=True)
            back_scores = probs * (back_probs - row_dot)
            scaled = (back_scores * factor).astype(BF)
            bqkv_ref[start:keys, lo : lo + size] = dot(scaled, k, 1, 0).astype(BF)
            bk_ref[:keys, lo : lo + size] += dot(scaled, q, 0, 0)
            bv_ref[:keys, lo : lo + size] += dot(probs.astype(BF), bc, 0, 0)
            lined = jnp.zeros((8, keys), F32)
            for row in range(0, BLOCK, 8):
                lined = lined + pltpu.roll(
                    back_scores[row : row + 8, :], (keys - start - row - 8) % keys, 1
                )
            lines_ref[8 * head : 8 * head + 8, length - keys :] += lined
    for head in range(heads):
        total = jnp.zeros((1, length), F32)
        for row in range(8):
            total = total + pltpu.roll(
                lines_ref[8 * head + row : 8 * head + row + 1, :], 7 - row, 1
            )
        diag_ref[head : head + 1, :] = total
    bqkv_ref[:, width : 2 * width] = bk_ref[...].astype(BF)
    bqkv_ref[:, 2 * width :] = bv_ref[...].astype(BF)
    normed = (x_ref[...].astype(F32) * gain_ref[...]).astype(BF)
    entry_ref[...] = dot(bqkv_ref[...], normed, 0, 0).astype(BF)
    back = dot(bqkv_ref[...], w_ref[...], 1, 0)
    back_ref[...] = back.astype(BF)
    gain_grad_ref[...] = jnp.sum(back * x_ref[...].astype(F32), axis=0, keepdims=True)


def attend_back(heads, size, up, exit_t, qkv, ctx, log, docs_row, docs_col, lag, xhat, gain, w):
    length, features = up.shape
    width = heads * size
    return pl.pallas_call(
        functools.partial(attend_back_kernel, heads, size),
        out_shape=(
            jax.ShapeDtypeStruct((3 * width, features), BF),
            jax.ShapeDtypeStruct((features, width), BF),
            jax.ShapeDtypeStruct((length, features), BF),
            jax.ShapeDtypeStruct((heads, length), F32),
            jax.ShapeDtypeStruct((1, features), F32),
        ),
        scratch_shapes=[
            pltpu.VMEM((length, width), BF),
            pltpu.VMEM((length, 3 * width), BF),
            pltpu.VMEM((length, width), F32),
            pltpu.VMEM((length, width), F32),
            pltpu.VMEM((8 * heads, length), F32),
        ],
        name="attend_back",
    )(up, exit_t, qkv, ctx, log, docs_row, docs_col, lag, xhat, gain, w)


def expert_kernel(rows_ref, up_ref, w_up_ref, w_down_ref, back_ref, result_ref, act_ref, bb_ref):
    before = dot(rows_ref[...], w_up_ref[...], 1, 0)
    tangent = jnp.tanh(SLOPE * (before + CUBIC * before * before * before))
    act_ref[...] = (0.5 * before * (1.0 + tangent)).astype(BF)
    slope = 0.5 * (1.0 + tangent) + 0.5 * before * (1.0 - tangent * tangent) * SLOPE * (
        1.0 + 3.0 * CUBIC * before * before
    )
    bb_ref[...] = (dot(up_ref[...], w_down_ref[...], 1, 1) * slope).astype(BF)
    back_ref[...] = dot(bb_ref[...], w_up_ref[...], 1, 1).astype(BF)
    result_ref[...] = dot(act_ref[...], w_down_ref[...], 1, 0).astype(BF)


def expert(rows, upstream, w_up, w_down):
    count, features = rows.shape
    hidden = w_up.shape[1]
    return pl.pallas_call(
        expert_kernel,
        out_shape=(
            jax.ShapeDtypeStruct((count, features), BF),
            jax.ShapeDtypeStruct((count, features), BF),
            jax.ShapeDtypeStruct((count, hidden), BF),
            jax.ShapeDtypeStruct((count, hidden), BF),
        ),
        name="expert",
    )(rows, upstream, w_up, w_down)


def expert_grad_kernel(count, *refs):
    rows, bbs = refs[:count], refs[count : 2 * count]
    acts, ups = refs[2 * count : 3 * count], refs[3 * count : 4 * count]
    up_ref, down_ref = refs[4 * count :]
    total = dot(rows[0][...], bbs[0][...], 0, 0)
    for i in range(1, count):
        total = total + dot(rows[i][...], bbs[i][...], 0, 0)
    up_ref[...] = total
    total = dot(acts[0][...], ups[0][...], 0, 0)
    for i in range(1, count):
        total = total + dot(acts[i][...], ups[i][...], 0, 0)
    down_ref[...] = total


def expert_grad(rows, bbs, acts, ups):
    features, hidden = rows[0].shape[1], bbs[0].shape[1]
    return pl.pallas_call(
        functools.partial(expert_grad_kernel, len(rows)),
        out_shape=(
            jax.ShapeDtypeStruct((features, hidden), F32),
            jax.ShapeDtypeStruct((hidden, features), F32),
        ),
        name="expert_grad",
    )(*rows, *bbs, *acts, *ups)


def ring(count, step):
    if count & (count - 1) == 0:
        return tuple((i, i ^ step) for i in range(count))
    return tuple((i, (i + step) % count) for i in range(count))


def back_ring(count, step):
    return tuple((b, a) for a, b in ring(count, step))


def local(
    block_input,
    documents,
    route_experts,
    route_gate,
    first_gain,
    entry_weight,
    exit_weight,
    position_bias,
    second_gain,
    expert_up,
    expert_down,
    cotangent,
):
    n_dp, n_seq, n_ex = (lax.axis_size(name) for name in ALL)
    devices = n_dp * n_seq * n_ex
    rows_here, features = block_input.shape[1:]
    buckets, head_count = position_bias.shape
    size = features // head_count
    heads = head_count // n_seq
    width = heads * size
    top_count = route_experts.shape[2]
    length = rows_here * n_seq
    me = lax.axis_index(ALL)
    here = lax.axis_index("seq")
    inputs = block_input.reshape(rows_here, features)
    upstream = cotangent.reshape(rows_here, features)

    owned = entry_weight.shape[1]
    share = exit_weight.shape[1]
    chunk, per, pairs, send, receive = weight_routes(features, owned, n_dp, n_seq, n_ex)
    pieces = pick(entry_weight.T.reshape(per, chunk, features), send, me)
    came = [lax.ppermute(piece, ALL, pair) for piece, pair in zip(pieces, pairs)]
    entry_mine = jnp.concatenate(pick(jnp.stack(came), receive, me), axis=0)
    entry_half = spread_out(entry_mine, "dp").reshape(n_dp * owned, features)
    entry_t = lax.all_gather(entry_half, "expert", axis=0, tiled=True)

    extra = -(-2 * share // width)
    gains = jnp.concatenate([first_gain, second_gain])
    gains = jnp.pad(gains, (0, extra * width - 2 * share)).reshape(1, extra, width)
    exit_send = jnp.concatenate(
        [
            exit_weight.T.reshape(share, n_seq, width).transpose(1, 0, 2),
            jnp.broadcast_to(gains, (n_seq, extra, width)),
        ],
        axis=1,
    )
    exit_send = jnp.broadcast_to(
        exit_send[None, :, None], (n_dp, n_seq, n_ex, share + extra, width)
    ).reshape(devices, share + extra, width)
    exit_came = lax.all_to_all(exit_send, ALL, 0, 0, tiled=True)
    exit_t = exit_came[:, :share].reshape(features, width)
    gains = exit_came[:, share:].reshape(devices, extra * width).astype(F32)
    gain_one = gains[:, :share].reshape(1, features)
    gain_two = gains[:, share : 2 * share].reshape(1, features)

    scale_one = rms_scale(inputs)
    xhat = spread_out((inputs * scale_one).astype(BF), "seq").reshape(length, features)
    docs = documents.reshape(length)
    docs_row, docs_col = docs.reshape(1, length), docs.reshape(length, 1)
    lane = jnp.arange(length, dtype=jnp.int32)
    hot = bucket_hot(jnp.where(lane == 0, 0, length - lane), buckets)
    bias_here = lax.dynamic_slice_in_dim(position_bias.T, here * heads, heads)
    lag = jnp.dot(bias_here, hot, precision=HIGH)
    qkv, ctx, log, part = attend(
        heads, size, xhat, gain_one, entry_t, exit_t, docs_row, docs_col, lag
    )

    group_size = n_dp * n_ex
    capacity = 3 * rows_here // group_size
    slots = group_size * capacity
    route_count = rows_here * top_count
    flat_routes = route_experts.reshape(rows_here, top_count).T.reshape(1, route_count)
    gates = route_gate.reshape(rows_here, top_count)
    named = flat_routes == jnp.arange(group_size, dtype=jnp.int32)[:, None]
    order = jnp.arange(route_count, dtype=jnp.int32)
    earlier = (order[:, None] < order[None, :]).astype(BF)
    rank = jnp.dot(named.astype(BF), earlier, preferred_element_type=F32)
    first = (jnp.arange(group_size, dtype=jnp.int32) * capacity).astype(F32)[:, None]
    slot_of = jnp.sum(jnp.where(named, rank + first, 0.0), axis=0, keepdims=True)
    place = (
        jnp.arange(slots, dtype=jnp.int32)[:, None] == slot_of.astype(jnp.int32)
    ).astype(BF)
    place_each = [place[:, k * rows_here : (k + 1) * rows_here] for k in range(top_count)]
    place_any = functools.reduce(jnp.add, place_each)
    shaped = (group_size, capacity, features)

    gated = jnp.concatenate(
        [(upstream * gates[:, k : k + 1]).astype(BF) for k in range(top_count)], axis=0
    )
    send_upstream = dot(place, gated, 1, 0).astype(BF)
    send_upstream, _ = lax.optimization_barrier((send_upstream, entry_t))
    came_upstream = lax.all_to_all(
        send_upstream.reshape(shaped), GROUP, 0, 0, tiled=True
    ).reshape(slots, features)
    ups = [came_upstream] + [
        lax.ppermute(came_upstream, "seq", ring(n_seq, m)) for m in range(1, n_seq)
    ]

    parts = lax.all_to_all(part.reshape(n_seq, rows_here, features), "seq", 0, 0, tiled=True)
    hidden = inputs + jnp.sum(parts.astype(F32), axis=0)
    scale_two = rms_scale(hidden)
    normed_two = (hidden * scale_two * gain_two).astype(BF)

    send_rows = dot(place_any, normed_two, 1, 0).astype(BF)
    came_rows = lax.all_to_all(
        send_rows.reshape(shaped), GROUP, 0, 0, tiled=True
    ).reshape(slots, features)
    rows = [came_rows] + [
        lax.ppermute(came_rows, "seq", ring(n_seq, m)) for m in range(1, n_seq)
    ]
    w_up, w_down = expert_up[0], expert_down[0]
    worked = [expert(rows[m], ups[m], w_up, w_down) for m in range(n_seq)]
    backs = [worked[0][0]] + [
        lax.ppermute(worked[m][0], "seq", back_ring(n_seq, m)) for m in range(1, n_seq)
    ]
    back_sum = functools.reduce(jnp.add, [b.astype(F32) for b in backs]).astype(BF)
    returned_back = lax.all_to_all(
        back_sum.reshape(shaped), GROUP, 0, 0, tiled=True
    ).reshape(slots, features)
    up_grad, down_grad = expert_grad(
        rows, [w[3] for w in worked], [w[2] for w in worked], ups
    )

    back_normed_two = dot(place_any, returned_back, 0, 0)
    upper_two = back_normed_two * gain_two
    gain_two_grad = jnp.sum(back_normed_two * hidden * scale_two, axis=0)
    back_hidden = upstream + scale_two * (
        upper_two
        - hidden * scale_two * scale_two * jnp.mean(upper_two * hidden, axis=1, keepdims=True)
    )
    up_hidden = spread_out(back_hidden.astype(BF), "seq").reshape(length, features)

    results = [w[1] for w in worked]
    *results, _ = lax.optimization_barrier((*results, back_sum))
    outs = [results[0]] + [
        lax.ppermute(results[m], "seq", back_ring(n_seq, m)) for m in range(1, n_seq)
    ]
    out_sum = functools.reduce(jnp.add, [o.astype(F32) for o in outs]).astype(BF)
    returned_out = lax.all_to_all(
        out_sum.reshape(shaped), GROUP, 0, 0, tiled=True
    ).reshape(slots, features)
    block_output = hidden
    for k in range(top_count):
        block_output = block_output + dot(place_each[k], returned_out, 0, 0) * gates[:, k : k + 1]

    entry_grad, exit_grad, back, diag, gain_one_grad = attend_back(
        heads, size, up_hidden, exit_t, qkv, ctx, log, docs_row, docs_col, lag,
        xhat, gain_one, entry_t,
    )
    halves = lax.all_to_all(
        entry_grad.reshape(n_ex, n_dp * owned, features), "expert", 0, 0, tiled=True
    )
    half = jnp.sum(halves.astype(F32), axis=0).astype(BF).reshape(n_dp, owned, features)
    mine = jnp.sum(lax.all_to_all(half, "dp", 0, 0, tiled=True).astype(F32), axis=0)
    pieces = pick(mine.reshape(per, chunk, features), inverse_rows(receive), me)
    came = [
        lax.ppermute(piece, ALL, tuple((b, a) for a, b in pair))
        for piece, pair in zip(pieces, pairs)
    ]
    entry_share = jnp.concatenate(pick(jnp.stack(came), inverse_rows(send), me), axis=0).T

    backs = lax.all_to_all(back.reshape(n_seq, rows_here, features), "seq", 0, 0, tiled=True)
    back_normed_one = jnp.sum(backs.astype(F32), axis=0)
    upper_one = back_normed_one * gain_one
    back_input = back_hidden + scale_one * (
        upper_one
        - inputs * scale_one * scale_one * jnp.mean(upper_one * inputs, axis=1, keepdims=True)
    )

    hot_back = bucket_hot(length - 1 - lane, buckets)
    bias_grad = jnp.dot(hot_back, diag.T, precision=HIGH)
    small = jnp.concatenate(
        [
            gain_one_grad.reshape(devices, share),
            gain_two_grad.reshape(devices, share),
            jnp.broadcast_to(bias_grad.reshape(1, buckets * heads), (devices, buckets * heads)),
        ],
        axis=1,
    )
    count = 2 * share + buckets * heads
    lines = -(-count // width)
    small = jnp.pad(small, ((0, 0), (0, lines * width - count))).reshape(devices, lines, width)
    upper = lax.reduce_precision(small, 8, 7)
    exit_send = jnp.concatenate(
        [
            exit_grad.reshape(devices, share, width),
            upper.astype(BF),
            (small - upper).astype(BF),
        ],
        axis=1,
    )
    exit_came = lax.all_to_all(exit_send, ALL, 0, 0, tiled=True).astype(F32)
    exit_came = exit_came.reshape(n_dp, n_seq, n_ex, share + 2 * lines, width)
    exit_came = jnp.sum(exit_came, axis=(0, 2))
    exit_share = exit_came[:, :share].transpose(0, 2, 1).reshape(features, share)
    small = (exit_came[:, share : share + lines] + exit_came[:, share + lines :]).reshape(
        n_seq, lines * width
    )
    gain_one_share = jnp.sum(small[:, :share], axis=0)
    gain_two_share = jnp.sum(small[:, share : 2 * share], axis=0)
    bias_total = (
        small[:, 2 * share : count]
        .reshape(n_seq, buckets, heads)
        .transpose(1, 0, 2)
        .reshape(buckets, head_count)
    )
    return (
        block_output.reshape(block_input.shape),
        back_input.reshape(block_input.shape),
        gain_one_share,
        entry_share,
        exit_share,
        bias_total,
        gain_two_share,
        up_grad[None],
        down_grad[None],
    )


def solution(mesh):
    tokens = P(("dp", "expert"), "seq", None)
    columns = P(None, ALL)
    placed = (
        tokens,
        P(("dp", "expert"), None),
        tokens,
        tokens,
        P(ALL),
        columns,
        columns,
        P(),
        P(ALL),
        P(("dp", "expert"), None, "seq"),
        P(("dp", "expert"), "seq", None),
        tokens,
    )
    return jax.shard_map(
        local,
        mesh=mesh,
        in_specs=placed,
        out_specs=(
            tokens,
            tokens,
            P(ALL),
            columns,
            columns,
            P(),
            P(ALL),
            P(("dp", "expert"), None, "seq"),
            P(("dp", "expert"), "seq", None),
        ),
        check_vma=False,
    )
```

time: 748 us -> 356 us (0.48); the launches traced: 736 us -> 354 us
  waiting for transfers between devices: 475 us -> 144 us
  blocking collectives: 82.7 us -> 8.1 us
  starting transfers between devices: 25 us -> 98.9 us
  matrix products: 73.2 us -> 5.88 us
  Pallas kernels: 0 us -> 49.4 us
  local copies, waits for them, and re-layouts: 43.3 us -> 15 us
    reduce_scatter x4 -> x0, waiting for transfers between devices: 283 us -> none  [the longest x1 125 us: local(): lax.psum_scatter(entry_grad, ('dp', 'seq', 'expert'), scatter_dimension=1...]
    all_gather x5 -> x0, waiting for transfers between devices: 157 us -> none  [the longest x1 52.1 us: local(): lax.all_gather(expert_down, 'seq', axis=1, tiled=True)]
    unnamed x2 -> x0, blocking collectives: 82.7 us -> none
    all_to_all x4 -> x12, waiting for transfers between devices: 22.1 us -> 90.8 us  [the longest x3 22.1 us: spread_out(): lax.all_to_all(jnp.broadcast_to(array[None], (count,) + array.shape), axi...]
    dot_general x20 -> x8, matrix products: 73.2 us -> 5.88 us  [the longest x5 4.12 us: dot(): lax.dot_general(left, right, (((left_dim,), (right_dim,)), ((), ())), pre...]
    ppermute x0 -> x18, waiting for transfers between devices: none -> 53.1 us  [the longest x3 25.5 us: local(): lax.ppermute(came_rows, 'seq', ring(n_seq, m))]
    pallas_call x0 -> x7, Pallas kernels: none -> 49.4 us  [the longest x4 20.5 us: expert(): pl.pallas_call(expert_kernel, out_shape=(jax.ShapeDtypeStruct((count, fea...]
    all_to_all x4 -> x12, starting transfers between devices: 24.2 us -> 63.1 us  [the longest x3 12.7 us: spread_out(): lax.all_to_all(jnp.broadcast_to(array[None], (count,) + array.shape), axi...]
  transfers between devices with their start and end apart: 14 -> 30, of which waited for: 12 -> 19; matrix products, arithmetic and copies ran while one was open for 14% -> 7% of each run, Pallas kernels for 0% -> 12%
where the time goes in v1:
time: 356 us; the launch traced here: 354 us
  waiting for transfers between devices  144 us (40%)
  starting transfers between devices  98.9 us (28%)
  Pallas kernels  49.4 us (14%)
  between operations  18.7 us (5%)
  local copies, waits for them, and re-layouts  15 us (4%)
  other arithmetic  14 us (4%)
  blocking collectives  8.1 us (2%)
  matrix products  5.88 us (2%)
    ppermute x3, waiting for transfers between devices, local(): lax.ppermute(came_rows, 'seq', ring(n_seq, m))  25.5 us
    all_to_all x3, waiting for transfers between devices, spread_out(): lax.all_to_all(jnp.broadcast_to(array[None], (count,) + array.shape), axi...  22.1 us
    pallas_call x4, Pallas kernels, expert(): pl.pallas_call(expert_kernel, out_shape=(jax.ShapeDtypeStruct((count, fea...  20.5 us
    all_to_all x3, starting transfers between devices, spread_out(): lax.all_to_all(jnp.broadcast_to(array[None], (count,) + array.shape), axi...  12.7 us
    all_to_all x1, waiting for transfers between devices, local(): lax.all_to_all(send_rows.reshape(shaped), GROUP, 0, 0, tiled=True)  12 us
    all_to_all x1, waiting for transfers between devices, local(): exit_came = lax.all_to_all(exit_send, ALL, 0, 0, tiled=True).astype(F32)  11.9 us
    ppermute x3, starting transfers between devices, local(): lax.ppermute(piece, ALL, tuple(((b, a) for a, b in pair)))  11.1 us
    all_to_all x1, waiting for transfers between devices, local(): lax.all_to_all(send_upstream.reshape(shaped), GROUP, 0, 0, tiled=True)  10.9 us
  transfers between devices with their start and end apart: 30, of which 19 were waited for; matrix products, arithmetic and copies ran while one was open for 7% of the time, Pallas kernels for 12%

profile of v1, /device:TPU:18, one launch (start us, length us, event | category | flops | bytes accessed | tf_op | source)
XLA Modules:
  0.0 353.8 jit_solution(6426687591490102257)
XLA Ops:
  3.3 5.9 %all-to-all-start.1 = ((bf16[32,25,192]{2,1,0:T(8,128)(2,1)}), bf16[32,25,192]{2,1,0:T(8,128)(2,1)S(1)}, u32[]{:S(2)}, u32[]{:S(2)}) async-start(bf16[32,25,192]{2,1,0:T(8,128)(2,1)} %bitcast.5), calls=%async_computation.1 | async-start | bytes 1048576 | tf_op jit(solution)/shard_map/all_to_all | solution.py:358
  41.6 10.0 %all-to-all-done.2 = bf16[4,72,768]{2,1,0:T(8,128)(2,1)S(1)} async-done(((bf16[4,72,768]{2,1,0:T(8,128)(2,1)}), bf16[4,72,768]{2,1,0:T(8,128)(2,1)S(1)}, u32[]{:S(2)}, u32[]{:S(2)}) %all-to-all-start.2) | async-done | bytes 442400 | tf_op jit(solution)/shard_map/all_to_all | solution.py:106
  60.2 6.9 %all-to-all-done = bf16[4,128,768]{2,1,0:T(8,128)(2,1)S(1)} async-done(((bf16[4,128,768]{2,1,0:T(8,128)(2,1)}), bf16[4,128,768]{2,1,0:T(8,128)(2,1)S(1)}, u32[]{:S(2)}, u32[]{:S(2)}) %all-to-all-start) | async-done | bytes 786464 | tf_op jit(solution)/shard_map/all_to_all | solution.py:106
  68.0 7.9 %attend.1 = (bf16[512,576]{1,0:T(8,128)(2,1)}, bf16[512,192]{1,0:T(8,128)(2,1)}, f32[512,3]{1,0:T(8,128)}, bf16[512,768]{1,0:T(8,128)(2,1)}) custom-call(bf16[512,768]{1,0:T(8,128)(2,1)} %bitcast.148, f32[1,768]{1,0:T(1,128)} %reshape.319.gain_ref, bf16[576,768]{1,0:T(8,128)(2,1)} %all_gather.3.w_ref, bf16[768,192]{1,0:T(8,128)(2,1)} %bitcast.162, ...), custom_call_target="tpu_custom_call" | custom-call | tf_op jit(solution)/shard_map/attend/pallas_call | solution.py:154
  81.5 9.1 %all-to-all-done.3 = bf16[4,128,768]{2,1,0:T(8,128)(2,1)S(1)} async-done(((bf16[4,128,768]{2,1,0:T(8,128)(2,1)}), bf16[4,128,768]{2,1,0:T(8,128)(2,1)S(1)}, u32[]{:S(2)}, u32[]{:S(2)}) %all-to-all-start.3) | async-done | bytes 786464 | tf_op jit(solution)/shard_map/all_to_all | solution.py:407
  90.6 6.4 %all-to-all-start.5 = ((bf16[8,48,768]{2,1,0:T(8,128)(2,1)}), bf16[8,48,768]{2,1,0:T(8,128)(2,1)S(1)}, u32[]{:S(2)}, u32[]{:S(2)}) async-start(bf16[8,48,768]{2,1,0:T(8,128)(2,1)} %bitcast.37), calls=%async_computation.5 | async-start | bytes 1179648 | tf_op jit(solution)/shard_map/all_to_all | solution.py:400
  99.5 10.9 %all-to-all-done.5 = bf16[8,48,768]{2,1,0:T(8,128)(2,1)S(1)} async-done(((bf16[8,48,768]{2,1,0:T(8,128)(2,1)}), bf16[8,48,768]{2,1,0:T(8,128)(2,1)S(1)}, u32[]{:S(2)}, u32[]{:S(2)}) %all-to-all-start.5) | async-done | bytes 589856 | tf_op jit(solution)/shard_map/all_to_all | solution.py:400
  110.4 6.7 %all-to-all-start.4 = ((bf16[8,48,768]{2,1,0:T(8,128)(2,1)}), bf16[8,48,768]{2,1,0:T(8,128)(2,1)S(1)}, u32[]{:S(2)}, u32[]{:S(2)}) async-start(bf16[8,48,768]{2,1,0:T(8,128)(2,1)} %bitcast.31), calls=%async_computation.4 | async-start | bytes 1179648 | tf_op jit(solution)/shard_map/all_to_all | solution.py:413
  118.6 12.0 %all-to-all-done.4 = bf16[8,48,768]{2,1,0:T(8,128)(2,1)S(1)} async-done(((bf16[8,48,768]{2,1,0:T(8,128)(2,1)}), bf16[8,48,768]{2,1,0:T(8,128)(2,1)S(1)}, u32[]{:S(2)}, u32[]{:S(2)}) %all-to-all-start.4) | async-done | bytes 589856 | tf_op jit(solution)/shard_map/all_to_all | solution.py:413
  136.2 11.6 %collective-permute-done.7.rows_ref.refs_3_ = bf16[384,768]{1,0:T(8,128)(2,1)S(1)} collective-permute-done((bf16[384,768]{1,0:T(8,128)(2,1)S(1)}, bf16[384,768]{1,0:T(8,128)(2,1)S(1)}, u32[]{:S(2)}, u32[]{:S(2)}) %collective-permute-start.7) | collective-permute-done | bytes 589856 | tf_op jit(solution)/shard_map/ppermute | solution.py:417
  159.1 13.9 %collective-permute-done.5.rows_ref.refs_2_ = bf16[384,768]{1,0:T(8,128)(2,1)} collective-permute-done((bf16[384,768]{1,0:T(8,128)(2,1)S(1)}, bf16[384,768]{1,0:T(8,128)(2,1)}, u32[]{:S(2)}, u32[]{:S(2)}) %collective-permute-start.5) | collective-permute-done | bytes 589856 | tf_op jit(solution)/shard_map/ppermute | solution.py:417
  190.5 6.4 %collective-permute-done.10 = bf16[384,768]{1,0:T(8,128)(2,1)S(1)} collective-permute-done((bf16[384,768]{1,0:T(8,128)(2,1)}, bf16[384,768]{1,0:T(8,128)(2,1)S(1)}, u32[]{:S(2)}, u32[]{:S(2)}) %collective-permute-start.10) | collective-permute-done | bytes 589856 | tf_op jit(solution)/shard_map/ppermute | solution.py:422
  201.2 6.9 %all-to-all-start.7 = ((bf16[8,48,768]{2,1,0:T(8,128)(2,1)}), bf16[8,48,768]{2,1,0:T(8,128)(2,1)S(1)}, u32[]{:S(2)}, u32[]{:S(2)}) async-start(bf16[8,48,768]{2,1,0:T(8,128)(2,1)} %bitcast.44), calls=%async_computation.7 | async-start | bytes 1179648 | tf_op jit(solution)/shard_map/all_to_all | solution.py:425
  211.5 10.0 %all-to-all-done.7 = bf16[8,48,768]{2,1,0:T(8,128)(2,1)S(1)} async-done(((bf16[8,48,768]{2,1,0:T(8,128)(2,1)}), bf16[8,48,768]{2,1,0:T(8,128)(2,1)S(1)}, u32[]{:S(2)}, u32[]{:S(2)}) %all-to-all-start.7) | async-done | bytes 589856 | tf_op jit(solution)/shard_map/all_to_all | solution.py:425
  228.7 8.5 %collective-permute-done.13 = bf16[384,768]{1,0:T(8,128)(2,1)S(1)} collective-permute-done((bf16[384,768]{1,0:T(8,128)(2,1)}, bf16[384,768]{1,0:T(8,128)(2,1)S(1)}, u32[]{:S(2)}, u32[]{:S(2)}) %collective-permute-start.13) | collective-permute-done | bytes 589856 | tf_op jit(solution)/shard_map/ppermute | solution.py:444
  240.4 5.2 %all-to-all-done.8 = bf16[4,128,768]{2,1,0:T(8,128)(2,1)S(1)} async-done(((bf16[4,128,768]{2,1,0:T(8,128)(2,1)}), bf16[4,128,768]{2,1,0:T(8,128)(2,1)S(1)}, u32[]{:S(2)}, u32[]{:S(2)}) %all-to-all-start.8) | async-done | bytes 786464 | tf_op jit(solution)/shard_map/all_to_all | solution.py:106
  257.2 10.8 %expert_grad.1 = (f32[768,768]{1,0:T(8,128)}, f32[768,768]{1,0:T(8,128)}) custom-call(bf16[384,768]{1,0:T(8,128)(2,1)} %bitcast.159, bf16[384,768]{1,0:T(8,128)(2,1)} %collective-permute-done.3.rows_ref.refs_1_, bf16[384,768]{1,0:T(8,128)(2,1)} %collective-permute-done.5.rows_ref.refs_2_, bf16[384,768]{1,0:T(8,128)(2,1)} %copy-done.7, ...), custom_call_target="tpu_custom_call" | custom-call | tf_op jit(solution)/shard_map/expert_grad/pallas_call | solution.py:288
  268.1 10.3 %attend_back.1 = (bf16[576,768]{1,0:T(8,128)(2,1)}, bf16[768,192]{1,0:T(8,128)(2,1)}, bf16[512,768]{1,0:T(8,128)(2,1)}, f32[3,512]{1,0:T(4,128)}, f32[1,768]{1,0:T(1,128)}) custom-call(bf16[512,768]{1,0:T(8,128)(2,1)} %bitcast.164, bf16[768,192]{1,0:T(8,128)(2,1)} %bitcast.163, bf16[512,576]{1,0:T(8,128)(2,1)} %get-tuple-element.55.qkv_ref, ...), custom_call_target="tpu_custom_call" | custom-call | tf_op jit(solution)/shard_map/attend_back/pallas_call | solution.py:225
  280.3 5.5 %all_to_all.65 = bf16[2,288,768]{2,1,0:T(8,128)(2,1)S(1)} all-to-all(bf16[2,288,768]{2,1,0:T(8,128)(2,1)} %bitcast.168), channel_id=1, replica_groups=mesh['dp'=4,'seq'=4,'expert'=2] {'expert'}, dimensions={0} | all-to-all | bytes 1769472 | tf_op jit(solution)/shard_map/all_to_all | solution.py:458
  294.3 7.3 %all-to-all-done.9 = bf16[4,128,768]{2,1,0:T(8,128)(2,1)S(1)} async-done(((bf16[4,128,768]{2,1,0:T(8,128)(2,1)}), bf16[4,128,768]{2,1,0:T(8,128)(2,1)S(1)}, u32[]{:S(2)}, u32[]{:S(2)}) %all-to-all-start.9) | async-done | bytes 786464 | tf_op jit(solution)/shard_map/all_to_all | solution.py:470
  307.8 11.9 %all-to-all-done.10 = bf16[32,26,192]{2,1,0:T(8,128)(2,1)S(1)} async-done(((bf16[32,26,192]{2,1,0:T(8,128)(2,1)}), bf16[32,26,192]{2,1,0:T(8,128)(2,1)S(1)}, u32[]{:S(2)}, u32[]{:S(2)}) %all-to-all-start.10) | async-done | bytes 319520 | tf_op jit(solution)/shard_map/all_to_all | solution.py:500
  319.7 5.4 %all-to-all-start.12 = ((bf16[4,72,768]{2,1,0:T(8,128)(2,1)}), bf16[4,72,768]{2,1,0:T(8,128)(2,1)S(1)}, u32[]{:S(2)}, u32[]{:S(2)}) async-start(bf16[4,72,768]{2,1,0:T(8,128)(2,1)} %bitcast.54), calls=%async_computation.12 | async-start | bytes 884736 | tf_op jit(solution)/shard_map/all_to_all | solution.py:462
  327.9 7.6 %all-to-all-done.12 = bf16[4,72,768]{2,1,0:T(8,128)(2,1)S(1)} async-done(((bf16[4,72,768]{2,1,0:T(8,128)(2,1)}), bf16[4,72,768]{2,1,0:T(8,128)(2,1)S(1)}, u32[]{:S(2)}, u32[]{:S(2)}) %all-to-all-start.12) | async-done | bytes 442400 | tf_op jit(solution)/shard_map/all_to_all | solution.py:462
  335.5 5.5 %collective-permute-start.17 = (f32[24,768]{1,0:T(8,128)S(1)}, f32[24,768]{1,0:T(8,128)S(1)}, u32[]{:S(2)}, u32[]{:S(2)}) collective-permute-start(f32[24,768]{1,0:T(8,128)S(1)} %get-tuple-element.87), channel_id=1, source_target_pairs={{0,0},{8,1},{2,2},{10,3},{18,4},{4,5},{12,6},{20,7},{6,8},{14,9},{... | collective-permute-start | bytes 221192 | tf_op jit(solution)/shard_map/ppermute | solution.py:465
  (181 shorter events, 132.8 us)
Async XLA Ops:
  3.3 32.5 %all-to-all-start.1 = ((bf16[32,25,192]{2,1,0:T(8,128)(2,1)}), bf16[32,25,192]{2,1,0:T(8,128)(2,1)S(1)}, u32[]{:S(2)}, u32[]{:S(2)}) async-start(bf16[32,25,192]{2,1,0:T(8,128)(2,1)} %bitcast.5), calls=%async_computation.1 | async-start | bytes 1048576 | tf_op jit(solution)/shard_map/all_to_all | solution.py:358
  16.4 19.3 %collective-permute-start.2 = (bf16[24,768]{1,0:T(8,128)(2,1)S(1)}, bf16[24,768]{1,0:T(8,128)(2,1)S(1)}, u32[]{:S(2)}, u32[]{:S(2)}) collective-permute-start(bf16[24,768]{1,0:T(8,128)(2,1)S(1)} %get-tuple-element.93), channel_id=1, source_target_pairs={{0,0},{1,8},{2,2},{3,10},{4,18},{5,4},{6,12},{7,20},{8,6},{9,14},{... | collective-permute-start | bytes 110600 | tf_op jit(solution)/shard_map/ppermute | solution.py:340
  19.8 15.9 %collective-permute-start.1 = (bf16[24,768]{1,0:T(8,128)(2,1)S(1)}, bf16[24,768]{1,0:T(8,128)(2,1)S(1)}, u32[]{:S(2)}, u32[]{:S(2)}) collective-permute-start(bf16[24,768]{1,0:T(8,128)(2,1)S(1)} %get-tuple-element.94), channel_id=1, source_target_pairs={{0,0},{1,8},{2,16},{3,2},{4,10},{5,4},{6,12},{7,20},{8,6},{9,14},{... | collective-permute-start | bytes 110600 | tf_op jit(solution)/shard_map/ppermute | solution.py:340
  36.6 15.0 %all-to-all-start.2 = ((bf16[4,72,768]{2,1,0:T(8,128)(2,1)}), bf16[4,72,768]{2,1,0:T(8,128)(2,1)S(1)}, u32[]{:S(2)}, u32[]{:S(2)}) async-start(bf16[4,72,768]{2,1,0:T(8,128)(2,1)} %broadcast_in_dim.30), calls=%async_computation.2 | async-start | bytes 884736 | tf_op jit(solution)/shard_map/all_to_all | solution.py:106
  90.6 19.8 %all-to-all-start.5 = ((bf16[8,48,768]{2,1,0:T(8,128)(2,1)}), bf16[8,48,768]{2,1,0:T(8,128)(2,1)S(1)}, u32[]{:S(2)}, u32[]{:S(2)}) async-start(bf16[8,48,768]{2,1,0:T(8,128)(2,1)} %bitcast.37), calls=%async_computation.5 | async-start | bytes 1179648 | tf_op jit(solution)/shard_map/all_to_all | solution.py:400
  110.4 20.2 %all-to-all-start.4 = ((bf16[8,48,768]{2,1,0:T(8,128)(2,1)}), bf16[8,48,768]{2,1,0:T(8,128)(2,1)S(1)}, u32[]{:S(2)}, u32[]{:S(2)}) async-start(bf16[8,48,768]{2,1,0:T(8,128)(2,1)} %bitcast.31), calls=%async_computation.4 | async-start | bytes 1179648 | tf_op jit(solution)/shard_map/all_to_all | solution.py:413
  117.1 17.5 %collective-permute-start.8 = (bf16[384,768]{1,0:T(8,128)(2,1)S(1)}, bf16[384,768]{1,0:T(8,128)(2,1)S(1)}, u32[]{:S(2)}, u32[]{:S(2)}) collective-permute-start(bf16[384,768]{1,0:T(8,128)(2,1)S(1)} %bitcast.150), channel_id=1, source_target_pairs={{0,6},{2,4},{4,2},{6,0},{1,7},{3,5},{5,3},{7,1},{8,14},{10,12},{12... | collective-permute-start | bytes 1769480 | tf_op jit(solution)/shard_map/ppermute | solution.py:404
  130.6 17.1 %collective-permute-start.7 = (bf16[384,768]{1,0:T(8,128)(2,1)S(1)}, bf16[384,768]{1,0:T(8,128)(2,1)S(1)}, u32[]{:S(2)}, u32[]{:S(2)}) collective-permute-start(bf16[384,768]{1,0:T(8,128)(2,1)S(1)} %bitcast.155), channel_id=1, source_target_pairs={{0,6},{2,4},{4,2},{6,0},{1,7},{3,5},{5,3},{7,1},{8,14},{10,12},{12... | collective-permute-start | bytes 1769480 | tf_op jit(solution)/shard_map/ppermute | solution.py:417
  132.1 27.0 %collective-permute-start.6 = (bf16[384,768]{1,0:T(8,128)(2,1)S(1)}, bf16[384,768]{1,0:T(8,128)(2,1)}, u32[]{:S(2)}, u32[]{:S(2)}) collective-permute-start(bf16[384,768]{1,0:T(8,128)(2,1)S(1)} %bitcast.151), channel_id=1, source_target_pairs={{0,4},{2,6},{4,0},{6,2},{1,5},{3,7},{5,1},{7,3},{8,12},{10,14},{12... | collective-permute-start | bytes 1769480 | tf_op jit(solution)/shard_map/ppermute | solution.py:404
  132.7 40.4 %collective-permute-start.5 = (bf16[384,768]{1,0:T(8,128)(2,1)S(1)}, bf16[384,768]{1,0:T(8,128)(2,1)}, u32[]{:S(2)}, u32[]{:S(2)}) collective-permute-start(bf16[384,768]{1,0:T(8,128)(2,1)S(1)} %bitcast.156), channel_id=1, source_target_pairs={{0,4},{2,6},{4,0},{6,2},{1,5},{3,7},{5,1},{7,3},{8,12},{10,14},{12... | collective-permute-start | bytes 1769480 | tf_op jit(solution)/shard_map/ppermute | solution.py:417
  134.1 44.6 %collective-permute-start.4 = (bf16[384,768]{1,0:T(8,128)(2,1)S(1)}, bf16[384,768]{1,0:T(8,128)(2,1)}, u32[]{:S(2)}, u32[]{:S(2)}) collective-permute-start(bf16[384,768]{1,0:T(8,128)(2,1)S(1)} %bitcast.152), channel_id=1, source_target_pairs={{0,2},{2,0},{4,6},{6,4},{1,3},{3,1},{5,7},{7,5},{8,10},{10,8},{12,... | collective-permute-start | bytes 1769480 | tf_op jit(solution)/shard_map/ppermute | solution.py:404
  134.6 44.1 %collective-permute-start.3 = (bf16[384,768]{1,0:T(8,128)(2,1)S(1)}, bf16[384,768]{1,0:T(8,128)(2,1)}, u32[]{:S(2)}, u32[]{:S(2)}) collective-permute-start(bf16[384,768]{1,0:T(8,128)(2,1)S(1)} %bitcast.157), channel_id=1, source_target_pairs={{0,2},{2,0},{4,6},{6,4},{1,3},{3,1},{5,7},{7,5},{8,10},{10,8},{12,... | collective-permute-start | bytes 1769480 | tf_op jit(solution)/shard_map/ppermute | solution.py:417
  153.7 36.8 %collective-permute-start.11 = (bf16[384,768]{1,0:T(8,128)(2,1)}, bf16[384,768]{1,0:T(8,128)(2,1)S(1)}, u32[]{:S(2)}, u32[]{:S(2)}) collective-permute-start(bf16[384,768]{1,0:T(8,128)(2,1)} %get-tuple-element.50), channel_id=1, source_target_pairs={{6,0},{4,2},{2,4},{0,6},{7,1},{5,3},{3,5},{1,7},{14,8},{12,10},{10... | collective-permute-start | bytes 1769480 | tf_op jit(solution)/shard_map/ppermute | solution.py:422
  178.2 18.7 %collective-permute-start.10 = (bf16[384,768]{1,0:T(8,128)(2,1)}, bf16[384,768]{1,0:T(8,128)(2,1)S(1)}, u32[]{:S(2)}, u32[]{:S(2)}) collective-permute-start(bf16[384,768]{1,0:T(8,128)(2,1)} %get-tuple-element.49), channel_id=1, source_target_pairs={{4,0},{6,2},{0,4},{2,6},{5,1},{7,3},{1,5},{3,7},{12,8},{14,10},{8,... | collective-permute-start | bytes 1769480 | tf_op jit(solution)/shard_map/ppermute | solution.py:422
  183.9 15.1 %collective-permute-start.9 = (bf16[384,768]{1,0:T(8,128)(2,1)}, bf16[384,768]{1,0:T(8,128)(2,1)S(1)}, u32[]{:S(2)}, u32[]{:S(2)}) collective-permute-start(bf16[384,768]{1,0:T(8,128)(2,1)} %get-tuple-element.48), channel_id=1, source_target_pairs={{2,0},{0,2},{6,4},{4,6},{3,1},{1,3},{7,5},{5,7},{10,8},{8,10},{14,... | collective-permute-start | bytes 1769480 | tf_op jit(solution)/shard_map/ppermute | solution.py:422
  201.2 20.3 %all-to-all-start.7 = ((bf16[8,48,768]{2,1,0:T(8,128)(2,1)}), bf16[8,48,768]{2,1,0:T(8,128)(2,1)S(1)}, u32[]{:S(2)}, u32[]{:S(2)}) async-start(bf16[8,48,768]{2,1,0:T(8,128)(2,1)} %bitcast.44), calls=%async_computation.7 | async-start | bytes 1179648 | tf_op jit(solution)/shard_map/all_to_all | solution.py:425
  208.0 20.7 %collective-permute-start.14 = (bf16[384,768]{1,0:T(8,128)(2,1)}, bf16[384,768]{1,0:T(8,128)(2,1)S(1)}, u32[]{:S(2)}, u32[]{:S(2)}) collective-permute-start(bf16[384,768]{1,0:T(8,128)(2,1)} %get-tuple-element.54), channel_id=1, source_target_pairs={{6,0},{4,2},{2,4},{0,6},{7,1},{5,3},{3,5},{1,7},{14,8},{12,10},{10... | collective-permute-start | bytes 1769480 | tf_op jit(solution)/shard_map/ppermute | solution.py:444
  209.5 27.7 %collective-permute-start.13 = (bf16[384,768]{1,0:T(8,128)(2,1)}, bf16[384,768]{1,0:T(8,128)(2,1)S(1)}, u32[]{:S(2)}, u32[]{:S(2)}) collective-permute-start(bf16[384,768]{1,0:T(8,128)(2,1)} %get-tuple-element.53), channel_id=1, source_target_pairs={{4,0},{6,2},{0,4},{2,6},{5,1},{7,3},{1,5},{3,7},{12,8},{14,10},{8,... | collective-permute-start | bytes 1769480 | tf_op jit(solution)/shard_map/ppermute | solution.py:444
  211.0 27.1 %collective-permute-start.12 = (bf16[384,768]{1,0:T(8,128)(2,1)}, bf16[384,768]{1,0:T(8,128)(2,1)}, u32[]{:S(2)}, u32[]{:S(2)}) collective-permute-start(bf16[384,768]{1,0:T(8,128)(2,1)} %get-tuple-element.52), channel_id=1, source_target_pairs={{2,0},{0,2},{6,4},{4,6},{3,1},{1,3},{7,5},{5,7},{10,8},{8,10},{14,... | collective-permute-start | bytes 1769480 | tf_op jit(solution)/shard_map/ppermute | solution.py:444
  223.8 21.8 %all-to-all-start.8 = ((bf16[4,128,768]{2,1,0:T(8,128)(2,1)}), bf16[4,128,768]{2,1,0:T(8,128)(2,1)S(1)}, u32[]{:S(2)}, u32[]{:S(2)}) async-start(bf16[4,128,768]{2,1,0:T(8,128)(2,1)} %broadcast_in_dim.32), calls=%async_computation.8 | async-start | bytes 1572864 | tf_op jit(solution)/shard_map/all_to_all | solution.py:106
  245.6 34.7 %all-to-all-start.6 = ((bf16[8,48,768]{2,1,0:T(8,128)(2,1)}), bf16[8,48,768]{2,1,0:T(8,128)(2,1)S(1)}, u32[]{:S(2)}, u32[]{:S(2)}) async-start(bf16[8,48,768]{2,1,0:T(8,128)(2,1)} %bitcast.41), calls=%async_computation.6 | async-start | bytes 1179648 | tf_op jit(solution)/shard_map/all_to_all | solution.py:447
  285.8 15.7 %all-to-all-start.9 = ((bf16[4,128,768]{2,1,0:T(8,128)(2,1)}), bf16[4,128,768]{2,1,0:T(8,128)(2,1)S(1)}, u32[]{:S(2)}, u32[]{:S(2)}) async-start(bf16[4,128,768]{2,1,0:T(8,128)(2,1)} %bitcast.170), calls=%async_computation.9 | async-start | bytes 1572864 | tf_op jit(solution)/shard_map/all_to_all | solution.py:470
  301.6 18.1 %all-to-all-start.10 = ((bf16[32,26,192]{2,1,0:T(8,128)(2,1)}), bf16[32,26,192]{2,1,0:T(8,128)(2,1)S(1)}, u32[]{:S(2)}, u32[]{:S(2)}) async-start(bf16[32,26,192]{2,1,0:T(8,128)(2,1)} %pad_maximum_fusion), calls=%async_computation.10 | async-start | bytes 1048576 | tf_op jit(solution)/shard_map/all_to_all | solution.py:500
  319.7 15.7 %all-to-all-start.12 = ((bf16[4,72,768]{2,1,0:T(8,128)(2,1)}), bf16[4,72,768]{2,1,0:T(8,128)(2,1)S(1)}, u32[]{:S(2)}, u32[]{:S(2)}) async-start(bf16[4,72,768]{2,1,0:T(8,128)(2,1)} %bitcast.54), calls=%async_computation.12 | async-start | bytes 884736 | tf_op jit(solution)/shard_map/all_to_all | solution.py:462
  (33 other events, 574.6 us)

commit v2 on v1

v2 whole, which is shorter than its diff:
```python
import functools
import math

import jax
import jax.numpy as jnp
import numpy as np
from jax import lax
from jax.experimental import pallas as pl
from jax.experimental.pallas import tpu as pltpu
from jax.sharding import PartitionSpec as P

EPSILON = 1e-06
SLOPE = 0.7978845608028654
CUBIC = 0.044715
LIMITS = (19, 21, 24, 27, 31, 35, 40, 46, 52, 59, 67, 77, 87, 99, 113)
MASKED = -1e30
HIGH = lax.Precision.HIGHEST
ALL = ("dp", "seq", "expert")
GROUP = ("dp", "expert")
BLOCK = 128
BF = jnp.bfloat16
F32 = jnp.float32


def dot(left, right, left_dim, right_dim):
    return lax.dot_general(
        left, right, (((left_dim,), (right_dim,)), ((), ())), preferred_element_type=F32
    )


def rms_scale(values):
    return lax.rsqrt(jnp.mean(values * values, axis=-1, keepdims=True) + EPSILON)


def bucket_hot(lag, count):
    bucket = jnp.minimum(lag, 16)
    for threshold in LIMITS:
        bucket = bucket + (lag >= threshold).astype(jnp.int32)
    return (jnp.arange(count, dtype=jnp.int32)[:, None] == bucket[None, :]).astype(F32)


@functools.lru_cache(maxsize=None)
def weight_routes(features, columns, n_dp, n_seq, n_ex):
    width = features // n_seq
    chunk = math.gcd(columns, width)
    per = columns // chunk
    devices = n_dp * n_seq * n_ex
    edges = []
    for group in range(n_seq):
        index = 0
        for part in range(3):
            for i in range(width // chunk):
                piece = (part * features + group * width) // chunk + i
                ex, rest = divmod(index, n_dp * per)
                dp, slot = divmod(rest, per)
                target = (dp * n_seq + group) * n_ex + ex
                edges.append((piece // per, piece % per, target, slot))
                index += 1
    rounds = []
    left = list(edges)
    for _ in range(per):
        out_edges = [[] for _ in range(devices)]
        for edge in left:
            out_edges[edge[0]].append(edge)
        matched = {}

        def place(source, seen):
            for edge in out_edges[source]:
                if edge[2] in seen:
                    continue
                seen.add(edge[2])
                if edge[2] not in matched or place(matched[edge[2]][0], seen):
                    matched[edge[2]] = edge
                    return True
            return False

        for source in range(devices):
            assert place(source, set())
        rounds.append(sorted(matched.values()))
        for edge in matched.values():
            left.remove(edge)
    pairs = tuple(tuple((e[0], e[2]) for e in r) for r in rounds)
    send = np.zeros((devices, per), np.int32)
    receive = np.zeros((devices, per), np.int32)
    for m, r in enumerate(rounds):
        for source, sub, target, slot in r:
            send[source, m] = sub
            receive[target, slot] = m
    return chunk, per, pairs, send, receive


def inverse_rows(table):
    return np.argsort(table, axis=1).astype(np.int32)


def positions_of(count, sign):
    me, step = np.arange(count)[:, None], np.arange(count)[None, :]
    return me ^ step if count & (count - 1) == 0 else (me + sign * step) % count


class Info:
    def __init__(self, features, columns, n_dp, n_seq, n_ex):
        self.chunk, self.per, self.pairs, send, receive = weight_routes(
            features, columns, n_dp, n_seq, n_ex
        )
        device = np.arange(n_dp * n_seq * n_ex)
        dp, seq, ex = device // (n_seq * n_ex), device // n_ex % n_seq, device % n_ex
        parts = {
            "send_sub": send,
            "slot_round": receive,
            "sub_round": inverse_rows(send),
            "send_slot": inverse_rows(receive),
            "from_seq": positions_of(n_seq, -1)[seq],
            "to_seq": positions_of(n_seq, 1)[seq],
            "from_dp": positions_of(n_dp, -1)[dp],
            "to_dp": positions_of(n_dp, 1)[dp],
            "from_ex": positions_of(n_ex, -1)[ex],
            "to_ex": positions_of(n_ex, 1)[ex],
        }
        self.start = {}
        width = 0
        for name, part in parts.items():
            self.start[name] = width
            width += part.shape[1]
        self.table = np.concatenate(list(parts.values()), axis=1).astype(np.int32)

    def at(self, ref, name, i):
        return ref[self.start[name] + i]


def chosen(values, index):
    out = values[0]
    for i in range(1, len(values)):
        out = jnp.where(index == i, values[i], out)
    return out


def specs(arrays):
    return [pl.BlockSpec(memory_space=pltpu.SMEM)] + [
        pl.BlockSpec(memory_space=pltpu.VMEM)
    ] * arrays


def small_call(kernel, info_row, arrays, outs, scratch):
    return pl.pallas_call(
        kernel,
        in_specs=specs(len(arrays)),
        out_shape=tuple(jax.ShapeDtypeStruct(shape, kind) for shape, kind in outs),
        scratch_shapes=[pltpu.VMEM(shape, kind) for shape, kind in scratch],
    )(info_row, *arrays)


def whole_tiles(rows):
    return -(-rows // 16) * 16


def pick_kernel(info, row_ref, entry_ref, *out_refs):
    entry = entry_ref[...].astype(F32)
    chunk = info.chunk
    parts = [entry[i * chunk : (i + 1) * chunk, :] for i in range(info.per)]
    for i, out_ref in enumerate(out_refs):
        out_ref[...] = chosen(parts, info.at(row_ref, "send_sub", i)).astype(BF)


def place_kernel(info, n_seq, share, row_ref, *refs):
    per, chunk = info.per, info.chunk
    came, exit_ref, gains = refs[:per], refs[per], refs[per + 1 : per + 1 + n_seq]
    out_ref, line_ref = refs[per + 1 + n_seq :]
    head = whole_tiles(share + n_seq)
    line_ref[...] = jnp.zeros_like(line_ref)
    line_ref[:share, :] = exit_ref[...].astype(F32)
    rows = [ref[...].astype(F32) for ref in gains]
    for i in range(n_seq):
        value = rows[0]
        for j in range(1, n_seq):
            value = jnp.where(info.at(row_ref, "from_seq", j) == i, rows[j], value)
        line_ref[share + i : share + i + 1, :] = value
    parts = [ref[...].astype(F32) for ref in came]
    for i in range(per):
        line_ref[head + i * chunk : head + (i + 1) * chunk, :] = chosen(
            parts, info.at(row_ref, "slot_round", i)
        )
    out_ref[...] = line_ref[...].astype(BF)


def arrange_kernel(info, n_dp, n_seq, n_ex, share, owned, row_ref, *refs):
    blocks, refs = refs[: n_dp * n_ex], refs[n_dp * n_ex :]
    entry_ref, gain_ref, *exit_refs = refs[: 2 + n_seq]
    all_ref, line_ref, exits_ref = refs[2 + n_seq :]
    width = exits_ref.shape[3]
    head = whole_tiles(share + n_seq)
    for i in range(n_dp):
        for j in range(n_ex):
            spot = info.at(row_ref, "from_ex", j) * n_dp + info.at(row_ref, "from_dp", i)
            all_ref[spot] = blocks[i * n_ex + j][...]
    for spot in range(n_ex * n_dp):
        ex, dp = divmod(spot, n_dp)
        value = all_ref[spot].astype(F32)
        line_ref[spot * owned : (spot + 1) * owned, :] = value[head : head + owned, :]
        for seq in range(n_seq):
            exits_ref[seq, spot] = value[:share, seq * width : (seq + 1) * width]
            lane = ((dp * n_seq + seq) * n_ex + ex) * share
            for k in range(2):
                gain_ref[k : k + 1, lane : lane + share] = value[
                    share + seq : share + seq + 1, k * share : (k + 1) * share
                ]
    entry_ref[...] = line_ref[...].astype(BF)
    for i in range(n_seq):
        exit_refs[i][...] = exits_ref[info.at(row_ref, "to_seq", i)].astype(BF)


def pack_kernel(info, n_dp, n_seq, n_ex, share, owned, row_ref, *refs):
    exits, refs = refs[:n_seq], refs[n_seq:]
    entry_ref, diag_ref, one_ref, two_ref, hot_ref = refs[:5]
    out_refs, (four_ref, small_ref, all_ref) = refs[5 : 5 + n_ex], refs[5 + n_ex :]
    width = exits[0].shape[2]
    heads, buckets = diag_ref.shape[0], hot_ref.shape[0]
    head = whole_tiles(share + 2)
    for i in range(n_seq):
        four_ref[info.at(row_ref, "from_seq", i)] = exits[i][...].astype(F32)
    bias = lax.dot_general(
        diag_ref[...], hot_ref[...], (((1,), (1,)), ((), ())), precision=HIGH,
        preferred_element_type=F32,
    )
    small_ref[...] = jnp.zeros_like(small_ref)
    all_ref[...] = jnp.zeros_like(all_ref)
    for seq in range(n_seq):
        for k in range(heads):
            lane = seq * width + 2 * share + k * buckets
            small_ref[0:1, lane : lane + buckets] = bias[k : k + 1, :]
    entry = entry_ref[...].astype(F32)
    for spot in range(n_ex * n_dp):
        ex, dp = divmod(spot, n_dp)
        for seq in range(n_seq):
            to = seq * width
            all_ref[ex, dp, :share, to : to + width] = four_ref[
                seq, dp, ex * share : (ex + 1) * share, :
            ]
            lane = ((dp * n_seq + seq) * n_ex + ex) * share
            small_ref[0:1, to : to + share] = one_ref[:, lane : lane + share]
            small_ref[0:1, to + share : to + 2 * share] = two_ref[:, lane : lane + share]
        small = small_ref[0:1, :]
        upper = small.astype(BF).astype(F32)
        all_ref[ex, dp, share : share + 1, :] = upper
        all_ref[ex, dp, share + 1 : share + 2, :] = small - upper
        all_ref[ex, dp, head : head + owned, :] = entry[spot * owned : (spot + 1) * owned, :]
    for i in range(n_ex):
        out_refs[i][...] = all_ref[info.at(row_ref, "to_ex", i)].astype(BF)


def fold_kernel(info, n_dp, n_ex, share, row_ref, *refs):
    parts, out_refs, all_ref = refs[:n_ex], refs[n_ex : n_ex + n_dp], refs[n_ex + n_dp]
    for dp in range(n_dp):
        total = parts[0][dp].astype(F32)
        for part in parts[1:]:
            total = total + part[dp].astype(F32)
        all_ref[dp] = total
        small = total[share : share + 1, :] + total[share + 1 : share + 2, :]
        upper = small.astype(BF).astype(F32)
        all_ref[dp, share : share + 1, :] = upper
        all_ref[dp, share + 1 : share + 2, :] = small - upper
    for i in range(n_dp):
        out_refs[i][...] = all_ref[info.at(row_ref, "to_dp", i)].astype(BF)


def finish_kernel(info, n_dp, n_seq, share, row_ref, *refs):
    parts, refs = refs[:n_dp], refs[n_dp:]
    exit_ref, *refs = refs
    piece_refs, small_refs, four_ref = refs[: info.per], refs[info.per : -1], refs[-1]
    head, chunk = whole_tiles(share + 2), info.chunk
    total = parts[0][...].astype(F32)
    for part in parts[1:]:
        total = total + part[...].astype(F32)
    exit_ref[...] = total[:share, :]
    small = total[share : share + 1, :] + total[share + 1 : share + 2, :]
    width = four_ref.shape[2]
    for seq in range(n_seq):
        four_ref[seq] = small[:, seq * width : (seq + 1) * width]
    for i in range(n_seq):
        small_refs[i][...] = four_ref[info.at(row_ref, "to_seq", i)]
    pieces = [total[head + i * chunk : head + (i + 1) * chunk, :] for i in range(info.per)]
    for i in range(info.per):
        piece_refs[i][...] = chosen(pieces, info.at(row_ref, "send_slot", i))


def close_kernel(info, n_seq, share, heads, row_ref, *refs):
    came, small, refs = refs[: info.per], refs[info.per : info.per + n_seq], refs[info.per + n_seq :]
    entry_ref, gain_ref, bias_ref, four_ref = refs
    chunk, buckets = info.chunk, bias_ref.shape[1]
    parts = [ref[...] for ref in came]
    for i in range(info.per):
        entry_ref[i * chunk : (i + 1) * chunk, :] = chosen(parts, info.at(row_ref, "sub_round", i))
    for i in range(n_seq):
        four_ref[info.at(row_ref, "from_seq", i)] = small[i][...]
    total = four_ref[0]
    for seq in range(1, n_seq):
        total = total + four_ref[seq]
    gain_ref[0:1, :] = total[:, :share]
    gain_ref[1:2, :] = total[:, share : 2 * share]
    for seq in range(n_seq):
        for k in range(heads):
            lane = 2 * share + k * buckets
            bias_ref[seq * heads + k : seq * heads + k + 1, :] = four_ref[
                seq, :, lane : lane + buckets
            ]


def allowed_of(docs_row, docs_col, start, rows, keys):
    query = start + lax.broadcasted_iota(jnp.int32, (rows, keys), 0)
    key = lax.broadcasted_iota(jnp.int32, (rows, keys), 1)
    return (key <= query) & (docs_col[start : start + rows, :] == docs_row[:, :keys])


def bias_rows(lag_ref, head, start, rows, keys):
    length = lag_ref.shape[1]
    flat = jnp.broadcast_to(lag_ref[head : head + 1, :], (rows, length))
    return pltpu.roll(flat, start, 1, stride=1, stride_axis=0)[:, :keys]


def aligned(block, index):
    return pl.ds(pl.multiple_of(index * block, block), block)


def attend_kernel(info, heads, size, count, row_ref, *refs):
    x_refs, refs = refs[:count], refs[count:]
    gain_ref, w_ref, doc_ref, col_ref, lag_ref, x_ref, qkv_ref, ctx_ref, log_ref = refs
    length = x_ref.shape[0]
    rows = length // count
    width = heads * size
    factor = size ** (-0.5)
    for i in range(count):
        x_ref[aligned(rows, info.at(row_ref, "from_seq", i)), :] = x_refs[i][...]
    normed = (x_ref[...].astype(F32) * gain_ref[0:1, :]).astype(BF)
    qkv_ref[...] = dot(normed, w_ref[...], 1, 1).astype(BF)
    for start in range(0, length, BLOCK):
        keys = start + BLOCK
        allowed = allowed_of(doc_ref, col_ref, start, BLOCK, keys)
        for head in range(heads):
            lo = head * size
            q = qkv_ref[start:keys, lo : lo + size]
            k = qkv_ref[:keys, width + lo : width + lo + size]
            v = qkv_ref[:keys, 2 * width + lo : 2 * width + lo + size]
            scores = dot(q, k, 1, 1) * factor + bias_rows(lag_ref, head, start, BLOCK, keys)
            scores = jnp.where(allowed, scores, MASKED)
            peak = jnp.max(scores, axis=1, keepdims=True)
            raised = jnp.exp(scores - peak)
            total = jnp.sum(raised, axis=1, keepdims=True)
            weights = (raised / total).astype(BF)
            log_ref[start:keys, head : head + 1] = peak + jnp.log(total)
            ctx_ref[start:keys, lo : lo + size] = dot(weights, v, 1, 0).astype(BF)


def attend(info, heads, size, info_row, blocks, gain, w, docs_row, docs_col, lag):
    count = len(blocks)
    rows, features = blocks[0].shape
    length = rows * count
    width = heads * size
    return small_call(
        functools.partial(attend_kernel, info, heads, size, count),
        info_row,
        (*blocks, gain, w, docs_row, docs_col, lag),
        [
            ((length, features), BF),
            ((length, 3 * width), BF),
            ((length, width), BF),
            ((length, heads), F32),
        ],
        [],
    )


def leave_kernel(info, n_dp, n_seq, n_ex, row_ref, ctx_ref, *refs):
    exits, refs = refs[:n_seq], refs[n_seq:]
    exit_ref, part_refs, (four_ref, line_ref) = refs[0], refs[1 : 1 + n_seq], refs[1 + n_seq :]
    rows = part_refs[0].shape[0]
    share = exits[0].shape[1]
    for i in range(n_seq):
        four_ref[info.at(row_ref, "from_seq", i)] = exits[i][...].astype(F32)
    for dp in range(n_dp):
        for seq in range(n_seq):
            for ex in range(n_ex):
                start = ((dp * n_seq + seq) * n_ex + ex) * share
                line_ref[start : start + share, :] = four_ref[seq, ex * n_dp + dp]
    exit_ref[...] = line_ref[...].astype(BF)
    for i, part_ref in enumerate(part_refs):
        block = aligned(rows, info.at(row_ref, "to_seq", i))
        part_ref[...] = dot(ctx_ref[block, :], exit_ref[...], 1, 1).astype(BF)


def leave(info, n_dp, n_seq, n_ex, info_row, ctx, exits):
    spots, share, width = exits[0].shape
    features = spots * share * n_seq
    out = small_call(
        functools.partial(leave_kernel, info, n_dp, n_seq, n_ex),
        info_row,
        (ctx, *exits),
        [((features, width), BF)] + [((ctx.shape[0] // n_seq, features), BF)] * n_seq,
        [((n_seq, spots, share, width), F32), ((features, width), F32)],
    )
    return out[0], out[1:]


def leave_back_kernel(info, count, n_dp, share, row_ref, *refs):
    up_refs, refs = refs[:count], refs[count:]
    ctx_ref, up_ref, *grad_refs, all_ref = refs
    rows = up_refs[0].shape[0]
    for i in range(count):
        up_ref[aligned(rows, info.at(row_ref, "from_seq", i)), :] = up_refs[i][...]
    grad = dot(up_ref[...], ctx_ref[...], 0, 0)
    for dp in range(n_dp):
        for i in range(count):
            start = (dp * count + i) * share
            all_ref[i, dp] = grad[start : start + share, :]
    for i in range(count):
        grad_refs[i][...] = all_ref[info.at(row_ref, "to_seq", i)].astype(BF)


def leave_back(info, n_dp, info_row, blocks, ctx):
    count = len(blocks)
    rows, features = blocks[0].shape
    share = features // (n_dp * count)
    width = ctx.shape[1]
    return small_call(
        functools.partial(leave_back_kernel, info, count, n_dp, share),
        info_row,
        (*blocks, ctx),
        [((rows * count, features), BF)] + [((n_dp, share, width), BF)] * count,
        [((count, n_dp, share, width), F32)],
    )


def attend_back_kernel(info, heads, size, count, row_ref, *refs):
    up_ref, exit_ref, qkv_ref, log_ref, doc_ref, col_ref, lag_ref, x_ref, gain_ref, w_ref = refs[:10]
    diag_ref, gain_grad_ref, entry_ref, *refs = refs[10:]
    back_refs, (bctx_ref, bqkv_ref, bk_ref, bv_ref, lines_ref) = refs[:count], refs[count:]
    length = up_ref.shape[0]
    rows = length // count
    width = heads * size
    factor = size ** (-0.5)
    bctx_ref[...] = dot(up_ref[...], exit_ref[...], 1, 0).astype(BF)
    bk_ref[...] = jnp.zeros_like(bk_ref)
    bv_ref[...] = jnp.zeros_like(bv_ref)
    lines_ref[...] = jnp.zeros_like(lines_ref)
    for start in range(0, length, BLOCK):
        keys = start + BLOCK
        allowed = allowed_of(doc_ref, col_ref, start, BLOCK, keys)
        for head in range(heads):
            lo = head * size
            q = qkv_ref[start:keys, lo : lo + size]
            k = qkv_ref[:keys, width + lo : width + lo + size]
            v = qkv_ref[:keys, 2 * width + lo : 2 * width + lo + size]
            bc = bctx_ref[start:keys, lo : lo + size]
            scores = dot(q, k, 1, 1) * factor + bias_rows(lag_ref, head, start, BLOCK, keys)
            probs = jnp.where(
                allowed, jnp.exp(scores - log_ref[start:keys, head : head + 1]), 0.0
            )
            back_probs = dot(bc, v, 1, 1)
            row_dot = jnp.sum(probs * back_probs, axis=1, keepdims=True)
            back_scores = probs * (back_probs - row_dot)
            scaled = (back_scores * factor).astype(BF)
            bqkv_ref[start:keys, lo : lo + size] = dot(scaled, k, 1, 0).astype(BF)
            bk_ref[:keys, lo : lo + size] += dot(scaled, q, 0, 0)
            bv_ref[:keys, lo : lo + size] += dot(probs.astype(BF), bc, 0, 0)
            lined = jnp.zeros((8, keys), F32)
            for row in range(0, BLOCK, 8):
                lined = lined + pltpu.roll(
                    back_scores[row : row + 8, :], (keys - start - row - 8) % keys, 1
                )
            lines_ref[8 * head : 8 * head + 8, length - keys :] += lined
    for head in range(heads):
        total = jnp.zeros((1, length), F32)
        for row in range(8):
            total = total + pltpu.roll(
                lines_ref[8 * head + row : 8 * head + row + 1, :], 7 - row, 1
            )
        diag_ref[head : head + 1, :] = total
    bqkv_ref[:, width : 2 * width] = bk_ref[...].astype(BF)
    bqkv_ref[:, 2 * width :] = bv_ref[...].astype(BF)
    normed = (x_ref[...].astype(F32) * gain_ref[0:1, :]).astype(BF)
    entry_ref[...] = dot(bqkv_ref[...], normed, 0, 0).astype(BF)
    gain_grad = jnp.zeros(gain_grad_ref.shape, F32)
    for i in range(count):
        block = aligned(rows, info.at(row_ref, "to_seq", i))
        back = dot(bqkv_ref[block, :], w_ref[...], 1, 0)
        back_refs[i][...] = back.astype(BF)
        gain_grad += jnp.sum(back * x_ref[block, :].astype(F32), axis=0, keepdims=True)
    gain_grad_ref[...] = gain_grad


def attend_back(
    info, heads, size, count, info_row, up, exit_t, qkv, log, docs_row, docs_col, lag, x, gain, w
):
    length, features = up.shape
    width = heads * size
    diag, gain_grad, entry, *backs = small_call(
        functools.partial(attend_back_kernel, info, heads, size, count),
        info_row,
        (up, exit_t, qkv, log, docs_row, docs_col, lag, x, gain, w),
        [
            ((heads, length), F32),
            ((1, features), F32),
            ((3 * width, features), BF),
            *[((length // count, features), BF)] * count,
        ],
        [
            ((length, width), BF),
            ((length, 3 * width), BF),
            ((length, width), F32),
            ((length, width), F32),
            ((8 * heads, length), F32),
        ],
    )
    return diag, gain_grad, entry, backs


def expert_kernel(count, rows_ref, up_ref, *refs):
    w_ups, w_downs, refs = refs[:count], refs[count : 2 * count], refs[2 * count :]
    back_ref, result_ref, acts, bbs = refs[0], refs[1], refs[2 : 2 + count], refs[2 + count :]
    for i in range(count):
        before = dot(rows_ref[...], w_ups[i][...], 1, 0)
        tangent = jnp.tanh(SLOPE * (before + CUBIC * before * before * before))
        acts[i][...] = (0.5 * before * (1.0 + tangent)).astype(BF)
        slope = 0.5 * (1.0 + tangent) + 0.5 * before * (1.0 - tangent * tangent) * SLOPE * (
            1.0 + 3.0 * CUBIC * before * before
        )
        bbs[i][...] = (dot(up_ref[...], w_downs[i][...], 1, 1) * slope).astype(BF)
    back = dot(bbs[0][...], w_ups[0][...], 1, 1)
    for i in range(1, count):
        back = back + dot(bbs[i][...], w_ups[i][...], 1, 1)
    back_ref[...] = back.astype(BF)
    result = dot(acts[0][...], w_downs[0][...], 1, 0)
    for i in range(1, count):
        result = result + dot(acts[i][...], w_downs[i][...], 1, 0)
    result_ref[...] = result.astype(BF)


def expert(rows, upstream, w_ups, w_downs):
    count = len(w_ups)
    tokens, features = rows.shape
    hidden = w_ups[0].shape[1]
    out = pl.pallas_call(
        functools.partial(expert_kernel, count),
        out_shape=(
            *[jax.ShapeDtypeStruct((tokens, features), BF)] * 2,
            *[jax.ShapeDtypeStruct((tokens, hidden), BF)] * (2 * count),
        ),
        name="expert",
    )(rows, upstream, *w_ups, *w_downs)
    return out[0], out[1], out[2 : 2 + count], out[2 + count :]


def expert_grad_kernel(count, *refs):
    rows, bbs = refs[:count], refs[count : 2 * count]
    acts, ups = refs[2 * count : 3 * count], refs[3 * count : 4 * count]
    up_ref, down_ref = refs[4 * count :]
    total = dot(rows[0][...], bbs[0][...], 0, 0)
    for i in range(1, count):
        total = total + dot(rows[i][...], bbs[i][...], 0, 0)
    up_ref[...] = total.astype(up_ref.dtype)
    total = dot(acts[0][...], ups[0][...], 0, 0)
    for i in range(1, count):
        total = total + dot(acts[i][...], ups[i][...], 0, 0)
    down_ref[...] = total.astype(down_ref.dtype)


def expert_grad(rows, bbs, acts, ups, kind):
    features, hidden = rows[0].shape[1], bbs[0].shape[1]
    return pl.pallas_call(
        functools.partial(expert_grad_kernel, len(rows)),
        out_shape=(
            jax.ShapeDtypeStruct((features, hidden), kind),
            jax.ShapeDtypeStruct((hidden, features), kind),
        ),
        name="expert_grad",
    )(*rows, *bbs, *acts, *ups)


def target(count, me, step):
    return me ^ step if count & (count - 1) == 0 else (me + step) % count


def source(count, me, step):
    return me ^ step if count & (count - 1) == 0 else (me - step) % count


def shift(array, axis, step):
    count = lax.axis_size(axis)
    return lax.ppermute(array, axis, tuple((i, target(count, i, step)) for i in range(count)))


def gathered(array, axis, steps):
    return [array] + [shift(array, axis, step) for step in steps]


def exchanged(array, axis):
    return lax.all_to_all(array, axis, 0, 0, tiled=True)


def traded(blocks, axis, steps):
    return [blocks[0]] + [shift(block, axis, step) for block, step in zip(blocks[1:], steps)]


def summed(blocks, axis, steps):
    came = traded(blocks, axis, steps)
    return functools.reduce(jnp.add, [block.astype(F32) for block in came])


def handed_back(blocks, axis, steps):
    count = lax.axis_size(axis)
    return summed(blocks, axis, tuple(source(count, 0, step) for step in steps))


def after(arrays, *others):
    return lax.optimization_barrier((tuple(arrays), others))[0]


def local(
    block_input,
    documents,
    route_experts,
    route_gate,
    first_gain,
    entry_weight,
    exit_weight,
    position_bias,
    second_gain,
    expert_up,
    expert_down,
    cotangent,
):
    n_dp, n_seq, n_ex = (lax.axis_size(name) for name in ALL)
    group_count = n_dp * n_ex
    rows_here, features = block_input.shape[1:]
    buckets, head_count = position_bias.shape
    size = features // head_count
    heads = head_count // n_seq
    width = heads * size
    top_count = route_experts.shape[2]
    length = rows_here * n_seq
    me = lax.axis_index(ALL)
    here = lax.axis_index("seq")
    inputs = block_input.reshape(rows_here, features)
    upstream = cotangent.reshape(rows_here, features)

    seq_steps = tuple(range(1, n_seq))
    owned = entry_weight.shape[1]
    share = exit_weight.shape[1]
    info = Info(features, owned, n_dp, n_seq, n_ex)
    per, chunk = info.per, info.chunk
    info_row = lax.dynamic_slice(jnp.asarray(info.table), (me, 0), (1, info.table.shape[1]))
    info_row = info_row.reshape(info.table.shape[1])

    pieces = small_call(
        functools.partial(pick_kernel, info),
        info_row, (entry_weight.T,), [((chunk, features), BF)] * per, [],
    )
    came = [lax.ppermute(piece, ALL, pair) for piece, pair in zip(pieces, info.pairs)]
    gains = jnp.pad(jnp.concatenate([first_gain, second_gain]), (0, features - 2 * share))
    gain_rows = gathered(gains[None], "seq", seq_steps)
    scale_one = rms_scale(inputs)
    xhats = gathered((inputs * scale_one).astype(BF), "seq", seq_steps)
    padded = whole_tiles(share + n_seq) + whole_tiles(owned)
    (weights,) = small_call(
        functools.partial(place_kernel, info, n_seq, share),
        info_row, (*came, exit_weight.T, *gain_rows),
        [((padded, features), BF)], [((padded, features), F32)],
    )
    weights = gathered(weights, "dp", range(1, n_dp))
    weights = [block for weight in weights for block in gathered(weight, "expert", range(1, n_ex))]
    entry_t, gains, *exits = small_call(
        functools.partial(arrange_kernel, info, n_dp, n_seq, n_ex, share, owned),
        info_row, weights,
        [((3 * width, features), BF), ((2, features), F32)]
        + [((group_count, share, width), BF)] * n_seq,
        [
            ((group_count, padded, features), BF),
            ((3 * width, features), F32),
            ((n_seq, group_count, share, width), F32),
        ],
    )
    gain_one, gain_two = gains[0:1], gains[1:2]
    exits = exits[:1] + [shift(part, "seq", step) for part, step in zip(exits[1:], seq_steps)]

    inner = 2 if n_seq > 1 and n_seq & (n_seq - 1) == 0 else 1
    in_steps = tuple(range(1, inner))
    out_steps = tuple(range(inner, n_seq, inner))
    w_send = (expert_up[0], expert_down[0])
    w_ups = gathered(w_send[0], "seq", out_steps)
    w_downs = gathered(w_send[1], "seq", out_steps)

    group_size = n_dp * n_ex
    capacity = 3 * rows_here // group_size
    slots = group_size * capacity
    route_count = rows_here * top_count
    flat_routes = route_experts.reshape(rows_here, top_count).T.reshape(1, route_count)
    gates = route_gate.reshape(rows_here, top_count)
    named = flat_routes == jnp.arange(group_size, dtype=jnp.int32)[:, None]
    order = jnp.arange(route_count, dtype=jnp.int32)
    earlier = (order[:, None] < order[None, :]).astype(BF)
    rank = jnp.dot(named.astype(BF), earlier, preferred_element_type=F32)
    first = (jnp.arange(group_size, dtype=jnp.int32) * capacity).astype(F32)[:, None]
    slot_of = jnp.sum(jnp.where(named, rank + first, 0.0), axis=0, keepdims=True)
    place = (
        jnp.arange(slots, dtype=jnp.int32)[:, None] == slot_of.astype(jnp.int32)
    ).astype(BF)
    place_each = [place[:, k * rows_here : (k + 1) * rows_here] for k in range(top_count)]
    place_any = functools.reduce(jnp.add, place_each)
    shaped = (group_size, capacity, features)

    gated = jnp.concatenate(
        [(upstream * gates[:, k : k + 1]).astype(BF) for k in range(top_count)], axis=0
    )
    send_upstream = dot(place, gated, 1, 0).astype(BF)
    came_upstream = exchanged(send_upstream.reshape(shaped), GROUP).reshape(slots, features)

    docs = documents.reshape(length)
    docs_row, docs_col = docs.reshape(1, length), docs.reshape(length, 1)
    lane = jnp.arange(length, dtype=jnp.int32)
    hot = bucket_hot(jnp.where(lane == 0, 0, length - lane), buckets)
    bias_here = lax.dynamic_slice_in_dim(position_bias.T, here * heads, heads)
    lag = jnp.dot(bias_here, hot, precision=HIGH)
    hot_back = bucket_hot(length - 1 - lane, buckets)
    (lag,) = after((lag,), send_upstream)
    xfull, qkv, ctx, log = attend(
        info, heads, size, info_row, xhats, gains, entry_t, docs_row, docs_col, lag
    )
    exit_t, parts = leave(info, n_dp, n_seq, n_ex, info_row, ctx, exits)

    hidden = inputs + summed(parts, "seq", seq_steps)
    scale_two = rms_scale(hidden)
    normed_two = (hidden * scale_two * gain_two).astype(BF)

    send_rows = dot(place_any, normed_two, 1, 0).astype(BF)
    ups = gathered(came_upstream, "seq", in_steps)
    came_rows = exchanged(send_rows.reshape(shaped), GROUP).reshape(slots, features)
    rows = gathered(came_rows, "seq", in_steps)
    worked = []
    for m in range(inner):
        worked.append(expert(rows[m], ups[m], w_ups, w_downs))
    back_sum = handed_back([w[0] for w in worked], "seq", in_steps).astype(BF)
    returned_back = exchanged(back_sum.reshape(shaped), GROUP).reshape(slots, features)
    grads = []
    for j in range(n_seq // inner):
        bbs, acts = [w[3][j] for w in worked], [w[2][j] for w in worked]
        grads.append(expert_grad(rows, bbs, acts, ups, BF if j else F32))
    back_normed_two = dot(place_any, returned_back, 0, 0)
    upper_two = back_normed_two * gain_two
    gain_two_grad = jnp.sum(back_normed_two * hidden * scale_two, axis=0, keepdims=True)
    back_hidden = upstream + scale_two * (
        upper_two
        - hidden * scale_two * scale_two * jnp.mean(upper_two * hidden, axis=1, keepdims=True)
    )
    up_hiddens = gathered(back_hidden.astype(BF), "seq", seq_steps)

    results = [w[1] for w in worked]
    out_sum = handed_back(results, "seq", in_steps).astype(BF)
    returned_out = exchanged(out_sum.reshape(shaped), GROUP).reshape(slots, features)
    block_output = hidden
    for k in range(top_count):
        block_output = block_output + dot(place_each[k], returned_out, 0, 0) * gates[:, k : k + 1]

    up_full, *exit_grads = leave_back(info, n_dp, info_row, up_hiddens, ctx)
    exit_grads = exit_grads[:1] + [
        shift(part, "seq", step)
        for part, step in zip(exit_grads[1:], seq_steps)
    ]
    diag, gain_one_grad, entry_grad, backs = attend_back(
        info, heads, size, n_seq, info_row, up_full, exit_t, qkv, log, docs_row, docs_col, lag,
        xfull, gains, entry_t,
    )

    count = 2 * share + buckets * heads
    assert count <= width
    padded = whole_tiles(share + 2) + whole_tiles(owned)
    halves = small_call(
        functools.partial(pack_kernel, info, n_dp, n_seq, n_ex, share, owned),
        info_row,
        (*exit_grads, entry_grad, diag, gain_one_grad, gain_two_grad, hot_back),
        [((n_dp, padded, features), BF)] * n_ex,
        [
            ((n_seq, n_dp, n_ex * share, width), F32),
            ((8, features), F32),
            ((n_ex, n_dp, padded, features), F32),
        ],
    )
    halves = traded(halves, "expert", range(1, n_ex))
    quarters = small_call(
        functools.partial(fold_kernel, info, n_dp, n_ex, share),
        info_row, halves, [((padded, features), BF)] * n_dp,
        [((n_dp, padded, features), F32)],
    )
    quarters = traded(quarters, "dp", range(1, n_dp))
    exit_share, *rest = small_call(
        functools.partial(finish_kernel, info, n_dp, n_seq, share),
        info_row, quarters,
        [((share, features), F32)]
        + [((chunk, features), F32)] * per
        + [((1, width), F32)] * n_seq,
        [((n_seq, 1, width), F32)],
    )
    pieces, small = rest[:per], rest[per:]
    came = [
        lax.ppermute(piece, ALL, tuple((b, a) for a, b in pair))
        for piece, pair in zip(pieces, info.pairs)
    ]
    small = traded(small, "seq", seq_steps)
    entry_share, gain_shares, bias_total = small_call(
        functools.partial(close_kernel, info, n_seq, share, heads),
        info_row, (*came, *small),
        [((owned, features), F32), ((2, share), F32), ((head_count, buckets), F32)],
        [((n_seq, 1, width), F32)],
    )
    entry_share, exit_share, bias_total = entry_share.T, exit_share.T, bias_total.T
    gain_one_share, gain_two_share = gain_shares[0], gain_shares[1]

    back_normed_one = summed(backs, "seq", seq_steps)
    upper_one = back_normed_one * gain_one
    back_input = back_hidden + scale_one * (
        upper_one
        - inputs * scale_one * scale_one * jnp.mean(upper_one * inputs, axis=1, keepdims=True)
    )

    (own_up, own_down), *others = grads
    own_up, own_down = after((own_up, own_down), gain_one_grad)
    grads = [(own_up, own_down), *others]
    up_grad = handed_back([g[0] for g in grads], "seq", out_steps)
    down_grad = handed_back([g[1] for g in grads], "seq", out_steps)

    return (
        block_output.reshape(block_input.shape),
        back_input.reshape(block_input.shape),
        gain_one_share,
        entry_share,
        exit_share,
        bias_total,
        gain_two_share,
        up_grad[None],
        down_grad[None],
    )


def solution(mesh):
    tokens = P(("dp", "expert"), "seq", None)
    columns = P(None, ALL)
    placed = (
        tokens,
        P(("dp", "expert"), None),
        tokens,
        tokens,
        P(ALL),
        columns,
        columns,
        P(),
        P(ALL),
        P(("dp", "expert"), None, "seq"),
        P(("dp", "expert"), "seq", None),
        tokens,
    )

    return jax.shard_map(
        local,
        mesh=mesh,
        in_specs=placed,
        out_specs=(
            tokens,
            tokens,
            P(ALL),
            columns,
            columns,
            P(),
            P(ALL),
            P(("dp", "expert"), None, "seq"),
            P(("dp", "expert"), "seq", None),
        ),
        check_vma=False,
    )
```

time: 356 us -> 310 us (0.87)
  waiting for transfers between devices: 144 us -> 118 us
  between operations: 18.7 us -> 1.33 us
  Pallas kernels: 49.4 us -> 66 us
  starting transfers between devices: 98.9 us -> 83.6 us
  blocking collectives: 8.1 us -> 0 us
  other arithmetic: 14 us -> 18.4 us
    all_to_all x12 -> x4, waiting for transfers between devices: 90.8 us -> 10.7 us  [exchanged(): return lax.all_to_all(array, axis, 0, 0, tiled=True)]
    ppermute x12 -> x43, waiting for transfers between devices: 47.2 us -> 104 us  [shift(): lax.ppermute(array, axis, tuple(((i, target(count, i, step)) for i in ran...]
    all_to_all x12 -> x4, starting transfers between devices: 63.1 us -> 19.9 us  [exchanged(): return lax.all_to_all(array, axis, 0, 0, tiled=True)]
    ppermute x12 -> x43, starting transfers between devices: 14.2 us -> 43.2 us  [shift(): lax.ppermute(array, axis, tuple(((i, target(count, i, step)) for i in ran...]
    pallas_call x6 -> x13, Pallas kernels: 38.6 us -> 53.5 us  [the longest x11 37.6 us: small_call(): pl.pallas_call(kernel, in_specs=specs(len(arrays)), out_shape=tuple((jax....]
    broadcast_in_dim x1 -> x2, other arithmetic: 0.09 us -> 6.24 us  [the longest x1 3.19 us: local(): up_grad[None]]
    ppermute x3, waiting for transfers between devices: 5.84 us -> 0.01 us  [local(): lax.ppermute(piece, ALL, tuple(((b, a) for a, b in pair)))]
    unnamed x56 -> x120, local copies, waits for them, and re-layouts: 2.16 us -> 7.76 us
  transfers between devices with their start and end apart: 30 -> 53, of which waited for: 19 -> 19; matrix products, arithmetic and copies ran while one was open for 7% -> 8% of each run, Pallas kernels for 12% -> 18%
where the time goes in v2:
time: 310 us; the launch traced here: 306 us
  waiting for transfers between devices  118 us (38%)
  starting transfers between devices  83.6 us (27%)
  Pallas kernels  66 us (21%)
  other arithmetic  18.4 us (6%)
  local copies, waits for them, and re-layouts  12.5 us (4%)
  matrix products  6.3 us (2%)
    ppermute x43, waiting for transfers between devices, shift(): lax.ppermute(array, axis, tuple(((i, target(count, i, step)) for i in ran...  104 us
    ppermute x43, starting transfers between devices, shift(): lax.ppermute(array, axis, tuple(((i, target(count, i, step)) for i in ran...  43.2 us
    pallas_call x11, Pallas kernels, small_call(): pl.pallas_call(kernel, in_specs=specs(len(arrays)), out_shape=tuple((jax....  37.6 us
    all_to_all x4, starting transfers between devices, exchanged(): return lax.all_to_all(array, axis, 0, 0, tiled=True)  19.9 us
    pallas_call x2, Pallas kernels, expert(): pl.pallas_call(functools.partial(expert_kernel, count), out_shape=(*[jax....  15.9 us
    pallas_call x2, Pallas kernels, expert_grad(): pl.pallas_call(functools.partial(expert_grad_kernel, len(rows)), out_shap...  12.5 us
    all_to_all x4, waiting for transfers between devices, exchanged(): return lax.all_to_all(array, axis, 0, 0, tiled=True)  10.7 us
    ppermute x3, starting transfers between devices, local(): lax.ppermute(piece, ALL, tuple(((b, a) for a, b in pair)))  10.5 us
  transfers between devices with their start and end apart: 53, of which 19 were waited for; matrix products, arithmetic and copies ran while one was open for 8% of the time, Pallas kernels for 18%

profile of v2, /device:TPU:18, one launch (start us, length us, event | category | flops | bytes accessed | tf_op | source)
XLA Modules:
  0.0 306.1 jit_solution(7799288909260168795)
XLA Ops:
  14.9 6.0 %collective-permute-start.5 = (bf16[24,768]{1,0:T(8,128)(2,1)}, bf16[24,768]{1,0:T(8,128)(2,1)S(1)}, u32[]{:S(2)}, u32[]{:S(2)}) collective-permute-start(bf16[24,768]{1,0:T(8,128)(2,1)} %get-tuple-element.77), channel_id=1, source_target_pairs={{0,0},{1,8},{2,2},{3,10},{4,18},{5,4},{6,12},{7,20},{8,6},{9,14},{... | collective-permute-start | bytes 110600 | tf_op jit(solution)/shard_map/ppermute | solution.py:657
  30.8 3.8 %collective-permute-done.10.refs_2_ = bf16[112,768]{1,0:T(8,128)(2,1)S(1)} collective-permute-done((bf16[112,768]{1,0:T(8,128)(2,1)}, bf16[112,768]{1,0:T(8,128)(2,1)S(1)}, u32[]{:S(2)}, u32[]{:S(2)}) %collective-permute-start.10) | collective-permute-done | bytes 172064 | tf_op jit(solution)/shard_map/ppermute | solution.py:588
  34.6 5.1 %collective-permute-done.12.refs_4_ = bf16[112,768]{1,0:T(8,128)(2,1)S(1)} collective-permute-done((bf16[112,768]{1,0:T(8,128)(2,1)}, bf16[112,768]{1,0:T(8,128)(2,1)S(1)}, u32[]{:S(2)}, u32[]{:S(2)}) %collective-permute-start.12) | collective-permute-done | bytes 172064 | tf_op jit(solution)/shard_map/ppermute | solution.py:588
  39.7 5.0 %collective-permute-done.14.refs_6_ = bf16[112,768]{1,0:T(8,128)(2,1)S(1)} collective-permute-done((bf16[112,768]{1,0:T(8,128)(2,1)}, bf16[112,768]{1,0:T(8,128)(2,1)S(1)}, u32[]{:S(2)}, u32[]{:S(2)}) %collective-permute-start.14) | collective-permute-done | bytes 172064 | tf_op jit(solution)/shard_map/ppermute | solution.py:588
  45.9 4.4 %all-to-all-start.1 = ((bf16[8,48,768]{2,1,0:T(8,128)(2,1)}), bf16[8,48,768]{2,1,0:T(8,128)(2,1)S(1)}, u32[]{:S(2)}, u32[]{:S(2)}) async-start(bf16[8,48,768]{2,1,0:T(8,128)(2,1)} %bitcast.14), calls=%async_computation.1 | async-start | bytes 1179648 | tf_op jit(solution)/shard_map/all_to_all | solution.py:596
  64.3 7.3 %shard_map.199 = (bf16[512,768]{1,0:T(8,128)(2,1)}, bf16[512,576]{1,0:T(8,128)(2,1)}, bf16[512,192]{1,0:T(8,128)(2,1)}, f32[512,3]{1,0:T(8,128)}) custom-call(s32[32]{0:T(128)} %dynamic-slice_bitcast_fusion.row_ref, bf16[128,768]{1,0:T(8,128)(2,1)} %copy-done.9, bf16[128,768]{1,0:T(8,128)(2,1)} %copy-done.16, bf16[128,768]{1,0:T(8,128)(2,1)} %copy-done.17, ...), custom_call_target="tpu_custom_call" | custom-call | tf_op jit(solution)/shard_map/pallas_call | solution.py:145
  76.0 3.7 %collective-permute-start.20 = (bf16[128,768]{1,0:T(8,128)(2,1)}, bf16[128,768]{1,0:T(8,128)(2,1)S(1)}, u32[]{:S(2)}, u32[]{:S(2)}) collective-permute-start(bf16[128,768]{1,0:T(8,128)(2,1)} %get-tuple-element.88), channel_id=1, source_target_pairs={{0,4},{2,6},{4,0},{6,2},{1,5},{3,7},{5,1},{7,3},{8,12},{10,14},{12... | collective-permute-start | bytes 589832 | tf_op jit(solution)/shard_map/ppermute | solution.py:588
  87.9 5.1 %all-to-all-start = ((bf16[8,48,768]{2,1,0:T(8,128)(2,1)}), bf16[8,48,768]{2,1,0:T(8,128)(2,1)S(1)}, u32[]{:S(2)}, u32[]{:S(2)}) async-start(bf16[8,48,768]{2,1,0:T(8,128)(2,1)} %bitcast.12), calls=%async_computation | async-start | bytes 1179648 | tf_op jit(solution)/shard_map/all_to_all | solution.py:596
  95.8 10.7 %all-to-all-done = bf16[8,48,768]{2,1,0:T(8,128)(2,1)S(1)} async-done(((bf16[8,48,768]{2,1,0:T(8,128)(2,1)}), bf16[8,48,768]{2,1,0:T(8,128)(2,1)S(1)}, u32[]{:S(2)}, u32[]{:S(2)}) %all-to-all-start) | async-done | bytes 589856 | tf_op jit(solution)/shard_map/all_to_all | solution.py:596
  107.2 14.9 %collective-permute-done.22.refs_1_ = bf16[768,768]{1,0:T(8,128)(2,1)} collective-permute-done((bf16[768,768]{1,0:T(8,128)(2,1)}, bf16[768,768]{1,0:T(8,128)(2,1)}, u32[]{:S(2)}, u32[]{:S(2)}) %collective-permute-start.22) | collective-permute-done | bytes 1179680 | tf_op jit(solution)/shard_map/ppermute | solution.py:588
  122.1 24.4 %collective-permute-done.23.refs_3_ = bf16[768,768]{1,0:T(8,128)(2,1)} collective-permute-done((bf16[768,768]{1,0:T(8,128)(2,1)}, bf16[768,768]{1,0:T(8,128)(2,1)}, u32[]{:S(2)}, u32[]{:S(2)}) %collective-permute-start.23) | collective-permute-done | bytes 1179680 | tf_op jit(solution)/shard_map/ppermute | solution.py:588
  148.3 8.0 %expert.3 = (bf16[384,768]{1,0:T(8,128)(2,1)}, bf16[384,768]{1,0:T(8,128)(2,1)}, bf16[384,768]{1,0:T(8,128)(2,1)}, bf16[384,768]{1,0:T(8,128)(2,1)}, bf16[384,768]{1,0:T(8,128)(2,1)}, /*index=5*/bf16[384,768]{1,0:T(8,128)(2,1)}) custom-call(bf16[384,768]{1,0:T(8,128)(2,1)} %copy-done.5, bf16[384,768]{1,0:T(8,128)(2,1)} %copy-done.4, ...), custom_call_target="tpu_custom_call" | custom-call | tf_op jit(solution)/shard_map/expert/pallas_call | solution.py:541
  157.1 8.0 %expert.2 = (bf16[384,768]{1,0:T(8,128)(2,1)}, bf16[384,768]{1,0:T(8,128)(2,1)}, bf16[384,768]{1,0:T(8,128)(2,1)}, bf16[384,768]{1,0:T(8,128)(2,1)}, bf16[384,768]{1,0:T(8,128)(2,1)}, /*index=5*/bf16[384,768]{1,0:T(8,128)(2,1)}) custom-call(bf16[384,768]{1,0:T(8,128)(2,1)} %bitcast.71, bf16[384,768]{1,0:T(8,128)(2,1)} %bitcast.67, ...), custom_call_target="tpu_custom_call" | custom-call | tf_op jit(solution)/shard_map/expert/pallas_call | solution.py:541
  165.0 6.0 %collective-permute-done.27 = bf16[384,768]{1,0:T(8,128)(2,1)S(1)} collective-permute-done((bf16[384,768]{1,0:T(8,128)(2,1)}, bf16[384,768]{1,0:T(8,128)(2,1)S(1)}, u32[]{:S(2)}, u32[]{:S(2)}) %collective-permute-start.27) | collective-permute-done | bytes 589856 | tf_op jit(solution)/shard_map/ppermute | solution.py:588
  173.1 5.1 %all-to-all-start.3 = ((bf16[8,48,768]{2,1,0:T(8,128)(2,1)}), bf16[8,48,768]{2,1,0:T(8,128)(2,1)S(1)}, u32[]{:S(2)}, u32[]{:S(2)}) async-start(bf16[8,48,768]{2,1,0:T(8,128)(2,1)} %bitcast.21), calls=%async_computation.3 | async-start | bytes 1179648 | tf_op jit(solution)/shard_map/all_to_all | solution.py:596
  179.0 6.1 %expert_grad.3 = (bf16[768,768]{1,0:T(8,128)(2,1)}, bf16[768,768]{1,0:T(8,128)(2,1)}) custom-call(bf16[384,768]{1,0:T(8,128)(2,1)} %bitcast.72, bf16[384,768]{1,0:T(8,128)(2,1)} %copy-done.5, bf16[384,768]{1,0:T(8,128)(2,1)} %get-tuple-element.134.refs_2_, bf16[384,768]{1,0:T(8,128)(2,1)} %get-tuple-element.135.refs_3_, ...), custom_call_target="tpu_custom_call" | custom-call | tf_op jit(solution)/shard_map/expert_grad/pallas_call | solution.py:568
  186.5 7.1 %collective-permute-done.26 = bf16[384,768]{1,0:T(8,128)(2,1)S(1)} collective-permute-done((bf16[384,768]{1,0:T(8,128)(2,1)S(1)}, bf16[384,768]{1,0:T(8,128)(2,1)S(1)}, u32[]{:S(2)}, u32[]{:S(2)}) %collective-permute-start.26) | collective-permute-done | bytes 589856 | tf_op jit(solution)/shard_map/ppermute | solution.py:588
  194.6 5.2 %all-to-all-start.2 = ((bf16[8,48,768]{2,1,0:T(8,128)(2,1)}), bf16[8,48,768]{2,1,0:T(8,128)(2,1)S(1)}, u32[]{:S(2)}, u32[]{:S(2)}) async-start(bf16[8,48,768]{2,1,0:T(8,128)(2,1)} %bitcast.18), calls=%async_computation.2 | async-start | bytes 1179648 | tf_op jit(solution)/shard_map/all_to_all | solution.py:596
  208.7 13.8 %collective-permute-done.29.refs_2_ = bf16[128,768]{1,0:T(8,128)(2,1)S(1)} collective-permute-done((bf16[128,768]{1,0:T(8,128)(2,1)S(1)}, bf16[128,768]{1,0:T(8,128)(2,1)S(1)}, u32[]{:S(2)}, u32[]{:S(2)}) %collective-permute-start.29) | collective-permute-done | bytes 196640 | tf_op jit(solution)/shard_map/ppermute | solution.py:588
  230.6 6.4 %expert_grad.2 = (f32[768,768]{1,0:T(8,128)}, f32[768,768]{1,0:T(8,128)}) custom-call(bf16[384,768]{1,0:T(8,128)(2,1)} %bitcast.73, bf16[384,768]{1,0:T(8,128)(2,1)} %copy-done.5, bf16[384,768]{1,0:T(8,128)(2,1)} %get-tuple-element.127.refs_2_, bf16[384,768]{1,0:T(8,128)(2,1)} %get-tuple-element.128.refs_3_, bf16[384,768]{1,0:T(8,128)(2,1)} %get-tuple-element.129.refs_4_, ...), custom_call_target="tpu_custom_call" | custom-call | tf_op jit(solution)/shard_map/expert_grad/pallas_call | solution.py:568
  237.7 10.3 %shard_map.202 = (f32[3,512]{1,0:T(4,128)}, f32[1,768]{1,0:T(1,128)}, bf16[576,768]{1,0:T(8,128)(2,1)}, bf16[128,768]{1,0:T(8,128)(2,1)}, bf16[128,768]{1,0:T(8,...) custom-call(s32[32]{0:T(128)} %dynamic-slice_bitcast_fusion.row_ref, ...), custom_call_target="tpu_custom_call" | custom-call | tf_op jit(solution)/shard_map/pallas_call | solution.py:145
  272.9 6.7 %collective-permute-done.39.refs_2_ = bf16[112,768]{1,0:T(8,128)(2,1)} collective-permute-done((bf16[112,768]{1,0:T(8,128)(2,1)}, bf16[112,768]{1,0:T(8,128)(2,1)}, u32[]{:S(2)}, u32[]{:S(2)}) %collective-permute-start.39) | collective-permute-done | bytes 172064 | tf_op jit(solution)/shard_map/ppermute | solution.py:588
  279.6 4.1 %collective-permute-done.40.refs_3_ = bf16[112,768]{1,0:T(8,128)(2,1)} collective-permute-done((bf16[112,768]{1,0:T(8,128)(2,1)}, bf16[112,768]{1,0:T(8,128)(2,1)}, u32[]{:S(2)}, u32[]{:S(2)}) %collective-permute-start.40) | collective-permute-done | bytes 172064 | tf_op jit(solution)/shard_map/ppermute | solution.py:588
  290.8 6.7 %collective-permute-start.43 = (f32[24,768]{1,0:T(8,128)}, f32[24,768]{1,0:T(8,128)S(1)}, u32[]{:S(2)}, u32[]{:S(2)}) collective-permute-start(f32[24,768]{1,0:T(8,128)} %get-tuple-element.118), channel_id=1, source_target_pairs={{0,0},{8,1},{2,2},{10,3},{18,4},{4,5},{12,6},{20,7},{6,8},{14,9},{... | collective-permute-start | bytes 221192 | tf_op jit(solution)/shard_map/ppermute | solution.py:803
  (253 shorter events, 121.0 us)
Async XLA Ops:
  2.1 19.7 %collective-permute-start.7 = (bf16[1,768]{1,0:T(2,128)(2,1)S(1)}, bf16[1,768]{1,0:T(2,128)(2,1)S(1)}, u32[]{:S(2)}, u32[]{:S(2)}) collective-permute-start(bf16[1,768]{1,0:T(2,128)(2,1)S(1)} %broadcast_in_dim.14.refs_4_), channel_id=1, source_target_pairs={{0,4},{2,6},{4,0},{6,2},{1,5},{3,7},{5,1},{7,3},{8,12},{10,14},{12... | collective-permute-start | bytes 4616 | tf_op jit(solution)/shard_map/ppermute | solution.py:588
  3.6 18.3 %collective-permute-start.8 = (bf16[1,768]{1,0:T(2,128)(2,1)S(1)}, bf16[1,768]{1,0:T(2,128)(2,1)S(1)}, u32[]{:S(2)}, u32[]{:S(2)}) collective-permute-start(bf16[1,768]{1,0:T(2,128)(2,1)S(1)} %broadcast_in_dim.14.refs_4_), channel_id=1, source_target_pairs={{0,6},{2,4},{4,2},{6,0},{1,7},{3,5},{5,3},{7,1},{8,14},{10,12},{12... | collective-permute-start | bytes 4616 | tf_op jit(solution)/shard_map/ppermute | solution.py:588
  21.8 37.2 %collective-permute-start = (bf16[128,768]{1,0:T(8,128)(2,1)S(1)}, bf16[128,768]{1,0:T(8,128)(2,1)S(1)}, u32[]{:S(2)}, u32[]{:S(2)}) collective-permute-start(bf16[128,768]{1,0:T(8,128)(2,1)S(1)} %fusion.12.refs_0_), channel_id=1, source_target_pairs={{0,2},{2,0},{4,6},{6,4},{1,3},{3,1},{5,7},{7,5},{8,10},{10,8},{12,... | collective-permute-start | bytes 589832 | tf_op jit(solution)/shard_map/ppermute | solution.py:588
  27.2 17.5 %collective-permute-start.14 = (bf16[112,768]{1,0:T(8,128)(2,1)}, bf16[112,768]{1,0:T(8,128)(2,1)S(1)}, u32[]{:S(2)}, u32[]{:S(2)}) collective-permute-start(bf16[112,768]{1,0:T(8,128)(2,1)} %shard_map.197.refs_0_), channel_id=1, source_target_pairs={{0,24},{8,16},{16,8},{24,0},{1,25},{9,17},{17,9},{25,1},{2,26},{10... | collective-permute-start | bytes 516104 | tf_op jit(solution)/shard_map/ppermute | solution.py:588
  30.8 19.6 %collective-permute-start.9 = (bf16[112,768]{1,0:T(8,128)(2,1)}, bf16[112,768]{1,0:T(8,128)(2,1)S(1)}, u32[]{:S(2)}, u32[]{:S(2)}) collective-permute-start(bf16[112,768]{1,0:T(8,128)(2,1)} %shard_map.197.refs_0_), channel_id=1, source_target_pairs={{0,1},{1,0},{2,3},{3,2},{4,5},{5,4},{6,7},{7,6},{8,9},{9,8},{10,11... | collective-permute-start | bytes 516104 | tf_op jit(solution)/shard_map/ppermute | solution.py:588
  34.6 16.7 %collective-permute-start.11 = (bf16[112,768]{1,0:T(8,128)(2,1)S(1)}, bf16[112,768]{1,0:T(8,128)(2,1)S(1)}, u32[]{:S(2)}, u32[]{:S(2)}) collective-permute-start(bf16[112,768]{1,0:T(8,128)(2,1)S(1)} %collective-permute-done.10.refs_2_), channel_id=1, source_target_pairs={{0,1},{1,0},{2,3},{3,2},{4,5},{5,4},{6,7},{7,6},{8,9},{9,8},{10,11... | collective-permute-start | bytes 516104 | tf_op jit(solution)/shard_map/ppermute | solution.py:588
  45.9 42.0 %all-to-all-start.1 = ((bf16[8,48,768]{2,1,0:T(8,128)(2,1)}), bf16[8,48,768]{2,1,0:T(8,128)(2,1)S(1)}, u32[]{:S(2)}, u32[]{:S(2)}) async-start(bf16[8,48,768]{2,1,0:T(8,128)(2,1)} %bitcast.14), calls=%async_computation.1 | async-start | bytes 1179648 | tf_op jit(solution)/shard_map/all_to_all | solution.py:596
  87.9 18.6 %all-to-all-start = ((bf16[8,48,768]{2,1,0:T(8,128)(2,1)}), bf16[8,48,768]{2,1,0:T(8,128)(2,1)S(1)}, u32[]{:S(2)}, u32[]{:S(2)}) async-start(bf16[8,48,768]{2,1,0:T(8,128)(2,1)} %bitcast.12), calls=%async_computation | async-start | bytes 1179648 | tf_op jit(solution)/shard_map/all_to_all | solution.py:596
  93.0 29.2 %collective-permute-start.22 = (bf16[768,768]{1,0:T(8,128)(2,1)}, bf16[768,768]{1,0:T(8,128)(2,1)}, u32[]{:S(2)}, u32[]{:S(2)}) collective-permute-start(bf16[768,768]{1,0:T(8,128)(2,1)} %bitcast.16.refs_0_), channel_id=1, source_target_pairs={{0,4},{2,6},{4,0},{6,2},{1,5},{3,7},{5,1},{7,3},{8,12},{10,14},{12... | collective-permute-start | bytes 3538952 | tf_op jit(solution)/shard_map/ppermute | solution.py:588
  93.7 52.9 %collective-permute-start.23 = (bf16[768,768]{1,0:T(8,128)(2,1)}, bf16[768,768]{1,0:T(8,128)(2,1)}, u32[]{:S(2)}, u32[]{:S(2)}) collective-permute-start(bf16[768,768]{1,0:T(8,128)(2,1)} %bitcast.17.refs_2_), channel_id=1, source_target_pairs={{0,4},{2,6},{4,0},{6,2},{1,5},{3,7},{5,1},{7,3},{8,12},{10,14},{12... | collective-permute-start | bytes 3538952 | tf_op jit(solution)/shard_map/ppermute | solution.py:588
  95.0 51.6 %collective-permute-start.25 = (bf16[384,768]{1,0:T(8,128)(2,1)S(1)}, bf16[384,768]{1,0:T(8,128)(2,1)S(1)}, u32[]{:S(2)}, u32[]{:S(2)}) collective-permute-start(bf16[384,768]{1,0:T(8,128)(2,1)S(1)} %bitcast.66), channel_id=1, source_target_pairs={{0,2},{2,0},{4,6},{6,4},{1,3},{3,1},{5,7},{7,5},{8,10},{10,8},{12,... | collective-permute-start | bytes 1769480 | tf_op jit(solution)/shard_map/ppermute | solution.py:588
  106.5 40.1 %collective-permute-start.24 = (bf16[384,768]{1,0:T(8,128)(2,1)S(1)}, bf16[384,768]{1,0:T(8,128)(2,1)S(1)}, u32[]{:S(2)}, u32[]{:S(2)}) collective-permute-start(bf16[384,768]{1,0:T(8,128)(2,1)S(1)} %bitcast.70), channel_id=1, source_target_pairs={{0,2},{2,0},{4,6},{6,4},{1,3},{3,1},{5,7},{7,5},{8,10},{10,8},{12,... | collective-permute-start | bytes 1769480 | tf_op jit(solution)/shard_map/ppermute | solution.py:588
  173.1 21.4 %all-to-all-start.3 = ((bf16[8,48,768]{2,1,0:T(8,128)(2,1)}), bf16[8,48,768]{2,1,0:T(8,128)(2,1)S(1)}, u32[]{:S(2)}, u32[]{:S(2)}) async-start(bf16[8,48,768]{2,1,0:T(8,128)(2,1)} %bitcast.21), calls=%async_computation.3 | async-start | bytes 1179648 | tf_op jit(solution)/shard_map/all_to_all | solution.py:596
  178.2 15.3 %collective-permute-start.26 = (bf16[384,768]{1,0:T(8,128)(2,1)S(1)}, bf16[384,768]{1,0:T(8,128)(2,1)S(1)}, u32[]{:S(2)}, u32[]{:S(2)}) collective-permute-start(bf16[384,768]{1,0:T(8,128)(2,1)S(1)} %copy-done.59), channel_id=1, source_target_pairs={{0,2},{2,0},{4,6},{6,4},{1,3},{3,1},{5,7},{7,5},{8,10},{10,8},{12,... | collective-permute-start | bytes 1769480 | tf_op jit(solution)/shard_map/ppermute | solution.py:588
  185.1 73.7 %collective-permute-start.47 = (bf16[768,768]{1,0:T(8,128)(2,1)}, bf16[768,768]{1,0:T(8,128)(2,1)}, u32[]{:S(2)}, u32[]{:S(2)}) collective-permute-start(bf16[768,768]{1,0:T(8,128)(2,1)} %get-tuple-element.138), channel_id=1, source_target_pairs={{0,4},{2,6},{4,0},{6,2},{1,5},{3,7},{5,1},{7,3},{8,12},{10,14},{12... | collective-permute-start | bytes 3538952 | tf_op jit(solution)/shard_map/ppermute | solution.py:588
  194.6 60.0 %all-to-all-start.2 = ((bf16[8,48,768]{2,1,0:T(8,128)(2,1)}), bf16[8,48,768]{2,1,0:T(8,128)(2,1)S(1)}, u32[]{:S(2)}, u32[]{:S(2)}) async-start(bf16[8,48,768]{2,1,0:T(8,128)(2,1)} %bitcast.18), calls=%async_computation.2 | async-start | bytes 1179648 | tf_op jit(solution)/shard_map/all_to_all | solution.py:596
  201.7 20.8 %collective-permute-start.29 = (bf16[128,768]{1,0:T(8,128)(2,1)S(1)}, bf16[128,768]{1,0:T(8,128)(2,1)S(1)}, u32[]{:S(2)}, u32[]{:S(2)}) collective-permute-start(bf16[128,768]{1,0:T(8,128)(2,1)S(1)} %get-tuple-element.145.refs_0_), channel_id=1, source_target_pairs={{0,4},{2,6},{4,0},{6,2},{1,5},{3,7},{5,1},{7,3},{8,12},{10,14},{12... | collective-permute-start | bytes 589832 | tf_op jit(solution)/shard_map/ppermute | solution.py:588
  203.1 19.4 %collective-permute-start.30 = (bf16[128,768]{1,0:T(8,128)(2,1)S(1)}, bf16[128,768]{1,0:T(8,128)(2,1)S(1)}, u32[]{:S(2)}, u32[]{:S(2)}) collective-permute-start(bf16[128,768]{1,0:T(8,128)(2,1)S(1)} %get-tuple-element.145.refs_0_), channel_id=1, source_target_pairs={{0,6},{2,4},{4,2},{6,0},{1,7},{3,5},{5,3},{7,1},{8,14},{10,12},{12... | collective-permute-start | bytes 589832 | tf_op jit(solution)/shard_map/ppermute | solution.py:588
  204.5 62.1 %collective-permute-start.48 = (bf16[768,768]{1,0:T(8,128)(2,1)}, bf16[768,768]{1,0:T(8,128)(2,1)}, u32[]{:S(2)}, u32[]{:S(2)}) collective-permute-start(bf16[768,768]{1,0:T(8,128)(2,1)} %get-tuple-element.140), channel_id=1, source_target_pairs={{0,4},{2,6},{4,0},{6,2},{1,5},{3,7},{5,1},{7,3},{8,12},{10,14},{12... | collective-permute-start | bytes 3538952 | tf_op jit(solution)/shard_map/ppermute | solution.py:588
  226.5 21.5 %collective-permute-start.34 = (bf16[4,48,192]{2,1,0:T(8,128)(2,1)}, bf16[4,48,192]{2,1,0:T(8,128)(2,1)S(1)}, u32[]{:S(2)}, u32[]{:S(2)}) collective-permute-start(bf16[4,48,192]{2,1,0:T(8,128)(2,1)} %get-tuple-element.104), channel_id=1, source_target_pairs={{0,2},{2,0},{4,6},{6,4},{1,3},{3,1},{5,7},{7,5},{8,10},{10,8},{12,... | collective-permute-start | bytes 221192 | tf_op jit(solution)/shard_map/ppermute | solution.py:588
  227.8 23.1 %collective-permute-start.35 = (bf16[4,48,192]{2,1,0:T(8,128)(2,1)}, bf16[4,48,192]{2,1,0:T(8,128)(2,1)S(1)}, u32[]{:S(2)}, u32[]{:S(2)}) collective-permute-start(bf16[4,48,192]{2,1,0:T(8,128)(2,1)} %get-tuple-element.105), channel_id=1, source_target_pairs={{0,4},{2,6},{4,0},{6,2},{1,5},{3,7},{5,1},{7,3},{8,12},{10,14},{12... | collective-permute-start | bytes 221192 | tf_op jit(solution)/shard_map/ppermute | solution.py:588
  228.5 22.4 %collective-permute-start.36 = (bf16[4,48,192]{2,1,0:T(8,128)(2,1)}, bf16[4,48,192]{2,1,0:T(8,128)(2,1)S(1)}, u32[]{:S(2)}, u32[]{:S(2)}) collective-permute-start(bf16[4,48,192]{2,1,0:T(8,128)(2,1)} %get-tuple-element.106), channel_id=1, source_target_pairs={{0,6},{2,4},{4,2},{6,0},{1,7},{3,5},{5,3},{7,1},{8,14},{10,12},{12... | collective-permute-start | bytes 221192 | tf_op jit(solution)/shard_map/ppermute | solution.py:588
  267.1 16.5 %collective-permute-start.40 = (bf16[112,768]{1,0:T(8,128)(2,1)}, bf16[112,768]{1,0:T(8,128)(2,1)}, u32[]{:S(2)}, u32[]{:S(2)}) collective-permute-start(bf16[112,768]{1,0:T(8,128)(2,1)} %get-tuple-element.115), channel_id=1, source_target_pairs={{0,24},{8,16},{16,8},{24,0},{1,25},{9,17},{17,9},{25,1},{2,26},{10... | collective-permute-start | bytes 516104 | tf_op jit(solution)/shard_map/ppermute | solution.py:588
  286.9 15.4 %collective-permute-start.41 = (f32[24,768]{1,0:T(8,128)}, f32[24,768]{1,0:T(8,128)S(1)}, u32[]{:S(2)}, u32[]{:S(2)}) collective-permute-start(f32[24,768]{1,0:T(8,128)} %get-tuple-element.116), channel_id=1, source_target_pairs={{0,0},{8,1},{16,2},{2,3},{10,4},{18,5},{4,6},{12,7},{6,8},{14,9},{... | collective-permute-start | bytes 221192 | tf_op jit(solution)/shard_map/ppermute | solution.py:803
  (89 other events, 920.7 us)

commit v3 on v2

--- a/solution.py
+++ b/solution.py
@@ -105,27 +105,24 @@
         )
         device = np.arange(n_dp * n_seq * n_ex)
         dp, seq, ex = device // (n_seq * n_ex), device // n_ex % n_seq, device % n_ex
-        parts = {
-            "send_sub": send,
-            "slot_round": receive,
-            "sub_round": inverse_rows(send),
-            "send_slot": inverse_rows(receive),
-            "from_seq": positions_of(n_seq, -1)[seq],
-            "to_seq": positions_of(n_seq, 1)[seq],
-            "from_dp": positions_of(n_dp, -1)[dp],
-            "to_dp": positions_of(n_dp, 1)[dp],
-            "from_ex": positions_of(n_ex, -1)[ex],
-            "to_ex": positions_of(n_ex, 1)[ex],
-        }
-        self.start = {}
-        width = 0
-        for name, part in parts.items():
-            self.start[name] = width
-            width += part.shape[1]
-        self.table = np.concatenate(list(parts.values()), axis=1).astype(np.int32)
-
-    def at(self, ref, name, i):
-        return ref[self.start[name] + i]
+        self.width = 0
+        self.columns = []
+        self.send_sub = self.add(send)
+        self.slot_round = self.add(receive)
+        self.sub_round = self.add(inverse_rows(send))
+        self.send_slot = self.add(inverse_rows(receive))
+        self.from_seq = self.add(positions_of(n_seq, -1)[seq])
+        self.to_seq = self.add(positions_of(n_seq, 1)[seq])
+        self.from_dp = self.add(positions_of(n_dp, -1)[dp])
+        self.to_dp = self.add(positions_of(n_dp, 1)[dp])
+        self.from_ex = self.add(positions_of(n_ex, -1)[ex])
+        self.to_ex = self.add(positions_of(n_ex, 1)[ex])
+        self.table = np.concatenate(self.columns, axis=1).astype(np.int32)
+
+    def add(self, part):
+        self.columns.append(part)
+        self.width += part.shape[1]
+        return self.width - part.shape[1]
 
 
 def chosen(values, index):
@@ -150,8 +147,8 @@
     )(info_row, *arrays)
 
 
-def whole_tiles(rows):
-    return -(-rows // 16) * 16
+def whole_tiles(rows, tile=16):
+    return -(-rows // tile) * tile
 
 
 def pick_kernel(info, row_ref, entry_ref, *out_refs):
@@ -159,7 +156,7 @@
     chunk = info.chunk
     parts = [entry[i * chunk : (i + 1) * chunk, :] for i in range(info.per)]
     for i, out_ref in enumerate(out_refs):
-        out_ref[...] = chosen(parts, info.at(row_ref, "send_sub", i)).astype(BF)
+        out_ref[...] = chosen(parts, row_ref[info.send_sub + i]).astype(BF)
 
 
 def place_kernel(info, n_seq, share, row_ref, *refs):
@@ -173,12 +170,12 @@
     for i in range(n_seq):
         value = rows[0]
         for j in range(1, n_seq):
-            value = jnp.where(info.at(row_ref, "from_seq", j) == i, rows[j], value)
+            value = jnp.where(row_ref[info.from_seq + j] == i, rows[j], value)
         line_ref[share + i : share + i + 1, :] = value
     parts = [ref[...].astype(F32) for ref in came]
     for i in range(per):
         line_ref[head + i * chunk : head + (i + 1) * chunk, :] = chosen(
-            parts, info.at(row_ref, "slot_round", i)
+            parts, row_ref[info.slot_round + i]
         )
     out_ref[...] = line_ref[...].astype(BF)
 
@@ -191,7 +188,7 @@
     head = whole_tiles(share + n_seq)
     for i in range(n_dp):
         for j in range(n_ex):
-            spot = info.at(row_ref, "from_ex", j) * n_dp + info.at(row_ref, "from_dp", i)
+            spot = row_ref[info.from_ex + j] * n_dp + row_ref[info.from_dp + i]
             all_ref[spot] = blocks[i * n_ex + j][...]
     for spot in range(n_ex * n_dp):
         ex, dp = divmod(spot, n_dp)
@@ -206,28 +203,17 @@
                 ]
     entry_ref[...] = line_ref[...].astype(BF)
     for i in range(n_seq):
-        exit_refs[i][...] = exits_ref[info.at(row_ref, "to_seq", i)].astype(BF)
+        exit_refs[i][...] = exits_ref[row_ref[info.to_seq + i]].astype(BF)
 
 
 def pack_kernel(info, n_dp, n_seq, n_ex, share, owned, row_ref, *refs):
     exits, refs = refs[:n_seq], refs[n_seq:]
-    entry_ref, diag_ref, one_ref, two_ref, hot_ref = refs[:5]
-    out_refs, (four_ref, small_ref, all_ref) = refs[5 : 5 + n_ex], refs[5 + n_ex :]
+    entry_ref, out_refs, (four_ref, all_ref) = refs[0], refs[1 : 1 + n_ex], refs[1 + n_ex :]
     width = exits[0].shape[2]
-    heads, buckets = diag_ref.shape[0], hot_ref.shape[0]
     head = whole_tiles(share + 2)
     for i in range(n_seq):
-        four_ref[info.at(row_ref, "from_seq", i)] = exits[i][...].astype(F32)
-    bias = lax.dot_general(
-        diag_ref[...], hot_ref[...], (((1,), (1,)), ((), ())), precision=HIGH,
-        preferred_element_type=F32,
-    )
-    small_ref[...] = jnp.zeros_like(small_ref)
+        four_ref[row_ref[info.from_seq + i]] = exits[i][...].astype(F32)
     all_ref[...] = jnp.zeros_like(all_ref)
-    for seq in range(n_seq):
-        for k in range(heads):
-            lane = seq * width + 2 * share + k * buckets
-            small_ref[0:1, lane : lane + buckets] = bias[k : k + 1, :]
     entry = entry_ref[...].astype(F32)
     for spot in range(n_ex * n_dp):
         ex, dp = divmod(spot, n_dp)
@@ -236,73 +222,71 @@
             all_ref[ex, dp, :share, to : to + width] = four_ref[
                 seq, dp, ex * share : (ex + 1) * share, :
             ]
-            lane = ((dp * n_seq + seq) * n_ex + ex) * share
-            small_ref[0:1, to : to + share] = one_ref[:, lane : lane + share]
-            small_ref[0:1, to + share : to + 2 * share] = two_ref[:, lane : lane + share]
-        small = small_ref[0:1, :]
-        upper = small.astype(BF).astype(F32)
-        all_ref[ex, dp, share : share + 1, :] = upper
-        all_ref[ex, dp, share + 1 : share + 2, :] = small - upper
         all_ref[ex, dp, head : head + owned, :] = entry[spot * owned : (spot + 1) * owned, :]
     for i in range(n_ex):
-        out_refs[i][...] = all_ref[info.at(row_ref, "to_ex", i)].astype(BF)
+        out_refs[i][...] = all_ref[row_ref[info.to_ex + i]].astype(BF)
+
+
+def small_kernel(info, n_dp, n_seq, n_ex, share, heads, buckets, row_ref, *refs):
+    small, out_refs, (four_ref, all_ref) = refs[:n_seq], refs[n_seq:-2], refs[-2:]
+    for i in range(n_seq):
+        four_ref[row_ref[info.from_seq + i]] = small[i][...]
+    total = four_ref[0]
+    for seq in range(1, n_seq):
+        total = total + four_ref[seq]
+    all_ref[...] = jnp.zeros_like(all_ref)
+    part = heads * buckets
+    for ex in range(n_ex):
+        lines = slice(ex * n_dp, (ex + 1) * n_dp)
+        all_ref[ex, :, : 2 * share] = total[lines, : 2 * share]
+        for seq in range(n_seq):
+            lane = 2 * share + seq * part
+            all_ref[ex, :, lane : lane + part] = four_ref[seq, lines, 2 * share : 2 * share + part]
+    for i in range(n_ex):
+        out_refs[i][...] = all_ref[row_ref[info.to_ex + i]]
 
 
 def fold_kernel(info, n_dp, n_ex, share, row_ref, *refs):
-    parts, out_refs, all_ref = refs[:n_ex], refs[n_ex : n_ex + n_dp], refs[n_ex + n_dp]
+    parts, small, refs = refs[:n_ex], refs[n_ex : 2 * n_ex], refs[2 * n_ex :]
+    out_refs, all_ref = refs[:n_dp], refs[n_dp]
+    line = small[0][...]
+    for part in small[1:]:
+        line = line + part[...]
+    upper = line.astype(BF).astype(F32)
+    lower = line - upper
+    width = line.shape[1]
     for dp in range(n_dp):
         total = parts[0][dp].astype(F32)
         for part in parts[1:]:
             total = total + part[dp].astype(F32)
         all_ref[dp] = total
-        small = total[share : share + 1, :] + total[share + 1 : share + 2, :]
-        upper = small.astype(BF).astype(F32)
-        all_ref[dp, share : share + 1, :] = upper
-        all_ref[dp, share + 1 : share + 2, :] = small - upper
+        all_ref[dp, share : share + 1, :width] = upper[dp : dp + 1, :]
+        all_ref[dp, share + 1 : share + 2, :width] = lower[dp : dp + 1, :]
     for i in range(n_dp):
-        out_refs[i][...] = all_ref[info.at(row_ref, "to_dp", i)].astype(BF)
-
-
-def finish_kernel(info, n_dp, n_seq, share, row_ref, *refs):
-    parts, refs = refs[:n_dp], refs[n_dp:]
-    exit_ref, *refs = refs
-    piece_refs, small_refs, four_ref = refs[: info.per], refs[info.per : -1], refs[-1]
-    head, chunk = whole_tiles(share + 2), info.chunk
+        out_refs[i][...] = all_ref[row_ref[info.to_dp + i]].astype(BF)
+
+
+def finish_kernel(info, n_dp, share, row_ref, *refs):
+    parts, (exit_ref, small_ref, *piece_refs) = refs[:n_dp], refs[n_dp:]
+    chunk = info.chunk
+    head = whole_tiles(share + 2)
     total = parts[0][...].astype(F32)
     for part in parts[1:]:
         total = total + part[...].astype(F32)
     exit_ref[...] = total[:share, :]
     small = total[share : share + 1, :] + total[share + 1 : share + 2, :]
-    width = four_ref.shape[2]
-    for seq in range(n_seq):
-        four_ref[seq] = small[:, seq * width : (seq + 1) * width]
-    for i in range(n_seq):
-        small_refs[i][...] = four_ref[info.at(row_ref, "to_seq", i)]
+    small_ref[...] = small[:, : small_ref.shape[1]]
     pieces = [total[head + i * chunk : head + (i + 1) * chunk, :] for i in range(info.per)]
     for i in range(info.per):
-        piece_refs[i][...] = chosen(pieces, info.at(row_ref, "send_slot", i))
-
-
-def close_kernel(info, n_seq, share, heads, row_ref, *refs):
-    came, small, refs = refs[: info.per], refs[info.per : info.per + n_seq], refs[info.per + n_seq :]
-    entry_ref, gain_ref, bias_ref, four_ref = refs
-    chunk, buckets = info.chunk, bias_ref.shape[1]
+        piece_refs[i][...] = chosen(pieces, row_ref[info.send_slot + i])
+
+
+def close_kernel(info, row_ref, *refs):
+    came, entry_ref = refs[: info.per], refs[info.per]
+    chunk = info.chunk
     parts = [ref[...] for ref in came]
     for i in range(info.per):
-        entry_ref[i * chunk : (i + 1) * chunk, :] = chosen(parts, info.at(row_ref, "sub_round", i))
-    for i in range(n_seq):
-        four_ref[info.at(row_ref, "from_seq", i)] = small[i][...]
-    total = four_ref[0]
-    for seq in range(1, n_seq):
-        total = total + four_ref[seq]
-    gain_ref[0:1, :] = total[:, :share]
-    gain_ref[1:2, :] = total[:, share : 2 * share]
-    for seq in range(n_seq):
-        for k in range(heads):
-            lane = 2 * share + k * buckets
-            bias_ref[seq * heads + k : seq * heads + k + 1, :] = four_ref[
-                seq, :, lane : lane + buckets
-            ]
+        entry_ref[i * chunk : (i + 1) * chunk, :] = chosen(parts, row_ref[info.sub_round + i])
 
 
 def allowed_of(docs_row, docs_col, start, rows, keys):
@@ -329,7 +313,7 @@
     width = heads * size
     factor = size ** (-0.5)
     for i in range(count):
-        x_ref[aligned(rows, info.at(row_ref, "from_seq", i)), :] = x_refs[i][...]
+        x_ref[aligned(rows, row_ref[info.from_seq + i]), :] = x_refs[i][...]
     normed = (x_ref[...].astype(F32) * gain_ref[0:1, :]).astype(BF)
     qkv_ref[...] = dot(normed, w_ref[...], 1, 1).astype(BF)
     for start in range(0, length, BLOCK):
@@ -375,7 +359,7 @@
     rows = part_refs[0].shape[0]
     share = exits[0].shape[1]
     for i in range(n_seq):
-        four_ref[info.at(row_ref, "from_seq", i)] = exits[i][...].astype(F32)
+        four_ref[row_ref[info.from_seq + i]] = exits[i][...].astype(F32)
     for dp in range(n_dp):
         for seq in range(n_seq):
             for ex in range(n_ex):
@@ -383,7 +367,7 @@
                 line_ref[start : start + share, :] = four_ref[seq, ex * n_dp + dp]
     exit_ref[...] = line_ref[...].astype(BF)
     for i, part_ref in enumerate(part_refs):
-        block = aligned(rows, info.at(row_ref, "to_seq", i))
+        block = aligned(rows, row_ref[info.to_seq + i])
         part_ref[...] = dot(ctx_ref[block, :], exit_ref[...], 1, 1).astype(BF)
 
 
@@ -405,14 +389,14 @@
     ctx_ref, up_ref, *grad_refs, all_ref = refs
     rows = up_refs[0].shape[0]
     for i in range(count):
-        up_ref[aligned(rows, info.at(row_ref, "from_seq", i)), :] = up_refs[i][...]
+        up_ref[aligned(rows, row_ref[info.from_seq + i]), :] = up_refs[i][...]
     grad = dot(up_ref[...], ctx_ref[...], 0, 0)
     for dp in range(n_dp):
         for i in range(count):
             start = (dp * count + i) * share
             all_ref[i, dp] = grad[start : start + share, :]
     for i in range(count):
-        grad_refs[i][...] = all_ref[info.at(row_ref, "to_seq", i)].astype(BF)
+        grad_refs[i][...] = all_ref[row_ref[info.to_seq + i]].astype(BF)
 
 
 def leave_back(info, n_dp, info_row, blocks, ctx):
@@ -429,10 +413,11 @@
     )
 
 
-def attend_back_kernel(info, heads, size, count, row_ref, *refs):
+def attend_back_kernel(info, heads, size, count, n_dp, n_ex, share, row_ref, *refs):
     up_ref, exit_ref, qkv_ref, log_ref, doc_ref, col_ref, lag_ref, x_ref, gain_ref, w_ref = refs[:10]
-    diag_ref, gain_grad_ref, entry_ref, *refs = refs[10:]
-    back_refs, (bctx_ref, bqkv_ref, bk_ref, bv_ref, lines_ref) = refs[:count], refs[count:]
+    two_ref, hot_ref, entry_ref, *refs = refs[10:]
+    back_refs, small_refs, refs = refs[:count], refs[count : 2 * count], refs[2 * count :]
+    bctx_ref, bqkv_ref, bk_ref, bv_ref, lines_ref, diag_ref, four_ref = refs
     length = up_ref.shape[0]
     rows = length // count
     width = heads * size
@@ -478,29 +463,47 @@
     bqkv_ref[:, 2 * width :] = bv_ref[...].astype(BF)
     normed = (x_ref[...].astype(F32) * gain_ref[0:1, :]).astype(BF)
     entry_ref[...] = dot(bqkv_ref[...], normed, 0, 0).astype(BF)
-    gain_grad = jnp.zeros(gain_grad_ref.shape, F32)
+    gain_grad = jnp.zeros((1, x_ref.shape[1]), F32)
     for i in range(count):
-        block = aligned(rows, info.at(row_ref, "to_seq", i))
+        block = aligned(rows, row_ref[info.to_seq + i])
         back = dot(bqkv_ref[block, :], w_ref[...], 1, 0)
         back_refs[i][...] = back.astype(BF)
         gain_grad += jnp.sum(back * x_ref[block, :].astype(F32), axis=0, keepdims=True)
-    gain_grad_ref[...] = gain_grad
+    bias = lax.dot_general(
+        diag_ref[...], hot_ref[...], (((1,), (1,)), ((), ())), precision=HIGH,
+        preferred_element_type=F32,
+    )
+    buckets = hot_ref.shape[0]
+    four_ref[...] = jnp.zeros_like(four_ref)
+    for k in range(heads):
+        lane = 2 * share + k * buckets
+        four_ref[:, :, lane : lane + buckets] = jnp.broadcast_to(
+            bias[k : k + 1, :].reshape(1, 1, buckets), (count, n_ex * n_dp, buckets)
+        )
+    for seq in range(count):
+        for spot in range(n_ex * n_dp):
+            ex, dp = divmod(spot, n_dp)
+            lane = ((dp * count + seq) * n_ex + ex) * share
+            four_ref[seq, spot : spot + 1, :share] = gain_grad[:, lane : lane + share]
+            four_ref[seq, spot : spot + 1, share : 2 * share] = two_ref[:, lane : lane + share]
+    for i in range(count):
+        small_refs[i][...] = four_ref[row_ref[info.to_seq + i]]
 
 
 def attend_back(
-    info, heads, size, count, info_row, up, exit_t, qkv, log, docs_row, docs_col, lag, x, gain, w
+    info, heads, size, count, n_dp, n_ex, share, info_row,
+    up, exit_t, qkv, log, docs_row, docs_col, lag, x, gain, w, gain_two_grad, hot,
 ):
     length, features = up.shape
     width = heads * size
-    diag, gain_grad, entry, *backs = small_call(
-        functools.partial(attend_back_kernel, info, heads, size, count),
+    entry, *rest = small_call(
+        functools.partial(attend_back_kernel, info, heads, size, count, n_dp, n_ex, share),
         info_row,
-        (up, exit_t, qkv, log, docs_row, docs_col, lag, x, gain, w),
+        (up, exit_t, qkv, log, docs_row, docs_col, lag, x, gain, w, gain_two_grad, hot),
         [
-            ((heads, length), F32),
-            ((1, features), F32),
             ((3 * width, features), BF),
             *[((length // count, features), BF)] * count,
+            *[((n_ex * n_dp, width), F32)] * count,
         ],
         [
             ((length, width), BF),
@@ -508,71 +511,103 @@
             ((length, width), F32),
             ((length, width), F32),
             ((8 * heads, length), F32),
+            ((heads, length), F32),
+            ((count, n_ex * n_dp, width), F32),
         ],
     )
-    return diag, gain_grad, entry, backs
-
-
-def expert_kernel(count, rows_ref, up_ref, *refs):
-    w_ups, w_downs, refs = refs[:count], refs[count : 2 * count], refs[2 * count :]
-    back_ref, result_ref, acts, bbs = refs[0], refs[1], refs[2 : 2 + count], refs[2 + count :]
-    for i in range(count):
-        before = dot(rows_ref[...], w_ups[i][...], 1, 0)
+    return entry, rest[:count], rest[count:]
+
+
+def norm_kernel(row_ref, in_ref, gain_ref, place_ref, *refs):
+    parts, (hidden_ref, scale_ref, send_ref) = refs[:-3], refs[-3:]
+    hidden = parts[0][...].astype(F32)
+    for part in parts[1:]:
+        hidden = hidden + part[...].astype(F32)
+    hidden = in_ref[...] + hidden
+    scale = rms_scale(hidden)
+    normed = (hidden * scale * gain_ref[1:2, :]).astype(BF)
+    hidden_ref[...] = hidden
+    scale_ref[...] = scale
+    send_ref[...] = dot(place_ref[...], normed, 1, 0).astype(BF)
+
+
+def joined(refs):
+    return refs[0][...] if len(refs) == 1 else jnp.concatenate([ref[...] for ref in refs], axis=0)
+
+
+def expert_kernel(tree, *refs):
+    rows_ref, up_ref, w_ups, w_downs, back_ref, acts, bbs = jax.tree.unflatten(tree, refs)
+    back = None
+    for w_up, w_down, act_ref, bb_ref in zip(w_ups, w_downs, acts, bbs):
+        w_up, w_down = joined(w_up), joined(w_down)
+        before = dot(rows_ref[...], w_up, 1, 0)
         tangent = jnp.tanh(SLOPE * (before + CUBIC * before * before * before))
-        acts[i][...] = (0.5 * before * (1.0 + tangent)).astype(BF)
+        act_ref[...] = (0.5 * before * (1.0 + tangent)).astype(BF)
         slope = 0.5 * (1.0 + tangent) + 0.5 * before * (1.0 - tangent * tangent) * SLOPE * (
             1.0 + 3.0 * CUBIC * before * before
         )
-        bbs[i][...] = (dot(up_ref[...], w_downs[i][...], 1, 1) * slope).astype(BF)
-    back = dot(bbs[0][...], w_ups[0][...], 1, 1)
-    for i in range(1, count):
-        back = back + dot(bbs[i][...], w_ups[i][...], 1, 1)
+        bb_ref[...] = (dot(up_ref[...], w_down, 1, 1) * slope).astype(BF)
+        part = dot(bb_ref[...], w_up, 1, 1)
+        back = part if back is None else back + part
     back_ref[...] = back.astype(BF)
-    result = dot(acts[0][...], w_downs[0][...], 1, 0)
-    for i in range(1, count):
-        result = result + dot(acts[i][...], w_downs[i][...], 1, 0)
-    result_ref[...] = result.astype(BF)
+
+
+def tree_call(kernel, inputs, outs):
+    tree = jax.tree.structure((*inputs, *outs))
+    return pl.pallas_call(
+        functools.partial(kernel, tree), out_shape=tuple(jax.tree.leaves(outs))
+    )(*jax.tree.leaves(inputs))
+
+
+def like(shape, kind=BF):
+    return jax.ShapeDtypeStruct(shape, kind)
 
 
 def expert(rows, upstream, w_ups, w_downs):
     count = len(w_ups)
-    tokens, features = rows.shape
-    hidden = w_ups[0].shape[1]
-    out = pl.pallas_call(
-        functools.partial(expert_kernel, count),
-        out_shape=(
-            *[jax.ShapeDtypeStruct((tokens, features), BF)] * 2,
-            *[jax.ShapeDtypeStruct((tokens, hidden), BF)] * (2 * count),
-        ),
-        name="expert",
-    )(rows, upstream, *w_ups, *w_downs)
-    return out[0], out[1], out[2 : 2 + count], out[2 + count :]
-
-
-def expert_grad_kernel(count, *refs):
-    rows, bbs = refs[:count], refs[count : 2 * count]
-    acts, ups = refs[2 * count : 3 * count], refs[3 * count : 4 * count]
-    up_ref, down_ref = refs[4 * count :]
-    total = dot(rows[0][...], bbs[0][...], 0, 0)
-    for i in range(1, count):
-        total = total + dot(rows[i][...], bbs[i][...], 0, 0)
-    up_ref[...] = total.astype(up_ref.dtype)
-    total = dot(acts[0][...], ups[0][...], 0, 0)
-    for i in range(1, count):
-        total = total + dot(acts[i][...], ups[i][...], 0, 0)
-    down_ref[...] = total.astype(down_ref.dtype)
-
-
-def expert_grad(rows, bbs, acts, ups, kind):
-    features, hidden = rows[0].shape[1], bbs[0].shape[1]
-    return pl.pallas_call(
-        functools.partial(expert_grad_kernel, len(rows)),
-        out_shape=(
-            jax.ShapeDtypeStruct((features, hidden), kind),
-            jax.ShapeDtypeStruct((hidden, features), kind),
-        ),
-        name="expert_grad",
-    )(*rows, *bbs, *acts, *ups)
+    hidden = w_ups[0][0].shape[1]
+    side = [like((rows.shape[0], hidden))] * count
+    out = tree_call(expert_kernel, (rows, upstream, w_ups, w_downs), (like(rows.shape), side, side))
+    return out[0], out[1 : 1 + count], out[1 + count :]
+
+
+def result_kernel(tree, *refs):
+    groups, w_downs, outs = jax.tree.unflatten(tree, refs)
+    w_downs = [joined(w_down) for w_down in w_downs]
+    for group, out_ref in zip(groups, outs):
+        start = 0
+        for acts in group:
+            total = dot(acts[0][...], w_downs[0], 1, 0)
+            for act, w_down in zip(acts[1:], w_downs[1:]):
+                total = total + dot(act[...], w_down, 1, 0)
+            out_ref[start : start + total.shape[0], :] = total.astype(BF)
+            start += total.shape[0]
+
+
+def result(groups, w_downs, shape):
+    return tree_call(result_kernel, (groups, w_downs), ([like(shape)] * len(groups),))
+
+
+def grad_kernel(tree, *refs):
+    lefts, rights, others, parts = jax.tree.unflatten(tree, refs)
+    total = None
+    for left, right in zip(lefts, rights):
+        part = dot(left[...], right[...], 0, 0)
+        total = part if total is None else total + part
+    size = total.shape[0] // len(parts)
+    for i, part_ref in enumerate(parts):
+        part_ref[...] = total[i * size : (i + 1) * size, :].astype(part_ref.dtype)
+    for other in others:
+        start = 0
+        for piece in other:
+            stop = start + piece.shape[0]
+            parts[0][start:stop, :] += piece[...].astype(F32)
+            start = stop
+
+
+def expert_grad(lefts, rights, kind, pieces=1, others=()):
+    shape = (lefts[0].shape[1] // pieces, rights[0].shape[1])
+    return tree_call(grad_kernel, (lefts, rights, list(others)), ([like(shape, kind)] * pieces,))
 
 
 def target(count, me, step):
@@ -656,38 +691,6 @@
     )
     came = [lax.ppermute(piece, ALL, pair) for piece, pair in zip(pieces, info.pairs)]
     gains = jnp.pad(jnp.concatenate([first_gain, second_gain]), (0, features - 2 * share))
-    gain_rows = gathered(gains[None], "seq", seq_steps)
-    scale_one = rms_scale(inputs)
-    xhats = gathered((inputs * scale_one).astype(BF), "seq", seq_steps)
-    padded = whole_tiles(share + n_seq) + whole_tiles(owned)
-    (weights,) = small_call(
-        functools.partial(place_kernel, info, n_seq, share),
-        info_row, (*came, exit_weight.T, *gain_rows),
-        [((padded, features), BF)], [((padded, features), F32)],
-    )
-    weights = gathered(weights, "dp", range(1, n_dp))
-    weights = [block for weight in weights for block in gathered(weight, "expert", range(1, n_ex))]
-    entry_t, gains, *exits = small_call(
-        functools.partial(arrange_kernel, info, n_dp, n_seq, n_ex, share, owned),
-        info_row, weights,
-        [((3 * width, features), BF), ((2, features), F32)]
-        + [((group_count, share, width), BF)] * n_seq,
-        [
-            ((group_count, padded, features), BF),
-            ((3 * width, features), F32),
-            ((n_seq, group_count, share, width), F32),
-        ],
-    )
-    gain_one, gain_two = gains[0:1], gains[1:2]
-    exits = exits[:1] + [shift(part, "seq", step) for part, step in zip(exits[1:], seq_steps)]
-
-    inner = 2 if n_seq > 1 and n_seq & (n_seq - 1) == 0 else 1
-    in_steps = tuple(range(1, inner))
-    out_steps = tuple(range(inner, n_seq, inner))
-    w_send = (expert_up[0], expert_down[0])
-    w_ups = gathered(w_send[0], "seq", out_steps)
-    w_downs = gathered(w_send[1], "seq", out_steps)
-
     group_size = n_dp * n_ex
     capacity = 3 * rows_here // group_size
     slots = group_size * capacity
@@ -711,8 +714,6 @@
         [(upstream * gates[:, k : k + 1]).astype(BF) for k in range(top_count)], axis=0
     )
     send_upstream = dot(place, gated, 1, 0).astype(BF)
-    came_upstream = exchanged(send_upstream.reshape(shaped), GROUP).reshape(slots, features)
-
     docs = documents.reshape(length)
     docs_row, docs_col = docs.reshape(1, length), docs.reshape(length, 1)
     lane = jnp.arange(length, dtype=jnp.int32)
@@ -720,29 +721,94 @@
     bias_here = lax.dynamic_slice_in_dim(position_bias.T, here * heads, heads)
     lag = jnp.dot(bias_here, hot, precision=HIGH)
     hot_back = bucket_hot(length - 1 - lane, buckets)
+    w_own = (expert_up[0], expert_down[0])
+    gain_rows = gathered(gains[None], "seq", seq_steps)
+    padded = whole_tiles(share + n_seq) + whole_tiles(owned, 8)
+    (weights,) = small_call(
+        functools.partial(place_kernel, info, n_seq, share),
+        info_row, (*came, exit_weight.T, *gain_rows),
+        [((padded, features), BF)], [((padded, features), F32)],
+    )
+    later, *w_later = after((inputs, *w_own), weights)
+    w_cut = [half for w in w_later for half in jnp.split(w, 2)]
+    scale_one = rms_scale(later)
+    xhats = gathered((later * scale_one).astype(BF), "seq", seq_steps)
+    weights = gathered(weights, "dp", range(1, n_dp))
+    weights = [block for weight in weights for block in gathered(weight, "expert", range(1, n_ex))]
+    entry_t, gains, *exits = small_call(
+        functools.partial(arrange_kernel, info, n_dp, n_seq, n_ex, share, owned),
+        info_row, weights,
+        [((3 * width, features), BF), ((2, features), F32)]
+        + [((group_count, share, width), BF)] * n_seq,
+        [
+            ((group_count, padded, features), BF),
+            ((3 * width, features), F32),
+            ((n_seq, group_count, share, width), F32),
+        ],
+    )
+    gain_one, gain_two = gains[0:1], gains[1:2]
+    exits = exits[:1] + [shift(part, "seq", step) for part, step in zip(exits[1:], seq_steps)]
+
+    inner = 2 if n_seq > 1 and n_seq & (n_seq - 1) == 0 else 1
+    in_steps = tuple(range(1, inner))
+    out_steps = tuple(range(inner, n_seq, inner))
+    w_ups, w_downs = [[w_own[0]]], [[w_own[1]]]
+    for step in out_steps:
+        cut = [shift(half, "seq", step) for half in w_cut]
+        w_ups.append(cut[:2])
+        w_downs.append(cut[2:])
+
+    came_upstream = exchanged(send_upstream.reshape(shaped), GROUP).reshape(slots, features)
+
     (lag,) = after((lag,), send_upstream)
     xfull, qkv, ctx, log = attend(
         info, heads, size, info_row, xhats, gains, entry_t, docs_row, docs_col, lag
     )
     exit_t, parts = leave(info, n_dp, n_seq, n_ex, info_row, ctx, exits)
 
-    hidden = inputs + summed(parts, "seq", seq_steps)
-    scale_two = rms_scale(hidden)
-    normed_two = (hidden * scale_two * gain_two).astype(BF)
-
-    send_rows = dot(place_any, normed_two, 1, 0).astype(BF)
-    ups = gathered(came_upstream, "seq", in_steps)
+    hidden, scale_two, send_rows = small_call(
+        norm_kernel,
+        info_row,
+        (inputs, gains, place_any, *traded(parts, "seq", seq_steps)),
+        [((rows_here, features), F32), ((rows_here, 1), F32), ((slots, features), BF)],
+        [],
+    )
+
     came_rows = exchanged(send_rows.reshape(shaped), GROUP).reshape(slots, features)
-    rows = gathered(came_rows, "seq", in_steps)
+    rows, ups = [came_rows], [came_upstream]
+    for step in in_steps:
+        for j in range(2):
+            part = slice(j * slots // 2, (j + 1) * slots // 2)
+            ups.append(shift(came_upstream[part], "seq", step))
+            rows.append(shift(came_rows[part], "seq", step))
     worked = []
-    for m in range(inner):
+    for m in range(1, len(rows)):
         worked.append(expert(rows[m], ups[m], w_ups, w_downs))
-    back_sum = handed_back([w[0] for w in worked], "seq", in_steps).astype(BF)
+    own = []
+    for j in range(len(w_ups)):
+        own.append(expert(rows[0], ups[0], w_ups[j : j + 1], w_downs[j : j + 1]))
+    back_sum = sum(o[0].astype(F32) for o in own)
+    for i, step in enumerate(in_steps):
+        parts = [shift(worked[2 * i + j][0], "seq", source(n_seq, 0, step)) for j in range(2)]
+        back_sum = back_sum + jnp.concatenate(parts).astype(F32)
+    back_sum = back_sum.astype(BF)
     returned_back = exchanged(back_sum.reshape(shaped), GROUP).reshape(slots, features)
-    grads = []
-    for j in range(n_seq // inner):
-        bbs, acts = [w[3][j] for w in worked], [w[2][j] for w in worked]
-        grads.append(expert_grad(rows, bbs, acts, ups, BF if j else F32))
+    own_acts = [o[1][0] for o in own]
+    own_bbs = [o[2][0] for o in own]
+    groups = [[own_acts]] + [
+        [worked[2 * i + j][1] for j in range(2)] for i in range(len(in_steps))
+    ]
+    results = result(groups, w_downs, came_rows.shape)
+    all_acts = [[own_acts[j]] + [w[1][j] for w in worked] for j in range(len(w_ups))]
+    all_bbs = [[own_bbs[j]] + [w[2][j] for w in worked] for j in range(len(w_ups))]
+    came_ups, came_downs = [], []
+    for i, step in enumerate(out_steps):
+        step = source(n_seq, 0, step)
+        part = expert_grad(rows, all_bbs[i + 1], BF, 2)
+        came_ups.append([shift(p, "seq", step) for p in part])
+        part = expert_grad(all_acts[i + 1], ups, BF, 2)
+        came_downs.append([shift(p, "seq", step) for p in part])
+
     back_normed_two = dot(place_any, returned_back, 0, 0)
     upper_two = back_normed_two * gain_two
     gain_two_grad = jnp.sum(back_normed_two * hidden * scale_two, axis=0, keepdims=True)
@@ -752,7 +818,6 @@
     )
     up_hiddens = gathered(back_hidden.astype(BF), "seq", seq_steps)
 
-    results = [w[1] for w in worked]
     out_sum = handed_back(results, "seq", in_steps).astype(BF)
     returned_out = exchanged(out_sum.reshape(shaped), GROUP).reshape(slots, features)
     block_output = hidden
@@ -764,54 +829,61 @@
         shift(part, "seq", step)
         for part, step in zip(exit_grads[1:], seq_steps)
     ]
-    diag, gain_one_grad, entry_grad, backs = attend_back(
-        info, heads, size, n_seq, info_row, up_full, exit_t, qkv, log, docs_row, docs_col, lag,
-        xfull, gains, entry_t,
-    )
-
-    count = 2 * share + buckets * heads
-    assert count <= width
-    padded = whole_tiles(share + 2) + whole_tiles(owned)
+    entry_grad, backs, smalls = attend_back(
+        info, heads, size, n_seq, n_dp, n_ex, share, info_row, up_full, exit_t, qkv, log,
+        docs_row, docs_col, lag, xfull, gains, entry_t, gain_two_grad, hot_back,
+    )
+
+    smalls = traded(smalls, "seq", seq_steps)
+    wide = -(-(2 * share + head_count * buckets) // 128) * 128
+    assert wide <= features and 2 * share + heads * buckets <= width
+    padded = whole_tiles(share + 2) + whole_tiles(owned, 8)
     halves = small_call(
         functools.partial(pack_kernel, info, n_dp, n_seq, n_ex, share, owned),
         info_row,
-        (*exit_grads, entry_grad, diag, gain_one_grad, gain_two_grad, hot_back),
+        (*exit_grads, entry_grad),
         [((n_dp, padded, features), BF)] * n_ex,
         [
             ((n_seq, n_dp, n_ex * share, width), F32),
-            ((8, features), F32),
             ((n_ex, n_dp, padded, features), F32),
         ],
     )
     halves = traded(halves, "expert", range(1, n_ex))
+    smalls = small_call(
+        functools.partial(small_kernel, info, n_dp, n_seq, n_ex, share, heads, buckets),
+        info_row,
+        smalls,
+        [((n_dp, wide), F32)] * n_ex,
+        [((n_seq, n_ex * n_dp, width), F32), ((n_ex, n_dp, wide), F32)],
+    )
+    smalls = traded(smalls, "expert", range(1, n_ex))
     quarters = small_call(
         functools.partial(fold_kernel, info, n_dp, n_ex, share),
-        info_row, halves, [((padded, features), BF)] * n_dp,
+        info_row,
+        (*halves, *smalls),
+        [((padded, features), BF)] * n_dp,
         [((n_dp, padded, features), F32)],
     )
+    folded = quarters
     quarters = traded(quarters, "dp", range(1, n_dp))
-    exit_share, *rest = small_call(
-        functools.partial(finish_kernel, info, n_dp, n_seq, share),
-        info_row, quarters,
-        [((share, features), F32)]
-        + [((chunk, features), F32)] * per
-        + [((1, width), F32)] * n_seq,
-        [((n_seq, 1, width), F32)],
-    )
-    pieces, small = rest[:per], rest[per:]
+    exit_share, small, *pieces = small_call(
+        functools.partial(finish_kernel, info, n_dp, share),
+        info_row,
+        quarters,
+        [((share, features), F32), ((1, wide), F32)] + [((chunk, features), F32)] * per,
+        [],
+    )
     came = [
         lax.ppermute(piece, ALL, tuple((b, a) for a, b in pair))
         for piece, pair in zip(pieces, info.pairs)
     ]
-    small = traded(small, "seq", seq_steps)
-    entry_share, gain_shares, bias_total = small_call(
-        functools.partial(close_kernel, info, n_seq, share, heads),
-        info_row, (*came, *small),
-        [((owned, features), F32), ((2, share), F32), ((head_count, buckets), F32)],
-        [((n_seq, 1, width), F32)],
-    )
-    entry_share, exit_share, bias_total = entry_share.T, exit_share.T, bias_total.T
-    gain_one_share, gain_two_share = gain_shares[0], gain_shares[1]
+    (entry_share,) = small_call(
+        functools.partial(close_kernel, info), info_row, came, [((owned, features), F32)], []
+    )
+    entry_share, exit_share = entry_share.T, exit_share.T
+    small = small[0]
+    gain_one_share, gain_two_share = small[:share], small[share : 2 * share]
+    bias_total = small[2 * share : 2 * share + head_count * buckets].reshape(head_count, buckets).T
 
     back_normed_one = summed(backs, "seq", seq_steps)
     upper_one = back_normed_one * gain_one
@@ -820,12 +892,9 @@
         - inputs * scale_one * scale_one * jnp.mean(upper_one * inputs, axis=1, keepdims=True)
     )
 
-    (own_up, own_down), *others = grads
-    own_up, own_down = after((own_up, own_down), gain_one_grad)
-    grads = [(own_up, own_down), *others]
-    up_grad = handed_back([g[0] for g in grads], "seq", out_steps)
-    down_grad = handed_back([g[1] for g in grads], "seq", out_steps)
-
+    own_bb, own_act = after((all_bbs[0][0], all_acts[0][0]), folded)
+    (up_grad,) = expert_grad(rows, [own_bb] + all_bbs[0][1:], F32, 1, came_ups)
+    (down_grad,) = expert_grad([own_act] + all_acts[0][1:], ups, F32, 1, came_downs)
     return (
         block_output.reshape(block_input.shape),
         back_input.reshape(block_input.shape),

time: 310 us -> 359 us (1.16)
  waiting for transfers between devices: 118 us -> 140 us
  Pallas kernels: 66 us -> 84.7 us
  starting transfers between devices: 83.6 us -> 93.8 us
  other arithmetic: 18.4 us -> 9.81 us
  local copies, waits for them, and re-layouts: 12.5 us -> 19.9 us
    ppermute x43 -> x51, waiting for transfers between devices: 104 us -> 133 us  [shift(): lax.ppermute(array, axis, tuple(((i, target(count, i, step)) for i in ran...]
    pallas_call x4 -> x9, Pallas kernels: 28.5 us -> 42.5 us  [tree_call(): pl.pallas_call(functools.partial(kernel, tree), out_shape=tuple(jax.tree....]
    ppermute x43 -> x51, starting transfers between devices: 43.2 us -> 53.8 us  [shift(): lax.ppermute(array, axis, tuple(((i, target(count, i, step)) for i in ran...]
    broadcast_in_dim x2 -> x0, other arithmetic: 6.24 us -> none  [the longest x1 3.19 us: local(): up_grad[None]]
    all_to_all x4, waiting for transfers between devices: 10.7 us -> 5.2 us  [exchanged(): return lax.all_to_all(array, axis, 0, 0, tiled=True)]
    pallas_call x11 -> x13, Pallas kernels: 37.6 us -> 42.2 us  [small_call(): pl.pallas_call(kernel, in_specs=specs(len(arrays)), out_shape=tuple((jax....]
    slice x0 -> x4, local copies, waits for them, and re-layouts: none -> 3.77 us  [the longest x1 1.31 us: local(): gain_one_share, gain_two_share = (small[:share], small[share:2 * share])]
    unnamed x120 -> x146, local copies, waits for them, and re-layouts: 7.76 us -> 9.76 us
  transfers between devices with their start and end apart: 53 -> 61, of which waited for: 19 -> 23; matrix products, arithmetic and copies ran while one was open for 8% -> 6% of each run, Pallas kernels for 18% -> 23%
where the time goes in v3:
time: 359 us; the launch traced here: 354 us
  waiting for transfers between devices  140 us (39%)
  starting transfers between devices  93.8 us (26%)
  Pallas kernels  84.7 us (24%)
  local copies, waits for them, and re-layouts  19.9 us (6%)
  other arithmetic  9.81 us (3%)
  matrix products  4.65 us (1%)
    ppermute x51, waiting for transfers between devices, shift(): lax.ppermute(array, axis, tuple(((i, target(count, i, step)) for i in ran...  133 us
    ppermute x51, starting transfers between devices, shift(): lax.ppermute(array, axis, tuple(((i, target(count, i, step)) for i in ran...  53.8 us
    pallas_call x9, Pallas kernels, tree_call(): pl.pallas_call(functools.partial(kernel, tree), out_shape=tuple(jax.tree....  42.5 us
    pallas_call x13, Pallas kernels, small_call(): pl.pallas_call(kernel, in_specs=specs(len(arrays)), out_shape=tuple((jax....  42.2 us
    all_to_all x4, starting transfers between devices, exchanged(): return lax.all_to_all(array, axis, 0, 0, tiled=True)  19.5 us
    ppermute x3, starting transfers between devices, local(): lax.ppermute(piece, ALL, tuple(((b, a) for a, b in pair)))  10.5 us
    ppermute x3, starting transfers between devices, local(): lax.ppermute(piece, ALL, pair)  9.96 us
    unnamed x146, local copies, waits for them, and re-layouts  9.76 us
  transfers between devices with their start and end apart: 61, of which 23 were waited for; matrix products, arithmetic and copies ran while one was open for 6% of the time, Pallas kernels for 23%

profile of v3, /device:TPU:18, one launch (start us, length us, event | category | flops | bytes accessed | tf_op | source)
XLA Modules:
  0.0 353.9 jit_solution(16940854607358034950)
XLA Ops:
  14.6 6.0 %collective-permute-start.2 = (bf16[24,768]{1,0:T(8,128)(2,1)}, bf16[24,768]{1,0:T(8,128)(2,1)S(1)}, u32[]{:S(2)}, u32[]{:S(2)}) collective-permute-start(bf16[24,768]{1,0:T(8,128)(2,1)} %get-tuple-element.87), channel_id=1, source_target_pairs={{0,0},{1,8},{2,2},{3,10},{4,18},{5,4},{6,12},{7,20},{8,6},{9,14},{... | collective-permute-start | bytes 110600 | tf_op jit(solution)/shard_map/ppermute | solution.py:692
  21.8 4.8 %all-to-all-start.1 = ((bf16[8,48,768]{2,1,0:T(8,128)(2,1)}), bf16[8,48,768]{2,1,0:T(8,128)(2,1)S(1)}, u32[]{:S(2)}, u32[]{:S(2)}) async-start(bf16[8,48,768]{2,1,0:T(8,128)(2,1)} %bitcast.16), calls=%async_computation.1 | async-start | bytes 1179648 | tf_op jit(solution)/shard_map/all_to_all | solution.py:631
  33.1 9.6 %collective-permute-done.7.refs_2_ = bf16[104,768]{1,0:T(8,128)(2,1)S(1)} collective-permute-done((bf16[104,768]{1,0:T(8,128)(2,1)}, bf16[104,768]{1,0:T(8,128)(2,1)S(1)}, u32[]{:S(2)}, u32[]{:S(2)}) %collective-permute-start.7) | collective-permute-done | bytes 159776 | tf_op jit(solution)/shard_map/ppermute | solution.py:623
  42.7 8.1 %collective-permute-done.9.refs_4_ = bf16[104,768]{1,0:T(8,128)(2,1)S(1)} collective-permute-done((bf16[104,768]{1,0:T(8,128)(2,1)}, bf16[104,768]{1,0:T(8,128)(2,1)S(1)}, u32[]{:S(2)}, u32[]{:S(2)}) %collective-permute-start.9) | collective-permute-done | bytes 159776 | tf_op jit(solution)/shard_map/ppermute | solution.py:623
  68.1 7.2 %shard_map.199 = (bf16[512,768]{1,0:T(8,128)(2,1)}, bf16[512,576]{1,0:T(8,128)(2,1)}, bf16[512,192]{1,0:T(8,128)(2,1)}, f32[512,3]{1,0:T(8,128)}) custom-call(s32[32]{0:T(128)} %dynamic-slice_bitcast_fusion.row_ref, bf16[128,768]{1,0:T(8,128)(2,1)} %copy-done.15, bf16[128,768]{1,0:T(8,128)(2,1)} %copy-done.23, bf16[128,768]{1,0:T(8,128)(2,1)} %copy-done.24, ...), custom_call_target="tpu_custom_call" | custom-call | tf_op jit(solution)/shard_map/pallas_call | solution.py:142
  93.2 4.4 %all-to-all-start = ((bf16[8,48,768]{2,1,0:T(8,128)(2,1)}), bf16[8,48,768]{2,1,0:T(8,128)(2,1)S(1)}, u32[]{:S(2)}, u32[]{:S(2)}) async-start(bf16[8,48,768]{2,1,0:T(8,128)(2,1)} %bitcast.83), calls=%async_computation | async-start | bytes 1179648 | tf_op jit(solution)/shard_map/all_to_all | solution.py:631
  105.8 5.2 %all-to-all-done = bf16[8,48,768]{2,1,0:T(8,128)(2,1)S(1)} async-done(((bf16[8,48,768]{2,1,0:T(8,128)(2,1)}), bf16[8,48,768]{2,1,0:T(8,128)(2,1)S(1)}, u32[]{:S(2)}, u32[]{:S(2)}) %all-to-all-start) | async-done | bytes 589856 | tf_op jit(solution)/shard_map/all_to_all | solution.py:631
  116.2 11.6 %collective-permute-done.23.refs_3_.refs_4_ = bf16[384,768]{1,0:T(8,128)(2,1)S(1)} collective-permute-done((bf16[384,768]{1,0:T(8,128)(2,1)}, bf16[384,768]{1,0:T(8,128)(2,1)S(1)}, u32[]{:S(2)}, u32[]{:S(2)}) %collective-permute-start.23) | collective-permute-done | bytes 589856 | tf_op jit(solution)/shard_map/ppermute | solution.py:623
  128.8 11.6 %collective-permute-done.24.refs_4_.refs_6_.refs_7_ = bf16[384,768]{1,0:T(8,128)(2,1)S(1)} collective-permute-done((bf16[384,768]{1,0:T(8,128)(2,1)}, bf16[384,768]{1,0:T(8,128)(2,1)S(1)}, u32[]{:S(2)}, u32[]{:S(2)}) %collective-permute-start.24) | collective-permute-done | bytes 589856 | tf_op jit(solution)/shard_map/ppermute | solution.py:623
  141.4 11.1 %collective-permute-done.25.refs_5_.refs_7_.refs_8_ = bf16[384,768]{1,0:T(8,128)(2,1)S(1)} collective-permute-done((bf16[384,768]{1,0:T(8,128)(2,1)}, bf16[384,768]{1,0:T(8,128)(2,1)S(1)}, u32[]{:S(2)}, u32[]{:S(2)}) %collective-permute-start.25) | collective-permute-done | bytes 589856 | tf_op jit(solution)/shard_map/ppermute | solution.py:623
  154.0 5.4 %shard_map.205 = (bf16[192,768]{1,0:T(8,128)(2,1)}, bf16[192,768]{1,0:T(8,128)(2,1)}, bf16[192,768]{1,0:T(8,128)(2,1)}, bf16[192,768]{1,0:T(8,128)(2,1)}, bf16[192,768]{1,0:T(8,128)(2,1)}) custom-call(bf16[192,768]{1,0:T(8,128)(2,1)} %copy-done.12, bf16[192,768]{1,0:T(8,128)(2,1)} %collective-permute-done.29.refs_1_.refs_5_, bf16[768,768]{1,0:T(8,128)(2,1)} %bitcast.71, ...), custom_call_target="tpu_custom_call" | custom-call | tf_op jit(solution)/shard_map/pallas_call | solution.py:557
  160.5 5.4 %shard_map.204 = (bf16[192,768]{1,0:T(8,128)(2,1)}, bf16[192,768]{1,0:T(8,128)(2,1)}, bf16[192,768]{1,0:T(8,128)(2,1)}, bf16[192,768]{1,0:T(8,128)(2,1)}, bf16[192,768]{1,0:T(8,128)(2,1)}) custom-call(bf16[192,768]{1,0:T(8,128)(2,1)} %collective-permute-done.26.refs_0_.refs_1_, bf16[192,768]{1,0:T(8,128)(2,1)} %collective-permute-done.27.refs_1_.refs_4_, ...), custom_call_target="tpu_custom_call" | custom-call | tf_op jit(solution)/shard_map/pallas_call | solution.py:557
  167.0 4.5 %shard_map.202 = (bf16[384,768]{1,0:T(8,128)(2,1)}, bf16[384,768]{1,0:T(8,128)(2,1)}, bf16[384,768]{1,0:T(8,128)(2,1)}) custom-call(bf16[384,768]{1,0:T(8,128)(2,1)} %bitcast.67, bf16[384,768]{1,0:T(8,128)(2,1)} %bitcast.63, bf16[768,768]{1,0:T(8,128)(2,1)} %bitcast.73, bf16[768,768]{1,0:T(8,128)(2,1)} %bitcast.60), custom_call_target="tpu_custom_call" | custom-call | tf_op jit(solution)/shard_map/pallas_call | solution.py:557
  171.5 4.5 %shard_map.203 = (bf16[384,768]{1,0:T(8,128)(2,1)}, bf16[384,768]{1,0:T(8,128)(2,1)}, bf16[384,768]{1,0:T(8,128)(2,1)}) custom-call(bf16[384,768]{1,0:T(8,128)(2,1)} %bitcast.68, bf16[384,768]{1,0:T(8,128)(2,1)} %bitcast.64, bf16[384,768]{1,0:T(8,128)(2,1)} %copy-done.9, bf16[384,768]{1,0:T(8,128)(2,1)} %copy-done.10, bf16[384,768]{1,0:T(8,128)(2,1)} %copy-done.7, ...), custom_call_target="tpu_custom_call" | custom-call | tf_op jit(solution)/shard_map/pallas_call | solution.py:557
  178.2 5.1 %all-to-all-start.3 = ((bf16[8,48,768]{2,1,0:T(8,128)(2,1)}), bf16[8,48,768]{2,1,0:T(8,128)(2,1)S(1)}, u32[]{:S(2)}, u32[]{:S(2)}) async-start(bf16[8,48,768]{2,1,0:T(8,128)(2,1)} %bitcast.25), calls=%async_computation.3 | async-start | bytes 1179648 | tf_op jit(solution)/shard_map/all_to_all | solution.py:631
  183.3 5.2 %shard_map.206 = (bf16[384,768]{1,0:T(8,128)(2,1)}, bf16[384,768]{1,0:T(8,128)(2,1)}) custom-call(bf16[384,768]{1,0:T(8,128)(2,1)} %get-tuple-element.158.refs_0_, bf16[384,768]{1,0:T(8,128)(2,1)} %get-tuple-element.106.refs_1_.refs_0_, bf16[192,768]{1,0:T(8,128)(2,1)} %get-tuple-element.107.refs_2_.refs_1_, ...), custom_call_target="tpu_custom_call" | custom-call | tf_op jit(solution)/shard_map/pallas_call | solution.py:557
  189.5 14.5 %collective-permute-done.30 = bf16[384,768]{1,0:T(8,128)(2,1)S(1)} collective-permute-done((bf16[384,768]{1,0:T(8,128)(2,1)}, bf16[384,768]{1,0:T(8,128)(2,1)S(1)}, u32[]{:S(2)}, u32[]{:S(2)}) %collective-permute-start.30) | collective-permute-done | bytes 589856 | tf_op jit(solution)/shard_map/ppermute | solution.py:623
  206.1 5.2 %all-to-all-start.2 = ((bf16[8,48,768]{2,1,0:T(8,128)(2,1)}), bf16[8,48,768]{2,1,0:T(8,128)(2,1)S(1)}, u32[]{:S(2)}, u32[]{:S(2)}) async-start(bf16[8,48,768]{2,1,0:T(8,128)(2,1)} %bitcast.22), calls=%async_computation.2 | async-start | bytes 1179648 | tf_op jit(solution)/shard_map/all_to_all | solution.py:631
  227.6 10.8 %shard_map.208 = (bf16[576,768]{1,0:T(8,128)(2,1)}, bf16[128,768]{1,0:T(8,128)(2,1)}, bf16[128,768]{1,0:T(8,128)(2,1)}, bf16[128,768]{1,0:T(8,128)(2,1)}, bf16[1...) custom-call(s32[32]{0:T(128)} %dynamic-slice_bitcast_fusion.row_ref, ...), custom_call_target="tpu_custom_call" | custom-call | tf_op jit(solution)/shard_map/pallas_call | solution.py:142
  259.6 4.0 %shard_map.216 = (bf16[384,768]{1,0:T(8,128)(2,1)}, bf16[384,768]{1,0:T(8,128)(2,1)}) custom-call(bf16[384,768]{1,0:T(8,128)(2,1)} %get-tuple-element.106.refs_1_.refs_0_, bf16[192,768]{1,0:T(8,128)(2,1)} %get-tuple-element.108.refs_3_.refs_1_, bf16[192,768]{1,0:T(8,128)(2,1)} %get-tuple-element.110.refs_5_.refs_2_, bf16[384,768]{1,0:T(8,128)(2,1)} %bitcast.65, ...), custom_call_target="tpu_custom_call" | custom-call | tf_op jit(solution)/shard_map/pallas_call | solution.py:557
  276.7 23.7 %collective-permute-done.37 = bf16[128,768]{1,0:T(8,128)(2,1)S(1)} collective-permute-done((bf16[128,768]{1,0:T(8,128)(2,1)}, bf16[128,768]{1,0:T(8,128)(2,1)S(1)}, u32[]{:S(2)}, u32[]{:S(2)}) %collective-permute-start.37) | collective-permute-done | bytes 196640 | tf_op jit(solution)/shard_map/ppermute | solution.py:623
  310.6 4.8 %shard_map.217 = f32[768,768]{1,0:T(8,128)} custom-call(bf16[384,768]{1,0:T(8,128)(2,1)} %get-tuple-element.158.refs_0_, bf16[192,768]{1,0:T(8,128)(2,1)} %get-tuple-element.107.refs_2_.refs_1_, bf16[192,768]{1,0:T(8,128)(2,1)} %get-tuple-element.109.refs_4_.refs_2_, bf16[384,768]{1,0:T(8,128)(2,1)} %bitcast.66, ...), custom_call_target="tpu_custom_call" | custom-call | tf_op jit(solution)/shard_map/pallas_call | solution.py:557
  316.9 11.4 %collective-permute-done.54.refs_7_ = bf16[384,768]{1,0:T(8,128)(2,1)} collective-permute-done((bf16[384,768]{1,0:T(8,128)(2,1)}, bf16[384,768]{1,0:T(8,128)(2,1)}, u32[]{:S(2)}, u32[]{:S(2)}) %collective-permute-start.54) | collective-permute-done | bytes 589856 | tf_op jit(solution)/shard_map/ppermute | solution.py:623
  328.3 4.8 %shard_map.215 = f32[768,768]{1,0:T(8,128)} custom-call(bf16[384,768]{1,0:T(8,128)(2,1)} %bitcast.70, bf16[192,768]{1,0:T(8,128)(2,1)} %collective-permute-done.26.refs_0_.refs_1_, bf16[192,768]{1,0:T(8,128)(2,1)} %copy-done.12, bf16[384,768]{1,0:T(8,128)(2,1)} %get-tuple-element.150.refs_3_, bf16[192,768]{1,0:T(8,128)(2,1)} %get-tuple-element.151.refs_4_, ...), custom_call_target="tpu_custom_call" | custom-call | tf_op jit(solution)/shard_map/pallas_call | solution.py:557
  (305 shorter events, 163.6 us)
Async XLA Ops:
  21.8 71.4 %all-to-all-start.1 = ((bf16[8,48,768]{2,1,0:T(8,128)(2,1)}), bf16[8,48,768]{2,1,0:T(8,128)(2,1)S(1)}, u32[]{:S(2)}, u32[]{:S(2)}) async-start(bf16[8,48,768]{2,1,0:T(8,128)(2,1)} %bitcast.16), calls=%async_computation.1 | async-start | bytes 1179648 | tf_op jit(solution)/shard_map/all_to_all | solution.py:631
  28.8 26.5 %collective-permute-start.6 = (bf16[104,768]{1,0:T(8,128)(2,1)}, bf16[104,768]{1,0:T(8,128)(2,1)S(1)}, u32[]{:S(2)}, u32[]{:S(2)}) collective-permute-start(bf16[104,768]{1,0:T(8,128)(2,1)} %shard_map.197.refs_0_), channel_id=1, source_target_pairs={{0,1},{1,0},{2,3},{3,2},{4,5},{5,4},{6,7},{7,6},{8,9},{9,8},{10,11... | collective-permute-start | bytes 479240 | tf_op jit(solution)/shard_map/ppermute | solution.py:623
  32.6 31.6 %collective-permute-start.13 = (bf16[128,768]{1,0:T(8,128)(2,1)S(1)}, bf16[128,768]{1,0:T(8,128)(2,1)S(1)}, u32[]{:S(2)}, u32[]{:S(2)}) collective-permute-start(bf16[128,768]{1,0:T(8,128)(2,1)S(1)} %multiply_convert_fusion.refs_0_), channel_id=1, source_target_pairs={{0,2},{2,0},{4,6},{6,4},{1,3},{3,1},{5,7},{7,5},{8,10},{10,8},{12,... | collective-permute-start | bytes 589832 | tf_op jit(solution)/shard_map/ppermute | solution.py:623
  100.8 27.0 %collective-permute-start.23 = (bf16[384,768]{1,0:T(8,128)(2,1)}, bf16[384,768]{1,0:T(8,128)(2,1)S(1)}, u32[]{:S(2)}, u32[]{:S(2)}) collective-permute-start(bf16[384,768]{1,0:T(8,128)(2,1)} %get-tuple-element.169), channel_id=1, source_target_pairs={{0,4},{2,6},{4,0},{6,2},{1,5},{3,7},{5,1},{7,3},{8,12},{10,14},{12... | collective-permute-start | bytes 1769480 | tf_op jit(solution)/shard_map/ppermute | solution.py:623
  101.9 38.5 %collective-permute-start.24 = (bf16[384,768]{1,0:T(8,128)(2,1)}, bf16[384,768]{1,0:T(8,128)(2,1)S(1)}, u32[]{:S(2)}, u32[]{:S(2)}) collective-permute-start(bf16[384,768]{1,0:T(8,128)(2,1)} %get-tuple-element.168), channel_id=1, source_target_pairs={{0,4},{2,6},{4,0},{6,2},{1,5},{3,7},{5,1},{7,3},{8,12},{10,14},{12... | collective-permute-start | bytes 1769480 | tf_op jit(solution)/shard_map/ppermute | solution.py:623
  103.9 48.6 %collective-permute-start.25 = (bf16[384,768]{1,0:T(8,128)(2,1)}, bf16[384,768]{1,0:T(8,128)(2,1)S(1)}, u32[]{:S(2)}, u32[]{:S(2)}) collective-permute-start(bf16[384,768]{1,0:T(8,128)(2,1)} %get-tuple-element.167), channel_id=1, source_target_pairs={{0,4},{2,6},{4,0},{6,2},{1,5},{3,7},{5,1},{7,3},{8,12},{10,14},{12... | collective-permute-start | bytes 1769480 | tf_op jit(solution)/shard_map/ppermute | solution.py:623
  104.9 47.7 %collective-permute-start.29 = (bf16[192,768]{1,0:T(8,128)(2,1)}, bf16[192,768]{1,0:T(8,128)(2,1)}, u32[]{:S(2)}, u32[]{:S(2)}) collective-permute-start(bf16[192,768]{1,0:T(8,128)(2,1)} %bitcast.21), channel_id=1, source_target_pairs={{0,2},{2,0},{4,6},{6,4},{1,3},{3,1},{5,7},{7,5},{8,10},{10,8},{12,... | collective-permute-start | bytes 884744 | tf_op jit(solution)/shard_map/ppermute | solution.py:623
  115.2 37.4 %collective-permute-start.28 = (bf16[192,768]{1,0:T(8,128)(2,1)S(1)}, bf16[192,768]{1,0:T(8,128)(2,1)S(1)}, u32[]{:S(2)}, u32[]{:S(2)}) collective-permute-start(bf16[192,768]{1,0:T(8,128)(2,1)S(1)} %bitcast.85), channel_id=1, source_target_pairs={{0,2},{2,0},{4,6},{6,4},{1,3},{3,1},{5,7},{7,5},{8,10},{10,8},{12,... | collective-permute-start | bytes 884744 | tf_op jit(solution)/shard_map/ppermute | solution.py:623
  127.8 32.7 %collective-permute-start.27 = (bf16[192,768]{1,0:T(8,128)(2,1)S(1)}, bf16[192,768]{1,0:T(8,128)(2,1)}, u32[]{:S(2)}, u32[]{:S(2)}) collective-permute-start(bf16[192,768]{1,0:T(8,128)(2,1)S(1)} %bitcast.84), channel_id=1, source_target_pairs={{0,2},{2,0},{4,6},{6,4},{1,3},{3,1},{5,7},{7,5},{8,10},{10,8},{12,... | collective-permute-start | bytes 884744 | tf_op jit(solution)/shard_map/ppermute | solution.py:623
  178.2 27.9 %all-to-all-start.3 = ((bf16[8,48,768]{2,1,0:T(8,128)(2,1)}), bf16[8,48,768]{2,1,0:T(8,128)(2,1)S(1)}, u32[]{:S(2)}, u32[]{:S(2)}) async-start(bf16[8,48,768]{2,1,0:T(8,128)(2,1)} %bitcast.25), calls=%async_computation.3 | async-start | bytes 1179648 | tf_op jit(solution)/shard_map/all_to_all | solution.py:631
  206.1 69.2 %all-to-all-start.2 = ((bf16[8,48,768]{2,1,0:T(8,128)(2,1)}), bf16[8,48,768]{2,1,0:T(8,128)(2,1)S(1)}, u32[]{:S(2)}, u32[]{:S(2)}) async-start(bf16[8,48,768]{2,1,0:T(8,128)(2,1)} %bitcast.22), calls=%async_computation.2 | async-start | bytes 1179648 | tf_op jit(solution)/shard_map/all_to_all | solution.py:631
  238.4 36.8 %collective-permute-start.38 = (bf16[128,768]{1,0:T(8,128)(2,1)}, bf16[128,768]{1,0:T(8,128)(2,1)S(1)}, u32[]{:S(2)}, u32[]{:S(2)}) collective-permute-start(bf16[128,768]{1,0:T(8,128)(2,1)} %get-tuple-element.126), channel_id=1, source_target_pairs={{0,6},{2,4},{4,2},{6,0},{1,7},{3,5},{5,3},{7,1},{8,14},{10,12},{12... | collective-permute-start | bytes 589832 | tf_op jit(solution)/shard_map/ppermute | solution.py:623
  240.9 26.7 %collective-permute-start.39 = (bf16[4,48,192]{2,1,0:T(8,128)(2,1)S(1)}, bf16[4,48,192]{2,1,0:T(8,128)(2,1)S(1)}, u32[]{:S(2)}, u32[]{:S(2)}) collective-permute-start(bf16[4,48,192]{2,1,0:T(8,128)(2,1)S(1)} %copy-done.72), channel_id=1, source_target_pairs={{0,2},{2,0},{4,6},{6,4},{1,3},{3,1},{5,7},{7,5},{8,10},{10,8},{12,... | collective-permute-start | bytes 221192 | tf_op jit(solution)/shard_map/ppermute | solution.py:623
  241.8 27.6 %collective-permute-start.40 = (bf16[4,48,192]{2,1,0:T(8,128)(2,1)S(1)}, bf16[4,48,192]{2,1,0:T(8,128)(2,1)S(1)}, u32[]{:S(2)}, u32[]{:S(2)}) collective-permute-start(bf16[4,48,192]{2,1,0:T(8,128)(2,1)S(1)} %copy-done.71), channel_id=1, source_target_pairs={{0,4},{2,6},{4,0},{6,2},{1,5},{3,7},{5,1},{7,3},{8,12},{10,14},{12... | collective-permute-start | bytes 221192 | tf_op jit(solution)/shard_map/ppermute | solution.py:623
  242.0 27.7 %collective-permute-start.41 = (bf16[4,48,192]{2,1,0:T(8,128)(2,1)S(1)}, bf16[4,48,192]{2,1,0:T(8,128)(2,1)S(1)}, u32[]{:S(2)}, u32[]{:S(2)}) collective-permute-start(bf16[4,48,192]{2,1,0:T(8,128)(2,1)S(1)} %copy-done.70), channel_id=1, source_target_pairs={{0,6},{2,4},{4,2},{6,0},{1,7},{3,5},{5,3},{7,1},{8,14},{10,12},{12... | collective-permute-start | bytes 221192 | tf_op jit(solution)/shard_map/ppermute | solution.py:623
  267.6 40.0 %collective-permute-start.55 = (bf16[384,768]{1,0:T(8,128)(2,1)}, bf16[384,768]{1,0:T(8,128)(2,1)}, u32[]{:S(2)}, u32[]{:S(2)}) collective-permute-start(bf16[384,768]{1,0:T(8,128)(2,1)} %get-tuple-element.159), channel_id=1, source_target_pairs={{0,4},{2,6},{4,0},{6,2},{1,5},{3,7},{5,1},{7,3},{8,12},{10,14},{12... | collective-permute-start | bytes 1769480 | tf_op jit(solution)/shard_map/ppermute | solution.py:623
  269.4 38.9 %collective-permute-start.56 = (bf16[384,768]{1,0:T(8,128)(2,1)}, bf16[384,768]{1,0:T(8,128)(2,1)}, u32[]{:S(2)}, u32[]{:S(2)}) collective-permute-start(bf16[384,768]{1,0:T(8,128)(2,1)} %get-tuple-element.160), channel_id=1, source_target_pairs={{0,4},{2,6},{4,0},{6,2},{1,5},{3,7},{5,1},{7,3},{8,12},{10,14},{12... | collective-permute-start | bytes 1769480 | tf_op jit(solution)/shard_map/ppermute | solution.py:623
  269.7 30.8 %collective-permute-start.37 = (bf16[128,768]{1,0:T(8,128)(2,1)}, bf16[128,768]{1,0:T(8,128)(2,1)S(1)}, u32[]{:S(2)}, u32[]{:S(2)}) collective-permute-start(bf16[128,768]{1,0:T(8,128)(2,1)} %get-tuple-element.125), channel_id=1, source_target_pairs={{0,4},{2,6},{4,0},{6,2},{1,5},{3,7},{5,1},{7,3},{8,12},{10,14},{12... | collective-permute-start | bytes 589832 | tf_op jit(solution)/shard_map/ppermute | solution.py:623
  274.3 27.9 %collective-permute-start.36 = (bf16[128,768]{1,0:T(8,128)(2,1)S(1)}, bf16[128,768]{1,0:T(8,128)(2,1)S(1)}, u32[]{:S(2)}, u32[]{:S(2)}) collective-permute-start(bf16[128,768]{1,0:T(8,128)(2,1)S(1)} %copy-done.69), channel_id=1, source_target_pairs={{0,2},{2,0},{4,6},{6,4},{1,3},{3,1},{5,7},{7,5},{8,10},{10,8},{12,... | collective-permute-start | bytes 589832 | tf_op jit(solution)/shard_map/ppermute | solution.py:623
  275.3 27.5 %collective-permute-start.42 = (bf16[4,104,768]{2,1,0:T(8,128)(2,1)}, bf16[4,104,768]{2,1,0:T(8,128)(2,1)S(1)}, u32[]{:S(2)}, u32[]{:S(2)}) collective-permute-start(bf16[4,104,768]{2,1,0:T(8,128)(2,1)} %get-tuple-element.133), channel_id=1, source_target_pairs={{0,1},{1,0},{2,3},{3,2},{4,5},{5,4},{6,7},{7,6},{8,9},{9,8},{10,11... | collective-permute-start | bytes 1916936 | tf_op jit(solution)/shard_map/ppermute | solution.py:623
  302.2 26.1 %collective-permute-start.54 = (bf16[384,768]{1,0:T(8,128)(2,1)}, bf16[384,768]{1,0:T(8,128)(2,1)}, u32[]{:S(2)}, u32[]{:S(2)}) collective-permute-start(bf16[384,768]{1,0:T(8,128)(2,1)} %get-tuple-element.157), channel_id=1, source_target_pairs={{0,4},{2,6},{4,0},{6,2},{1,5},{3,7},{5,1},{7,3},{8,12},{10,14},{12... | collective-permute-start | bytes 1769480 | tf_op jit(solution)/shard_map/ppermute | solution.py:623
  306.1 27.0 %collective-permute-start.47 = (bf16[104,768]{1,0:T(8,128)(2,1)}, bf16[104,768]{1,0:T(8,128)(2,1)S(1)}, u32[]{:S(2)}, u32[]{:S(2)}) collective-permute-start(bf16[104,768]{1,0:T(8,128)(2,1)} %get-tuple-element.141), channel_id=1, source_target_pairs={{0,8},{8,0},{16,24},{24,16},{1,9},{9,1},{17,25},{25,17},{2,10},{10... | collective-permute-start | bytes 479240 | tf_op jit(solution)/shard_map/ppermute | solution.py:623
  307.6 25.5 %collective-permute-start.48 = (bf16[104,768]{1,0:T(8,128)(2,1)}, bf16[104,768]{1,0:T(8,128)(2,1)S(1)}, u32[]{:S(2)}, u32[]{:S(2)}) collective-permute-start(bf16[104,768]{1,0:T(8,128)(2,1)} %get-tuple-element.142), channel_id=1, source_target_pairs={{0,16},{8,24},{16,0},{24,8},{1,17},{9,25},{17,1},{25,9},{2,18},{10... | collective-permute-start | bytes 479240 | tf_op jit(solution)/shard_map/ppermute | solution.py:623
  308.3 24.9 %collective-permute-start.49 = (bf16[104,768]{1,0:T(8,128)(2,1)}, bf16[104,768]{1,0:T(8,128)(2,1)S(1)}, u32[]{:S(2)}, u32[]{:S(2)}) collective-permute-start(bf16[104,768]{1,0:T(8,128)(2,1)} %get-tuple-element.143), channel_id=1, source_target_pairs={{0,24},{8,16},{16,8},{24,0},{1,25},{9,17},{17,9},{25,1},{2,26},{10... | collective-permute-start | bytes 479240 | tf_op jit(solution)/shard_map/ppermute | solution.py:623
  (110 other events, 1108.4 us)

commit v4 on v3

--- a/solution.py
+++ b/solution.py
@@ -151,27 +151,35 @@
     return -(-rows // tile) * tile
 
 
-def pick_kernel(info, row_ref, entry_ref, *out_refs):
+def pick_kernel(info, n_seq, share, row_ref, entry_ref, exit_ref, gain_ref, *refs):
+    piece_refs, tiny_refs, four_ref = refs[: info.per], refs[info.per : -1], refs[-1]
     entry = entry_ref[...].astype(F32)
     chunk = info.chunk
     parts = [entry[i * chunk : (i + 1) * chunk, :] for i in range(info.per)]
-    for i, out_ref in enumerate(out_refs):
-        out_ref[...] = chosen(parts, row_ref[info.send_sub + i]).astype(BF)
+    for i, piece_ref in enumerate(piece_refs):
+        piece_ref[...] = chosen(parts, row_ref[info.send_sub + i]).astype(BF)
+    width = four_ref.shape[2]
+    leaving = exit_ref[...].astype(F32)
+    four_ref[...] = jnp.zeros_like(four_ref)
+    for seq in range(n_seq):
+        four_ref[seq, :share, :] = leaving[:, seq * width : (seq + 1) * width]
+        four_ref[seq, share : share + 1, :] = gain_ref[...].astype(F32)
+    for i in range(n_seq):
+        tiny_refs[i][...] = four_ref[row_ref[info.to_seq + i]].astype(BF)
 
 
 def place_kernel(info, n_seq, share, row_ref, *refs):
     per, chunk = info.per, info.chunk
-    came, exit_ref, gains = refs[:per], refs[per], refs[per + 1 : per + 1 + n_seq]
-    out_ref, line_ref = refs[per + 1 + n_seq :]
+    came, tiny = refs[:per], refs[per : per + n_seq]
+    out_ref, line_ref, four_ref = refs[per + n_seq :]
     head = whole_tiles(share + n_seq)
+    width = four_ref.shape[2]
     line_ref[...] = jnp.zeros_like(line_ref)
-    line_ref[:share, :] = exit_ref[...].astype(F32)
-    rows = [ref[...].astype(F32) for ref in gains]
     for i in range(n_seq):
-        value = rows[0]
-        for j in range(1, n_seq):
-            value = jnp.where(row_ref[info.from_seq + j] == i, rows[j], value)
-        line_ref[share + i : share + i + 1, :] = value
+        four_ref[row_ref[info.from_seq + i]] = tiny[i][...].astype(F32)
+    for seq in range(n_seq):
+        line_ref[:share, seq * width : (seq + 1) * width] = four_ref[seq, :share, :]
+        line_ref[share + seq : share + seq + 1, :width] = four_ref[seq, share : share + 1, :]
     parts = [ref[...].astype(F32) for ref in came]
     for i in range(per):
         line_ref[head + i * chunk : head + (i + 1) * chunk, :] = chosen(
@@ -182,9 +190,8 @@
 
 def arrange_kernel(info, n_dp, n_seq, n_ex, share, owned, row_ref, *refs):
     blocks, refs = refs[: n_dp * n_ex], refs[n_dp * n_ex :]
-    entry_ref, gain_ref, *exit_refs = refs[: 2 + n_seq]
-    all_ref, line_ref, exits_ref = refs[2 + n_seq :]
-    width = exits_ref.shape[3]
+    entry_ref, gain_ref, exit_ref, all_ref, line_ref, exit_line_ref = refs
+    width = exit_ref.shape[1]
     head = whole_tiles(share + n_seq)
     for i in range(n_dp):
         for j in range(n_ex):
@@ -195,15 +202,14 @@
         value = all_ref[spot].astype(F32)
         line_ref[spot * owned : (spot + 1) * owned, :] = value[head : head + owned, :]
         for seq in range(n_seq):
-            exits_ref[seq, spot] = value[:share, seq * width : (seq + 1) * width]
             lane = ((dp * n_seq + seq) * n_ex + ex) * share
+            exit_line_ref[lane : lane + share, :] = value[:share, seq * width : (seq + 1) * width]
             for k in range(2):
                 gain_ref[k : k + 1, lane : lane + share] = value[
                     share + seq : share + seq + 1, k * share : (k + 1) * share
                 ]
     entry_ref[...] = line_ref[...].astype(BF)
-    for i in range(n_seq):
-        exit_refs[i][...] = exits_ref[row_ref[info.to_seq + i]].astype(BF)
+    exit_ref[...] = exit_line_ref[...].astype(BF)
 
 
 def pack_kernel(info, n_dp, n_seq, n_ex, share, owned, row_ref, *refs):
@@ -297,8 +303,11 @@
 
 def bias_rows(lag_ref, head, start, rows, keys):
     length = lag_ref.shape[1]
-    flat = jnp.broadcast_to(lag_ref[head : head + 1, :], (rows, length))
-    return pltpu.roll(flat, start, 1, stride=1, stride_axis=0)[:, :keys]
+    line = lag_ref[head : head + 1, length - keys :]
+    lane = lax.broadcasted_iota(jnp.int32, (1, keys), 1)
+    line = jnp.where(lane == 0, lag_ref[head : head + 1, :1], line)
+    flat = jnp.broadcast_to(line, (rows, keys))
+    return pltpu.roll(flat, start, 1, stride=1, stride_axis=0)
 
 
 def aligned(block, index):
@@ -353,35 +362,21 @@
     )
 
 
-def leave_kernel(info, n_dp, n_seq, n_ex, row_ref, ctx_ref, *refs):
-    exits, refs = refs[:n_seq], refs[n_seq:]
-    exit_ref, part_refs, (four_ref, line_ref) = refs[0], refs[1 : 1 + n_seq], refs[1 + n_seq :]
+def leave_kernel(info, row_ref, ctx_ref, exit_ref, *part_refs):
     rows = part_refs[0].shape[0]
-    share = exits[0].shape[1]
-    for i in range(n_seq):
-        four_ref[row_ref[info.from_seq + i]] = exits[i][...].astype(F32)
-    for dp in range(n_dp):
-        for seq in range(n_seq):
-            for ex in range(n_ex):
-                start = ((dp * n_seq + seq) * n_ex + ex) * share
-                line_ref[start : start + share, :] = four_ref[seq, ex * n_dp + dp]
-    exit_ref[...] = line_ref[...].astype(BF)
     for i, part_ref in enumerate(part_refs):
         block = aligned(rows, row_ref[info.to_seq + i])
         part_ref[...] = dot(ctx_ref[block, :], exit_ref[...], 1, 1).astype(BF)
 
 
-def leave(info, n_dp, n_seq, n_ex, info_row, ctx, exits):
-    spots, share, width = exits[0].shape
-    features = spots * share * n_seq
-    out = small_call(
-        functools.partial(leave_kernel, info, n_dp, n_seq, n_ex),
+def leave(info, n_seq, info_row, ctx, exit_t):
+    return small_call(
+        functools.partial(leave_kernel, info),
         info_row,
-        (ctx, *exits),
-        [((features, width), BF)] + [((ctx.shape[0] // n_seq, features), BF)] * n_seq,
-        [((n_seq, spots, share, width), F32), ((features, width), F32)],
-    )
-    return out[0], out[1:]
+        (ctx, exit_t),
+        [((ctx.shape[0] // n_seq, exit_t.shape[0]), BF)] * n_seq,
+        [],
+    )
 
 
 def leave_back_kernel(info, count, n_dp, share, row_ref, *refs):
@@ -685,12 +680,17 @@
     info_row = lax.dynamic_slice(jnp.asarray(info.table), (me, 0), (1, info.table.shape[1]))
     info_row = info_row.reshape(info.table.shape[1])
 
-    pieces = small_call(
-        functools.partial(pick_kernel, info),
-        info_row, (entry_weight.T,), [((chunk, features), BF)] * per, [],
-    )
+    gains = jnp.concatenate([first_gain, second_gain])
+    gains = jnp.pad(gains, (0, width - 2 * share))[None]
+    lines = whole_tiles(share + 1)
+    out = small_call(
+        functools.partial(pick_kernel, info, n_seq, share),
+        info_row, (entry_weight.T, exit_weight.T, gains),
+        [((chunk, features), BF)] * per + [((lines, width), BF)] * n_seq,
+        [((n_seq, lines, width), F32)],
+    )
+    pieces, tiny = out[:per], out[per:]
     came = [lax.ppermute(piece, ALL, pair) for piece, pair in zip(pieces, info.pairs)]
-    gains = jnp.pad(jnp.concatenate([first_gain, second_gain]), (0, features - 2 * share))
     group_size = n_dp * n_ex
     capacity = 3 * rows_here // group_size
     slots = group_size * capacity
@@ -722,12 +722,13 @@
     lag = jnp.dot(bias_here, hot, precision=HIGH)
     hot_back = bucket_hot(length - 1 - lane, buckets)
     w_own = (expert_up[0], expert_down[0])
-    gain_rows = gathered(gains[None], "seq", seq_steps)
+    tiny = traded(tiny, "seq", seq_steps)
     padded = whole_tiles(share + n_seq) + whole_tiles(owned, 8)
     (weights,) = small_call(
         functools.partial(place_kernel, info, n_seq, share),
-        info_row, (*came, exit_weight.T, *gain_rows),
-        [((padded, features), BF)], [((padded, features), F32)],
+        info_row, (*came, *tiny),
+        [((padded, features), BF)],
+        [((padded, features), F32), ((n_seq, lines, width), F32)],
     )
     later, *w_later = after((inputs, *w_own), weights)
     w_cut = [half for w in w_later for half in jnp.split(w, 2)]
@@ -735,19 +736,17 @@
     xhats = gathered((later * scale_one).astype(BF), "seq", seq_steps)
     weights = gathered(weights, "dp", range(1, n_dp))
     weights = [block for weight in weights for block in gathered(weight, "expert", range(1, n_ex))]
-    entry_t, gains, *exits = small_call(
+    entry_t, gains, exit_t = small_call(
         functools.partial(arrange_kernel, info, n_dp, n_seq, n_ex, share, owned),
         info_row, weights,
-        [((3 * width, features), BF), ((2, features), F32)]
-        + [((group_count, share, width), BF)] * n_seq,
+        [((3 * width, features), BF), ((2, features), F32), ((features, width), BF)],
         [
             ((group_count, padded, features), BF),
             ((3 * width, features), F32),
-            ((n_seq, group_count, share, width), F32),
+            ((features, width), F32),
         ],
     )
     gain_one, gain_two = gains[0:1], gains[1:2]
-    exits = exits[:1] + [shift(part, "seq", step) for part, step in zip(exits[1:], seq_steps)]
 
     inner = 2 if n_seq > 1 and n_seq & (n_seq - 1) == 0 else 1
     in_steps = tuple(range(1, inner))
@@ -764,7 +763,7 @@
     xfull, qkv, ctx, log = attend(
         info, heads, size, info_row, xhats, gains, entry_t, docs_row, docs_col, lag
     )
-    exit_t, parts = leave(info, n_dp, n_seq, n_ex, info_row, ctx, exits)
+    parts = leave(info, n_seq, info_row, ctx, exit_t)
 
     hidden, scale_two, send_rows = small_call(
         norm_kernel,

time: 359 us -> 351 us (0.978)
  waiting for transfers between devices: 140 us -> 134 us
    ppermute x51 -> x48, waiting for transfers between devices: 133 us -> 128 us  [shift(): lax.ppermute(array, axis, tuple(((i, target(count, i, step)) for i in ran...]
    ppermute x51 -> x48, starting transfers between devices: 53.8 us -> 50.8 us  [shift(): lax.ppermute(array, axis, tuple(((i, target(count, i, step)) for i in ran...]
    unnamed x146 -> x136, local copies, waits for them, and re-layouts: 9.76 us -> 9.58 us
  transfers between devices with their start and end apart: 61 -> 58, of which waited for: 23 -> 23; matrix products, arithmetic and copies ran while one was open for 6% -> 6% of each run, Pallas kernels for 23% -> 23%
where the time goes in v4:
time: 351 us; the launch traced here: 346 us
  waiting for transfers between devices  134 us (38%)
  starting transfers between devices  90.6 us (26%)
  Pallas kernels  85.1 us (24%)
  local copies, waits for them, and re-layouts  20.2 us (6%)
  other arithmetic  9.81 us (3%)
  matrix products  4.62 us (1%)
    ppermute x48, waiting for transfers between devices, shift(): lax.ppermute(array, axis, tuple(((i, target(count, i, step)) for i in ran...  128 us
    ppermute x48, starting transfers between devices, shift(): lax.ppermute(array, axis, tuple(((i, target(count, i, step)) for i in ran...  50.8 us
    pallas_call x9, Pallas kernels, tree_call(): pl.pallas_call(functools.partial(kernel, tree), out_shape=tuple(jax.tree....  42.6 us
    pallas_call x13, Pallas kernels, small_call(): pl.pallas_call(kernel, in_specs=specs(len(arrays)), out_shape=tuple((jax....  42.5 us
    all_to_all x4, starting transfers between devices, exchanged(): return lax.all_to_all(array, axis, 0, 0, tiled=True)  19.3 us
    ppermute x3, starting transfers between devices, local(): lax.ppermute(piece, ALL, tuple(((b, a) for a, b in pair)))  10.5 us
    ppermute x3, starting transfers between devices, local(): lax.ppermute(piece, ALL, pair)  9.96 us
    unnamed x136, local copies, waits for them, and re-layouts  9.58 us
  transfers between devices with their start and end apart: 58, of which 23 were waited for; matrix products, arithmetic and copies ran while one was open for 6% of the time, Pallas kernels for 23%

profile of v4, /device:TPU:18, one launch (start us, length us, event | category | flops | bytes accessed | tf_op | source)
XLA Modules:
  0.0 345.8 jit_solution(8795330446871103502)
XLA Ops:
  9.7 5.1 %collective-permute-start.2 = (bf16[24,768]{1,0:T(8,128)(2,1)}, bf16[24,768]{1,0:T(8,128)(2,1)S(1)}, u32[]{:S(2)}, u32[]{:S(2)}) collective-permute-start(bf16[24,768]{1,0:T(8,128)(2,1)} %get-tuple-element.87), channel_id=1, source_target_pairs={{0,0},{1,8},{2,2},{3,10},{4,18},{5,4},{6,12},{7,20},{8,6},{9,14},{... | collective-permute-start | bytes 110600 | tf_op jit(solution)/shard_map/ppermute | solution.py:693
  20.9 4.5 %all-to-all-start.1 = ((bf16[8,48,768]{2,1,0:T(8,128)(2,1)}), bf16[8,48,768]{2,1,0:T(8,128)(2,1)S(1)}, u32[]{:S(2)}, u32[]{:S(2)}) async-start(bf16[8,48,768]{2,1,0:T(8,128)(2,1)} %bitcast.16), calls=%async_computation.1 | async-start | bytes 1179648 | tf_op jit(solution)/shard_map/all_to_all | solution.py:626
  36.1 5.6 %collective-permute-done.7.refs_2_ = bf16[104,768]{1,0:T(8,128)(2,1)S(1)} collective-permute-done((bf16[104,768]{1,0:T(8,128)(2,1)}, bf16[104,768]{1,0:T(8,128)(2,1)S(1)}, u32[]{:S(2)}, u32[]{:S(2)}) %collective-permute-start.7) | collective-permute-done | bytes 159776 | tf_op jit(solution)/shard_map/ppermute | solution.py:618
  44.4 5.4 %collective-permute-done.9.refs_4_ = bf16[104,768]{1,0:T(8,128)(2,1)S(1)} collective-permute-done((bf16[104,768]{1,0:T(8,128)(2,1)}, bf16[104,768]{1,0:T(8,128)(2,1)S(1)}, u32[]{:S(2)}, u32[]{:S(2)}) %collective-permute-start.9) | collective-permute-done | bytes 159776 | tf_op jit(solution)/shard_map/ppermute | solution.py:618
  59.7 7.3 %shard_map.199 = (bf16[512,768]{1,0:T(8,128)(2,1)}, bf16[512,576]{1,0:T(8,128)(2,1)}, bf16[512,192]{1,0:T(8,128)(2,1)}, f32[512,3]{1,0:T(8,128)}) custom-call(s32[32]{0:T(128)} %dynamic-slice_bitcast_fusion.row_ref, bf16[128,768]{1,0:T(8,128)(2,1)} %copy-done.15, bf16[128,768]{1,0:T(8,128)(2,1)} %copy-done.23, bf16[128,768]{1,0:T(8,128)(2,1)} %copy-done.24, ...), custom_call_target="tpu_custom_call" | custom-call | tf_op jit(solution)/shard_map/pallas_call | solution.py:142
  77.3 4.7 %collective-permute-done.17.refs_2_ = bf16[128,768]{1,0:T(8,128)(2,1)S(1)} collective-permute-done((bf16[128,768]{1,0:T(8,128)(2,1)}, bf16[128,768]{1,0:T(8,128)(2,1)S(1)}, u32[]{:S(2)}, u32[]{:S(2)}) %collective-permute-start.17) | collective-permute-done | bytes 196640 | tf_op jit(solution)/shard_map/ppermute | solution.py:618
  98.3 5.1 %all-to-all-done = bf16[8,48,768]{2,1,0:T(8,128)(2,1)S(1)} async-done(((bf16[8,48,768]{2,1,0:T(8,128)(2,1)}), bf16[8,48,768]{2,1,0:T(8,128)(2,1)S(1)}, u32[]{:S(2)}, u32[]{:S(2)}) %all-to-all-start) | async-done | bytes 589856 | tf_op jit(solution)/shard_map/all_to_all | solution.py:626
  108.7 11.4 %collective-permute-done.20.refs_3_.refs_4_ = bf16[384,768]{1,0:T(8,128)(2,1)S(1)} collective-permute-done((bf16[384,768]{1,0:T(8,128)(2,1)}, bf16[384,768]{1,0:T(8,128)(2,1)S(1)}, u32[]{:S(2)}, u32[]{:S(2)}) %collective-permute-start.20) | collective-permute-done | bytes 589856 | tf_op jit(solution)/shard_map/ppermute | solution.py:618
  121.3 11.4 %collective-permute-done.21.refs_4_.refs_6_.refs_7_ = bf16[384,768]{1,0:T(8,128)(2,1)S(1)} collective-permute-done((bf16[384,768]{1,0:T(8,128)(2,1)}, bf16[384,768]{1,0:T(8,128)(2,1)S(1)}, u32[]{:S(2)}, u32[]{:S(2)}) %collective-permute-start.21) | collective-permute-done | bytes 589856 | tf_op jit(solution)/shard_map/ppermute | solution.py:618
  134.0 10.6 %collective-permute-done.22.refs_5_.refs_7_.refs_8_ = bf16[384,768]{1,0:T(8,128)(2,1)S(1)} collective-permute-done((bf16[384,768]{1,0:T(8,128)(2,1)}, bf16[384,768]{1,0:T(8,128)(2,1)S(1)}, u32[]{:S(2)}, u32[]{:S(2)}) %collective-permute-start.22) | collective-permute-done | bytes 589856 | tf_op jit(solution)/shard_map/ppermute | solution.py:618
  146.1 5.5 %shard_map.205 = (bf16[192,768]{1,0:T(8,128)(2,1)}, bf16[192,768]{1,0:T(8,128)(2,1)}, bf16[192,768]{1,0:T(8,128)(2,1)}, bf16[192,768]{1,0:T(8,128)(2,1)}, bf16[192,768]{1,0:T(8,128)(2,1)}) custom-call(bf16[192,768]{1,0:T(8,128)(2,1)} %copy-done.12, bf16[192,768]{1,0:T(8,128)(2,1)} %collective-permute-done.26.refs_1_.refs_5_, bf16[768,768]{1,0:T(8,128)(2,1)} %bitcast.71, ...), custom_call_target="tpu_custom_call" | custom-call | tf_op jit(solution)/shard_map/pallas_call | solution.py:552
  152.8 5.4 %shard_map.204 = (bf16[192,768]{1,0:T(8,128)(2,1)}, bf16[192,768]{1,0:T(8,128)(2,1)}, bf16[192,768]{1,0:T(8,128)(2,1)}, bf16[192,768]{1,0:T(8,128)(2,1)}, bf16[192,768]{1,0:T(8,128)(2,1)}) custom-call(bf16[192,768]{1,0:T(8,128)(2,1)} %collective-permute-done.23.refs_0_.refs_1_, bf16[192,768]{1,0:T(8,128)(2,1)} %collective-permute-done.24.refs_1_.refs_4_, ...), custom_call_target="tpu_custom_call" | custom-call | tf_op jit(solution)/shard_map/pallas_call | solution.py:552
  159.1 4.5 %shard_map.202 = (bf16[384,768]{1,0:T(8,128)(2,1)}, bf16[384,768]{1,0:T(8,128)(2,1)}, bf16[384,768]{1,0:T(8,128)(2,1)}) custom-call(bf16[384,768]{1,0:T(8,128)(2,1)} %bitcast.67, bf16[384,768]{1,0:T(8,128)(2,1)} %bitcast.63, bf16[768,768]{1,0:T(8,128)(2,1)} %bitcast.73, bf16[768,768]{1,0:T(8,128)(2,1)} %bitcast.60), custom_call_target="tpu_custom_call" | custom-call | tf_op jit(solution)/shard_map/pallas_call | solution.py:552
  163.6 4.5 %shard_map.203 = (bf16[384,768]{1,0:T(8,128)(2,1)}, bf16[384,768]{1,0:T(8,128)(2,1)}, bf16[384,768]{1,0:T(8,128)(2,1)}) custom-call(bf16[384,768]{1,0:T(8,128)(2,1)} %bitcast.68, bf16[384,768]{1,0:T(8,128)(2,1)} %bitcast.64, bf16[384,768]{1,0:T(8,128)(2,1)} %copy-done.9, bf16[384,768]{1,0:T(8,128)(2,1)} %copy-done.10, bf16[384,768]{1,0:T(8,128)(2,1)} %copy-done.7, ...), custom_call_target="tpu_custom_call" | custom-call | tf_op jit(solution)/shard_map/pallas_call | solution.py:552
  170.3 5.1 %all-to-all-start.3 = ((bf16[8,48,768]{2,1,0:T(8,128)(2,1)}), bf16[8,48,768]{2,1,0:T(8,128)(2,1)S(1)}, u32[]{:S(2)}, u32[]{:S(2)}) async-start(bf16[8,48,768]{2,1,0:T(8,128)(2,1)} %bitcast.25), calls=%async_computation.3 | async-start | bytes 1179648 | tf_op jit(solution)/shard_map/all_to_all | solution.py:626
  175.4 5.2 %shard_map.206 = (bf16[384,768]{1,0:T(8,128)(2,1)}, bf16[384,768]{1,0:T(8,128)(2,1)}) custom-call(bf16[384,768]{1,0:T(8,128)(2,1)} %get-tuple-element.158.refs_0_, bf16[384,768]{1,0:T(8,128)(2,1)} %get-tuple-element.107.refs_1_.refs_0_, bf16[192,768]{1,0:T(8,128)(2,1)} %get-tuple-element.108.refs_2_.refs_1_, ...), custom_call_target="tpu_custom_call" | custom-call | tf_op jit(solution)/shard_map/pallas_call | solution.py:552
  181.9 14.1 %collective-permute-done.27 = bf16[384,768]{1,0:T(8,128)(2,1)S(1)} collective-permute-done((bf16[384,768]{1,0:T(8,128)(2,1)}, bf16[384,768]{1,0:T(8,128)(2,1)S(1)}, u32[]{:S(2)}, u32[]{:S(2)}) %collective-permute-start.27) | collective-permute-done | bytes 589856 | tf_op jit(solution)/shard_map/ppermute | solution.py:618
  198.2 5.2 %all-to-all-start.2 = ((bf16[8,48,768]{2,1,0:T(8,128)(2,1)}), bf16[8,48,768]{2,1,0:T(8,128)(2,1)S(1)}, u32[]{:S(2)}, u32[]{:S(2)}) async-start(bf16[8,48,768]{2,1,0:T(8,128)(2,1)} %bitcast.22), calls=%async_computation.2 | async-start | bytes 1179648 | tf_op jit(solution)/shard_map/all_to_all | solution.py:626
  220.2 11.1 %shard_map.208 = (bf16[576,768]{1,0:T(8,128)(2,1)}, bf16[128,768]{1,0:T(8,128)(2,1)}, bf16[128,768]{1,0:T(8,128)(2,1)}, bf16[128,768]{1,0:T(8,128)(2,1)}, bf16[1...) custom-call(s32[32]{0:T(128)} %dynamic-slice_bitcast_fusion.row_ref, ...), custom_call_target="tpu_custom_call" | custom-call | tf_op jit(solution)/shard_map/pallas_call | solution.py:142
  268.7 24.1 %collective-permute-done.34 = bf16[128,768]{1,0:T(8,128)(2,1)S(1)} collective-permute-done((bf16[128,768]{1,0:T(8,128)(2,1)}, bf16[128,768]{1,0:T(8,128)(2,1)S(1)}, u32[]{:S(2)}, u32[]{:S(2)}) %collective-permute-start.34) | collective-permute-done | bytes 196640 | tf_op jit(solution)/shard_map/ppermute | solution.py:618
  302.9 4.8 %shard_map.217 = f32[768,768]{1,0:T(8,128)} custom-call(bf16[384,768]{1,0:T(8,128)(2,1)} %get-tuple-element.158.refs_0_, bf16[192,768]{1,0:T(8,128)(2,1)} %get-tuple-element.108.refs_2_.refs_1_, bf16[192,768]{1,0:T(8,128)(2,1)} %get-tuple-element.110.refs_4_.refs_2_, bf16[384,768]{1,0:T(8,128)(2,1)} %bitcast.66, ...), custom_call_target="tpu_custom_call" | custom-call | tf_op jit(solution)/shard_map/pallas_call | solution.py:552
  309.2 11.4 %collective-permute-done.51.refs_7_ = bf16[384,768]{1,0:T(8,128)(2,1)} collective-permute-done((bf16[384,768]{1,0:T(8,128)(2,1)}, bf16[384,768]{1,0:T(8,128)(2,1)}, u32[]{:S(2)}, u32[]{:S(2)}) %collective-permute-start.51) | collective-permute-done | bytes 589856 | tf_op jit(solution)/shard_map/ppermute | solution.py:618
  320.6 4.8 %shard_map.215 = f32[768,768]{1,0:T(8,128)} custom-call(bf16[384,768]{1,0:T(8,128)(2,1)} %bitcast.70, bf16[192,768]{1,0:T(8,128)(2,1)} %collective-permute-done.23.refs_0_.refs_1_, bf16[192,768]{1,0:T(8,128)(2,1)} %copy-done.12, bf16[384,768]{1,0:T(8,128)(2,1)} %get-tuple-element.150.refs_3_, bf16[192,768]{1,0:T(8,128)(2,1)} %get-tuple-element.151.refs_4_, ...), custom_call_target="tpu_custom_call" | custom-call | tf_op jit(solution)/shard_map/pallas_call | solution.py:552
  332.3 4.4 %collective-permute-start.48 = (f32[24,768]{1,0:T(8,128)}, f32[24,768]{1,0:T(8,128)S(1)}, u32[]{:S(2)}, u32[]{:S(2)}) collective-permute-start(f32[24,768]{1,0:T(8,128)} %get-tuple-element.146), channel_id=1, source_target_pairs={{0,0},{8,1},{16,2},{2,3},{10,4},{4,5},{12,6},{20,7},{6,8},{14,9},{... | collective-permute-start | bytes 221192 | tf_op jit(solution)/shard_map/ppermute | solution.py:876
  (289 shorter events, 163.3 us)
Async XLA Ops:
  4.8 25.4 %collective-permute-start = (bf16[24,768]{1,0:T(8,128)(2,1)}, bf16[24,768]{1,0:T(8,128)(2,1)S(1)}, u32[]{:S(2)}, u32[]{:S(2)}) collective-permute-start(bf16[24,768]{1,0:T(8,128)(2,1)} %get-tuple-element.85), channel_id=1, source_target_pairs={{0,0},{1,8},{2,16},{3,2},{4,10},{5,18},{6,4},{7,12},{8,6},{9,14},{... | collective-permute-start | bytes 110600 | tf_op jit(solution)/shard_map/ppermute | solution.py:693
  7.4 22.8 %collective-permute-start.1 = (bf16[24,768]{1,0:T(8,128)(2,1)}, bf16[24,768]{1,0:T(8,128)(2,1)S(1)}, u32[]{:S(2)}, u32[]{:S(2)}) collective-permute-start(bf16[24,768]{1,0:T(8,128)(2,1)} %get-tuple-element.86), channel_id=1, source_target_pairs={{0,0},{1,8},{2,16},{3,2},{4,10},{5,4},{6,12},{7,20},{8,6},{9,14},{... | collective-permute-start | bytes 110600 | tf_op jit(solution)/shard_map/ppermute | solution.py:693
  20.9 64.6 %all-to-all-start.1 = ((bf16[8,48,768]{2,1,0:T(8,128)(2,1)}), bf16[8,48,768]{2,1,0:T(8,128)(2,1)S(1)}, u32[]{:S(2)}, u32[]{:S(2)}) async-start(bf16[8,48,768]{2,1,0:T(8,128)(2,1)} %bitcast.16), calls=%async_computation.1 | async-start | bytes 1179648 | tf_op jit(solution)/shard_map/all_to_all | solution.py:626
  92.0 28.1 %collective-permute-start.20 = (bf16[384,768]{1,0:T(8,128)(2,1)}, bf16[384,768]{1,0:T(8,128)(2,1)S(1)}, u32[]{:S(2)}, u32[]{:S(2)}) collective-permute-start(bf16[384,768]{1,0:T(8,128)(2,1)} %get-tuple-element.169), channel_id=1, source_target_pairs={{0,4},{2,6},{4,0},{6,2},{1,5},{3,7},{5,1},{7,3},{8,12},{10,14},{12... | collective-permute-start | bytes 1769480 | tf_op jit(solution)/shard_map/ppermute | solution.py:618
  94.2 38.6 %collective-permute-start.21 = (bf16[384,768]{1,0:T(8,128)(2,1)}, bf16[384,768]{1,0:T(8,128)(2,1)S(1)}, u32[]{:S(2)}, u32[]{:S(2)}) collective-permute-start(bf16[384,768]{1,0:T(8,128)(2,1)} %get-tuple-element.168), channel_id=1, source_target_pairs={{0,4},{2,6},{4,0},{6,2},{1,5},{3,7},{5,1},{7,3},{8,12},{10,14},{12... | collective-permute-start | bytes 1769480 | tf_op jit(solution)/shard_map/ppermute | solution.py:618
  95.2 49.4 %collective-permute-start.22 = (bf16[384,768]{1,0:T(8,128)(2,1)}, bf16[384,768]{1,0:T(8,128)(2,1)S(1)}, u32[]{:S(2)}, u32[]{:S(2)}) collective-permute-start(bf16[384,768]{1,0:T(8,128)(2,1)} %get-tuple-element.167), channel_id=1, source_target_pairs={{0,4},{2,6},{4,0},{6,2},{1,5},{3,7},{5,1},{7,3},{8,12},{10,14},{12... | collective-permute-start | bytes 1769480 | tf_op jit(solution)/shard_map/ppermute | solution.py:618
  97.1 47.5 %collective-permute-start.26 = (bf16[192,768]{1,0:T(8,128)(2,1)}, bf16[192,768]{1,0:T(8,128)(2,1)}, u32[]{:S(2)}, u32[]{:S(2)}) collective-permute-start(bf16[192,768]{1,0:T(8,128)(2,1)} %bitcast.21), channel_id=1, source_target_pairs={{0,2},{2,0},{4,6},{6,4},{1,3},{3,1},{5,7},{7,5},{8,10},{10,8},{12,... | collective-permute-start | bytes 884744 | tf_op jit(solution)/shard_map/ppermute | solution.py:618
  107.5 37.1 %collective-permute-start.25 = (bf16[192,768]{1,0:T(8,128)(2,1)S(1)}, bf16[192,768]{1,0:T(8,128)(2,1)S(1)}, u32[]{:S(2)}, u32[]{:S(2)}) collective-permute-start(bf16[192,768]{1,0:T(8,128)(2,1)S(1)} %bitcast.85), channel_id=1, source_target_pairs={{0,2},{2,0},{4,6},{6,4},{1,3},{3,1},{5,7},{7,5},{8,10},{10,8},{12,... | collective-permute-start | bytes 884744 | tf_op jit(solution)/shard_map/ppermute | solution.py:618
  120.1 32.7 %collective-permute-start.24 = (bf16[192,768]{1,0:T(8,128)(2,1)S(1)}, bf16[192,768]{1,0:T(8,128)(2,1)}, u32[]{:S(2)}, u32[]{:S(2)}) collective-permute-start(bf16[192,768]{1,0:T(8,128)(2,1)S(1)} %bitcast.84), channel_id=1, source_target_pairs={{0,2},{2,0},{4,6},{6,4},{1,3},{3,1},{5,7},{7,5},{8,10},{10,8},{12,... | collective-permute-start | bytes 884744 | tf_op jit(solution)/shard_map/ppermute | solution.py:618
  170.3 27.9 %all-to-all-start.3 = ((bf16[8,48,768]{2,1,0:T(8,128)(2,1)}), bf16[8,48,768]{2,1,0:T(8,128)(2,1)S(1)}, u32[]{:S(2)}, u32[]{:S(2)}) async-start(bf16[8,48,768]{2,1,0:T(8,128)(2,1)} %bitcast.25), calls=%async_computation.3 | async-start | bytes 1179648 | tf_op jit(solution)/shard_map/all_to_all | solution.py:626
  198.2 69.0 %all-to-all-start.2 = ((bf16[8,48,768]{2,1,0:T(8,128)(2,1)}), bf16[8,48,768]{2,1,0:T(8,128)(2,1)S(1)}, u32[]{:S(2)}, u32[]{:S(2)}) async-start(bf16[8,48,768]{2,1,0:T(8,128)(2,1)} %bitcast.22), calls=%async_computation.2 | async-start | bytes 1179648 | tf_op jit(solution)/shard_map/all_to_all | solution.py:626
  231.2 36.0 %collective-permute-start.35 = (bf16[128,768]{1,0:T(8,128)(2,1)}, bf16[128,768]{1,0:T(8,128)(2,1)S(1)}, u32[]{:S(2)}, u32[]{:S(2)}) collective-permute-start(bf16[128,768]{1,0:T(8,128)(2,1)} %get-tuple-element.126), channel_id=1, source_target_pairs={{0,6},{2,4},{4,2},{6,0},{1,7},{3,5},{5,3},{7,1},{8,14},{10,12},{12... | collective-permute-start | bytes 589832 | tf_op jit(solution)/shard_map/ppermute | solution.py:618
  231.8 28.1 %collective-permute-start.36 = (bf16[4,48,192]{2,1,0:T(8,128)(2,1)S(1)}, bf16[4,48,192]{2,1,0:T(8,128)(2,1)S(1)}, u32[]{:S(2)}, u32[]{:S(2)}) collective-permute-start(bf16[4,48,192]{2,1,0:T(8,128)(2,1)S(1)} %copy-done.66), channel_id=1, source_target_pairs={{0,2},{2,0},{4,6},{6,4},{1,3},{3,1},{5,7},{7,5},{8,10},{10,8},{12,... | collective-permute-start | bytes 221192 | tf_op jit(solution)/shard_map/ppermute | solution.py:618
  233.8 27.2 %collective-permute-start.37 = (bf16[4,48,192]{2,1,0:T(8,128)(2,1)S(1)}, bf16[4,48,192]{2,1,0:T(8,128)(2,1)S(1)}, u32[]{:S(2)}, u32[]{:S(2)}) collective-permute-start(bf16[4,48,192]{2,1,0:T(8,128)(2,1)S(1)} %copy-done.65), channel_id=1, source_target_pairs={{0,4},{2,6},{4,0},{6,2},{1,5},{3,7},{5,1},{7,3},{8,12},{10,14},{12... | collective-permute-start | bytes 221192 | tf_op jit(solution)/shard_map/ppermute | solution.py:618
  234.8 27.2 %collective-permute-start.38 = (bf16[4,48,192]{2,1,0:T(8,128)(2,1)S(1)}, bf16[4,48,192]{2,1,0:T(8,128)(2,1)S(1)}, u32[]{:S(2)}, u32[]{:S(2)}) collective-permute-start(bf16[4,48,192]{2,1,0:T(8,128)(2,1)S(1)} %copy-done.64), channel_id=1, source_target_pairs={{0,6},{2,4},{4,2},{6,0},{1,7},{3,5},{5,3},{7,1},{8,14},{10,12},{12... | collective-permute-start | bytes 221192 | tf_op jit(solution)/shard_map/ppermute | solution.py:618
  259.9 40.0 %collective-permute-start.52 = (bf16[384,768]{1,0:T(8,128)(2,1)}, bf16[384,768]{1,0:T(8,128)(2,1)}, u32[]{:S(2)}, u32[]{:S(2)}) collective-permute-start(bf16[384,768]{1,0:T(8,128)(2,1)} %get-tuple-element.159), channel_id=1, source_target_pairs={{0,4},{2,6},{4,0},{6,2},{1,5},{3,7},{5,1},{7,3},{8,12},{10,14},{12... | collective-permute-start | bytes 1769480 | tf_op jit(solution)/shard_map/ppermute | solution.py:618
  261.0 39.5 %collective-permute-start.53 = (bf16[384,768]{1,0:T(8,128)(2,1)}, bf16[384,768]{1,0:T(8,128)(2,1)}, u32[]{:S(2)}, u32[]{:S(2)}) collective-permute-start(bf16[384,768]{1,0:T(8,128)(2,1)} %get-tuple-element.160), channel_id=1, source_target_pairs={{0,4},{2,6},{4,0},{6,2},{1,5},{3,7},{5,1},{7,3},{8,12},{10,14},{12... | collective-permute-start | bytes 1769480 | tf_op jit(solution)/shard_map/ppermute | solution.py:618
  262.0 30.8 %collective-permute-start.34 = (bf16[128,768]{1,0:T(8,128)(2,1)}, bf16[128,768]{1,0:T(8,128)(2,1)S(1)}, u32[]{:S(2)}, u32[]{:S(2)}) collective-permute-start(bf16[128,768]{1,0:T(8,128)(2,1)} %get-tuple-element.125), channel_id=1, source_target_pairs={{0,4},{2,6},{4,0},{6,2},{1,5},{3,7},{5,1},{7,3},{8,12},{10,14},{12... | collective-permute-start | bytes 589832 | tf_op jit(solution)/shard_map/ppermute | solution.py:618
  265.9 27.9 %collective-permute-start.33 = (bf16[128,768]{1,0:T(8,128)(2,1)S(1)}, bf16[128,768]{1,0:T(8,128)(2,1)S(1)}, u32[]{:S(2)}, u32[]{:S(2)}) collective-permute-start(bf16[128,768]{1,0:T(8,128)(2,1)S(1)} %copy-done.63), channel_id=1, source_target_pairs={{0,2},{2,0},{4,6},{6,4},{1,3},{3,1},{5,7},{7,5},{8,10},{10,8},{12,... | collective-permute-start | bytes 589832 | tf_op jit(solution)/shard_map/ppermute | solution.py:618
  267.2 27.8 %collective-permute-start.39 = (bf16[4,104,768]{2,1,0:T(8,128)(2,1)}, bf16[4,104,768]{2,1,0:T(8,128)(2,1)S(1)}, u32[]{:S(2)}, u32[]{:S(2)}) collective-permute-start(bf16[4,104,768]{2,1,0:T(8,128)(2,1)} %get-tuple-element.133), channel_id=1, source_target_pairs={{0,1},{1,0},{2,3},{3,2},{4,5},{5,4},{6,7},{7,6},{8,9},{9,8},{10,11... | collective-permute-start | bytes 1916936 | tf_op jit(solution)/shard_map/ppermute | solution.py:618
  293.8 26.9 %collective-permute-start.51 = (bf16[384,768]{1,0:T(8,128)(2,1)}, bf16[384,768]{1,0:T(8,128)(2,1)}, u32[]{:S(2)}, u32[]{:S(2)}) collective-permute-start(bf16[384,768]{1,0:T(8,128)(2,1)} %get-tuple-element.157), channel_id=1, source_target_pairs={{0,4},{2,6},{4,0},{6,2},{1,5},{3,7},{5,1},{7,3},{8,12},{10,14},{12... | collective-permute-start | bytes 1769480 | tf_op jit(solution)/shard_map/ppermute | solution.py:618
  298.4 27.0 %collective-permute-start.44 = (bf16[104,768]{1,0:T(8,128)(2,1)}, bf16[104,768]{1,0:T(8,128)(2,1)S(1)}, u32[]{:S(2)}, u32[]{:S(2)}) collective-permute-start(bf16[104,768]{1,0:T(8,128)(2,1)} %get-tuple-element.141), channel_id=1, source_target_pairs={{0,8},{8,0},{16,24},{24,16},{1,9},{9,1},{17,25},{25,17},{2,10},{10... | collective-permute-start | bytes 479240 | tf_op jit(solution)/shard_map/ppermute | solution.py:618
  299.9 25.5 %collective-permute-start.45 = (bf16[104,768]{1,0:T(8,128)(2,1)}, bf16[104,768]{1,0:T(8,128)(2,1)S(1)}, u32[]{:S(2)}, u32[]{:S(2)}) collective-permute-start(bf16[104,768]{1,0:T(8,128)(2,1)} %get-tuple-element.142), channel_id=1, source_target_pairs={{0,16},{8,24},{16,0},{24,8},{1,17},{9,25},{17,1},{25,9},{2,18},{10... | collective-permute-start | bytes 479240 | tf_op jit(solution)/shard_map/ppermute | solution.py:618
  300.5 25.0 %collective-permute-start.46 = (bf16[104,768]{1,0:T(8,128)(2,1)}, bf16[104,768]{1,0:T(8,128)(2,1)S(1)}, u32[]{:S(2)}, u32[]{:S(2)}) collective-permute-start(bf16[104,768]{1,0:T(8,128)(2,1)} %get-tuple-element.143), channel_id=1, source_target_pairs={{0,24},{8,16},{16,8},{24,0},{1,25},{9,17},{17,9},{25,1},{2,26},{10... | collective-permute-start | bytes 479240 | tf_op jit(solution)/shard_map/ppermute | solution.py:618
  (102 other events, 896.8 us)
